TPU v7x, 128 devices: a whole 4x4x4 slice. The times are simulated.
128 devices in a mesh: sx: 4 (over x), sy: 2 (over z_hi), op: 16 (over y, z_lo, core).
Axes of the slice: x: 4, y: 4, z: 4 (z_hi: 2, z_lo: 2; z = z_hi * 2 + z_lo), core: 2. Of those that a mesh axis runs over, the one named last changes fastest.
Arguments:
- op_real: float32 [4, 2, 6144, 6144], P('sx', 'sy', 'op'), may hold values from -0.0546875 to 0.0546875
- op_imag: float32 [4, 2, 6144, 6144], P('sx', 'sy', 'op'), may hold values from -0.0546875 to 0.0546875
- coef_right: float32 [4, 2, 2, 6144], P('sx', 'sy', None, 'op'), may hold values from -3 to 3
- coef_upper: float32 [4, 2, 2, 6144], P('sx', 'sy', None, 'op'), may hold values from -3 to 3
- sources: float32 [4, 2, 2, 16, 6144], P('sx', 'sy', None, None, 'op'), may hold values from -6 to 6
Outputs:
- traces: float32 [4, 2, 2, 16, 6144], P('sx', 'sy', None, None, 'op')
All inputs are finite; a program needn't handle non-finite values.
Results may differ from a plain program's by a relative error of at most 0.0003.
Values sent between devices are 32-bit elements; how exact they have to be, the bound alone decides.
No kernel may reach another device: no remote copies, remote signals or barrier semaphores. Data moves between devices by JAX's collectives and lax.ppermute only.
A program may use at most 64 MiB of HBM per device.

v0:
```python
import jax
import jax.numpy as jnp
from jax import lax
from jax.sharding import PartitionSpec as P

NB = 2


def from_behind(value, axis, by):
    size = lax.axis_size(axis)
    pairs = [(i, i + by) for i in range(size) if 0 <= i + by < size]
    return lax.ppermute(value, axis, pairs)


def in_order(blocks, dim):
    blocks = jnp.moveaxis(blocks, 0, dim)
    lengths = blocks.shape
    return blocks.reshape(*lengths[:dim], lengths[dim] * lengths[dim + 1], *lengths[dim + 2 :])


def from_everyone(value, axis):
    copies = jnp.broadcast_to(value, (lax.axis_size(axis), *value.shape))
    return lax.all_to_all(copies, axis, split_axis=0, concat_axis=0, tiled=True)


def gathered_copies(value, axis, dim):
    return in_order(from_everyone(value, axis), dim)


def contract(left, right):
    return lax.dot_general(
        left,
        right,
        (((1,), (1,)), ((), ())),
        precision=lax.Precision.HIGHEST,
        preferred_element_type=jnp.float32,
    )


def complex_scale(coef, field):
    real_part = coef[0][None, :] * field[0] - coef[1][None, :] * field[1]
    imag_part = coef[0][None, :] * field[1] + coef[1][None, :] * field[0]
    return jnp.stack([real_part, imag_part])


def shards(op_real, op_imag, coef_right, coef_upper, sources):
    real_rows = op_real[0, 0]
    imag_rows = op_imag[0, 0]
    right_coef = coef_right[0, 0]
    upper_coef = coef_upper[0, 0]
    fields = sources[0, 0]
    local_rows = real_rows.shape[0]
    batch_width = fields.shape[1] // NB
    diagonal_index = lax.axis_index("sx") + lax.axis_index("sy")
    diagonals = lax.axis_size("sx") + lax.axis_size("sy") - 1

    def accumulate(portion):
        columns = portion.shape[2]
        stacked = portion.reshape(2 * batch_width, columns)
        with_real = contract(stacked, real_rows)
        with_imag = contract(stacked, imag_rows)
        real_part = with_real[:batch_width] - with_imag[batch_width:]
        imag_part = with_imag[:batch_width] + with_real[batch_width:]
        return jnp.stack([real_part, imag_part])

    def section(which, active, state, outputs):
        from_left = from_behind(state, "sx", 1)
        from_below = from_behind(state, "sy", 1)
        offset = (jnp.clip(which, 0, NB - 1) * batch_width).astype(jnp.int32)
        source_block = lax.dynamic_slice_in_dim(fields, offset, batch_width, 1)
        incoming = (
            source_block
            + complex_scale(right_coef, from_left)
            + complex_scale(upper_coef, from_below)
        )
        result = accumulate(gathered_copies(incoming, "op", 2))
        new_state = jnp.where(active, result, state)
        current = lax.dynamic_slice_in_dim(outputs, offset, batch_width, 1)
        written = lax.dynamic_update_slice_in_dim(
            outputs, jnp.where(active, result, current), offset, 1
        )
        return (new_state, written)

    state0 = jnp.zeros((2, batch_width, local_rows), jnp.float32)
    outputs0 = jnp.zeros(fields.shape, jnp.float32)

    def turn_natural(section_no, carry):
        which = section_no // diagonals
        active = diagonal_index == section_no % diagonals
        return section(which, active, carry[0], carry[1])

    final_state, outputs = lax.fori_loop(0, NB * diagonals, turn_natural, (state0, outputs0))
    return outputs[None, None]


def solution(mesh):
    return jax.shard_map(
        shards,
        mesh=mesh,
        in_specs=(
            P("sx", "sy", "op", None),
            P("sx", "sy", "op", None),
            P("sx", "sy", None, "op"),
            P("sx", "sy", None, "op"),
            P("sx", "sy", None, None, "op"),
        ),
        out_specs=P("sx", "sy", None, None, "op"),
        check_vma=False,
    )
```

profile of v0, /device:TPU:71, one launch (start us, length us, event | category | flops | bytes accessed | tf_op | source)
XLA Modules:
  0.0 403.0 jit_solution(10128393401548741505)
XLA Ops:
  0.0 402.3 %while.18 = (s32[]{:T(128)}, f32[2,8,384]{2,1,0:T(8,128)S(1)}, f32[2,16,384]{2,1,0:T(8,128)S(1)}, s32[]{:T(128)}, f32[2,16,384]{2,1,0:T(8,128)}, /*index=5*/f32[...) while((s32[]{:T(128)}, f32[2,8,384]{2,1,0:T(8,128)S(1)}, ...), condition=%wide.region_1.2_spmd.clone, body=%wide.region_0.1_spmd.clone.sunk | while | flops 906067968 | bytes 61286888 | solution.py:92
  7.7 7.4 %all-to-all-start = ((f32[16,2,8,384]{3,2,1,0:T(8,128)}), f32[16,2,8,384]{3,2,1,0:T(8,128)S(1)}, u32[]{:S(2)}, u32[]{:S(2)}) async-start(f32[16,2,8,384]{3,2,1,0:T(8,128)} %broadcast_in_dim.24), calls=%async_computation | async-start | bytes 786432 | tf_op jit(solution)/shard_map/while/body/eval_jaxpr/all_to_all | solution.py:23
  15.0 8.6 %all-to-all-done = f32[16,2,8,384]{3,2,1,0:T(8,128)S(1)} async-done(((f32[16,2,8,384]{3,2,1,0:T(8,128)}), f32[16,2,8,384]{3,2,1,0:T(8,128)S(1)}, u32[]{:S(2)}, u32[]{:S(2)}) %all-to-all-start) | async-done | bytes 393248 | tf_op jit(solution)/shard_map/while/body/eval_jaxpr/all_to_all | solution.py:23
  23.9 10.3 %fusion.24 = f32[16,384]{1,0:T(8,128)S(1)} fusion(f32[16,6144]{1,0:T(8,128)S(1)} %bitcast.38, f32[384,6144]{1,0:T(8,128)} %get-tuple-element.407), kind=kOutput, calls=%fused_computation.19.clone.1 | convolution fusion | flops 452984832 | bytes 9854976 | tf_op jit(solution)/shard_map/while/body/eval_jaxpr/dot_general | solution.py:31
  34.2 7.9 %fusion.23 = f32[16,384]{1,0:T(8,128)S(1)} fusion(f32[16,6144]{1,0:T(8,128)S(1)} %bitcast.39, f32[384,6144]{1,0:T(8,128)S(1)} %copy-done), kind=kOutput, calls=%fused_computation.20.clone.1 | convolution fusion | flops 452984832 | bytes 9854976 | tf_op jit(solution)/shard_map/while/body/eval_jaxpr/dot_general | solution.py:31
  49.7 5.2 %all-to-all-start = ((f32[16,2,8,384]{3,2,1,0:T(8,128)}), f32[16,2,8,384]{3,2,1,0:T(8,128)S(1)}, u32[]{:S(2)}, u32[]{:S(2)}) async-start(f32[16,2,8,384]{3,2,1,0:T(8,128)} %broadcast_in_dim.24), calls=%async_computation | async-start | bytes 786432 | tf_op jit(solution)/shard_map/while/body/eval_jaxpr/all_to_all | solution.py:23
  54.9 8.6 %all-to-all-done = f32[16,2,8,384]{3,2,1,0:T(8,128)S(1)} async-done(((f32[16,2,8,384]{3,2,1,0:T(8,128)}), f32[16,2,8,384]{3,2,1,0:T(8,128)S(1)}, u32[]{:S(2)}, u32[]{:S(2)}) %all-to-all-start) | async-done | bytes 393248 | tf_op jit(solution)/shard_map/while/body/eval_jaxpr/all_to_all | solution.py:23
  63.8 10.3 %fusion.24 = f32[16,384]{1,0:T(8,128)S(1)} fusion(f32[16,6144]{1,0:T(8,128)S(1)} %bitcast.38, f32[384,6144]{1,0:T(8,128)} %get-tuple-element.407), kind=kOutput, calls=%fused_computation.19.clone.1 | convolution fusion | flops 452984832 | bytes 9854976 | tf_op jit(solution)/shard_map/while/body/eval_jaxpr/dot_general | solution.py:31
  74.2 7.9 %fusion.23 = f32[16,384]{1,0:T(8,128)S(1)} fusion(f32[16,6144]{1,0:T(8,128)S(1)} %bitcast.39, f32[384,6144]{1,0:T(8,128)S(1)} %copy-done), kind=kOutput, calls=%fused_computation.20.clone.1 | convolution fusion | flops 452984832 | bytes 9854976 | tf_op jit(solution)/shard_map/while/body/eval_jaxpr/dot_general | solution.py:31
  85.5 2.7 collective-permute-done.1
  89.8 5.2 %all-to-all-start = ((f32[16,2,8,384]{3,2,1,0:T(8,128)}), f32[16,2,8,384]{3,2,1,0:T(8,128)S(1)}, u32[]{:S(2)}, u32[]{:S(2)}) async-start(f32[16,2,8,384]{3,2,1,0:T(8,128)} %broadcast_in_dim.24), calls=%async_computation | async-start | bytes 786432 | tf_op jit(solution)/shard_map/while/body/eval_jaxpr/all_to_all | solution.py:23
  95.0 8.6 %all-to-all-done = f32[16,2,8,384]{3,2,1,0:T(8,128)S(1)} async-done(((f32[16,2,8,384]{3,2,1,0:T(8,128)}), f32[16,2,8,384]{3,2,1,0:T(8,128)S(1)}, u32[]{:S(2)}, u32[]{:S(2)}) %all-to-all-start) | async-done | bytes 393248 | tf_op jit(solution)/shard_map/while/body/eval_jaxpr/all_to_all | solution.py:23
  103.9 10.3 %fusion.24 = f32[16,384]{1,0:T(8,128)S(1)} fusion(f32[16,6144]{1,0:T(8,128)S(1)} %bitcast.38, f32[384,6144]{1,0:T(8,128)} %get-tuple-element.407), kind=kOutput, calls=%fused_computation.19.clone.1 | convolution fusion | flops 452984832 | bytes 9854976 | tf_op jit(solution)/shard_map/while/body/eval_jaxpr/dot_general | solution.py:31
  114.2 7.9 %fusion.23 = f32[16,384]{1,0:T(8,128)S(1)} fusion(f32[16,6144]{1,0:T(8,128)S(1)} %bitcast.39, f32[384,6144]{1,0:T(8,128)S(1)} %copy-done), kind=kOutput, calls=%fused_computation.20.clone.1 | convolution fusion | flops 452984832 | bytes 9854976 | tf_op jit(solution)/shard_map/while/body/eval_jaxpr/dot_general | solution.py:31
  125.6 2.7 collective-permute-done.1
  129.8 5.2 %all-to-all-start = ((f32[16,2,8,384]{3,2,1,0:T(8,128)}), f32[16,2,8,384]{3,2,1,0:T(8,128)S(1)}, u32[]{:S(2)}, u32[]{:S(2)}) async-start(f32[16,2,8,384]{3,2,1,0:T(8,128)} %broadcast_in_dim.24), calls=%async_computation | async-start | bytes 786432 | tf_op jit(solution)/shard_map/while/body/eval_jaxpr/all_to_all | solution.py:23
  135.0 8.6 %all-to-all-done = f32[16,2,8,384]{3,2,1,0:T(8,128)S(1)} async-done(((f32[16,2,8,384]{3,2,1,0:T(8,128)}), f32[16,2,8,384]{3,2,1,0:T(8,128)S(1)}, u32[]{:S(2)}, u32[]{:S(2)}) %all-to-all-start) | async-done | bytes 393248 | tf_op jit(solution)/shard_map/while/body/eval_jaxpr/all_to_all | solution.py:23
  143.9 10.3 %fusion.24 = f32[16,384]{1,0:T(8,128)S(1)} fusion(f32[16,6144]{1,0:T(8,128)S(1)} %bitcast.38, f32[384,6144]{1,0:T(8,128)} %get-tuple-element.407), kind=kOutput, calls=%fused_computation.19.clone.1 | convolution fusion | flops 452984832 | bytes 9854976 | tf_op jit(solution)/shard_map/while/body/eval_jaxpr/dot_general | solution.py:31
  154.2 7.9 %fusion.23 = f32[16,384]{1,0:T(8,128)S(1)} fusion(f32[16,6144]{1,0:T(8,128)S(1)} %bitcast.39, f32[384,6144]{1,0:T(8,128)S(1)} %copy-done), kind=kOutput, calls=%fused_computation.20.clone.1 | convolution fusion | flops 452984832 | bytes 9854976 | tf_op jit(solution)/shard_map/while/body/eval_jaxpr/dot_general | solution.py:31
  165.6 2.7 collective-permute-done.1
  169.8 5.2 %all-to-all-start = ((f32[16,2,8,384]{3,2,1,0:T(8,128)}), f32[16,2,8,384]{3,2,1,0:T(8,128)S(1)}, u32[]{:S(2)}, u32[]{:S(2)}) async-start(f32[16,2,8,384]{3,2,1,0:T(8,128)} %broadcast_in_dim.24), calls=%async_computation | async-start | bytes 786432 | tf_op jit(solution)/shard_map/while/body/eval_jaxpr/all_to_all | solution.py:23
  175.1 8.6 %all-to-all-done = f32[16,2,8,384]{3,2,1,0:T(8,128)S(1)} async-done(((f32[16,2,8,384]{3,2,1,0:T(8,128)}), f32[16,2,8,384]{3,2,1,0:T(8,128)S(1)}, u32[]{:S(2)}, u32[]{:S(2)}) %all-to-all-start) | async-done | bytes 393248 | tf_op jit(solution)/shard_map/while/body/eval_jaxpr/all_to_all | solution.py:23
  184.0 10.3 %fusion.24 = f32[16,384]{1,0:T(8,128)S(1)} fusion(f32[16,6144]{1,0:T(8,128)S(1)} %bitcast.38, f32[384,6144]{1,0:T(8,128)} %get-tuple-element.407), kind=kOutput, calls=%fused_computation.19.clone.1 | convolution fusion | flops 452984832 | bytes 9854976 | tf_op jit(solution)/shard_map/while/body/eval_jaxpr/dot_general | solution.py:31
  194.3 7.9 %fusion.23 = f32[16,384]{1,0:T(8,128)S(1)} fusion(f32[16,6144]{1,0:T(8,128)S(1)} %bitcast.39, f32[384,6144]{1,0:T(8,128)S(1)} %copy-done), kind=kOutput, calls=%fused_computation.20.clone.1 | convolution fusion | flops 452984832 | bytes 9854976 | tf_op jit(solution)/shard_map/while/body/eval_jaxpr/dot_general | solution.py:31
  205.6 2.7 collective-permute-done.1
  209.9 5.2 %all-to-all-start = ((f32[16,2,8,384]{3,2,1,0:T(8,128)}), f32[16,2,8,384]{3,2,1,0:T(8,128)S(1)}, u32[]{:S(2)}, u32[]{:S(2)}) async-start(f32[16,2,8,384]{3,2,1,0:T(8,128)} %broadcast_in_dim.24), calls=%async_computation | async-start | bytes 786432 | tf_op jit(solution)/shard_map/while/body/eval_jaxpr/all_to_all | solution.py:23
  215.1 8.6 %all-to-all-done = f32[16,2,8,384]{3,2,1,0:T(8,128)S(1)} async-done(((f32[16,2,8,384]{3,2,1,0:T(8,128)}), f32[16,2,8,384]{3,2,1,0:T(8,128)S(1)}, u32[]{:S(2)}, u32[]{:S(2)}) %all-to-all-start) | async-done | bytes 393248 | tf_op jit(solution)/shard_map/while/body/eval_jaxpr/all_to_all | solution.py:23
  224.0 10.3 %fusion.24 = f32[16,384]{1,0:T(8,128)S(1)} fusion(f32[16,6144]{1,0:T(8,128)S(1)} %bitcast.38, f32[384,6144]{1,0:T(8,128)} %get-tuple-element.407), kind=kOutput, calls=%fused_computation.19.clone.1 | convolution fusion | flops 452984832 | bytes 9854976 | tf_op jit(solution)/shard_map/while/body/eval_jaxpr/dot_general | solution.py:31
  234.3 7.9 %fusion.23 = f32[16,384]{1,0:T(8,128)S(1)} fusion(f32[16,6144]{1,0:T(8,128)S(1)} %bitcast.39, f32[384,6144]{1,0:T(8,128)S(1)} %copy-done), kind=kOutput, calls=%fused_computation.20.clone.1 | convolution fusion | flops 452984832 | bytes 9854976 | tf_op jit(solution)/shard_map/while/body/eval_jaxpr/dot_general | solution.py:31
  245.7 2.7 collective-permute-done.1
  249.9 5.2 %all-to-all-start = ((f32[16,2,8,384]{3,2,1,0:T(8,128)}), f32[16,2,8,384]{3,2,1,0:T(8,128)S(1)}, u32[]{:S(2)}, u32[]{:S(2)}) async-start(f32[16,2,8,384]{3,2,1,0:T(8,128)} %broadcast_in_dim.24), calls=%async_computation | async-start | bytes 786432 | tf_op jit(solution)/shard_map/while/body/eval_jaxpr/all_to_all | solution.py:23
  255.1 8.6 %all-to-all-done = f32[16,2,8,384]{3,2,1,0:T(8,128)S(1)} async-done(((f32[16,2,8,384]{3,2,1,0:T(8,128)}), f32[16,2,8,384]{3,2,1,0:T(8,128)S(1)}, u32[]{:S(2)}, u32[]{:S(2)}) %all-to-all-start) | async-done | bytes 393248 | tf_op jit(solution)/shard_map/while/body/eval_jaxpr/all_to_all | solution.py:23
  264.0 10.3 %fusion.24 = f32[16,384]{1,0:T(8,128)S(1)} fusion(f32[16,6144]{1,0:T(8,128)S(1)} %bitcast.38, f32[384,6144]{1,0:T(8,128)} %get-tuple-element.407), kind=kOutput, calls=%fused_computation.19.clone.1 | convolution fusion | flops 452984832 | bytes 9854976 | tf_op jit(solution)/shard_map/while/body/eval_jaxpr/dot_general | solution.py:31
  274.3 7.9 %fusion.23 = f32[16,384]{1,0:T(8,128)S(1)} fusion(f32[16,6144]{1,0:T(8,128)S(1)} %bitcast.39, f32[384,6144]{1,0:T(8,128)S(1)} %copy-done), kind=kOutput, calls=%fused_computation.20.clone.1 | convolution fusion | flops 452984832 | bytes 9854976 | tf_op jit(solution)/shard_map/while/body/eval_jaxpr/dot_general | solution.py:31
  285.7 2.7 collective-permute-done.1
  289.9 5.2 %all-to-all-start = ((f32[16,2,8,384]{3,2,1,0:T(8,128)}), f32[16,2,8,384]{3,2,1,0:T(8,128)S(1)}, u32[]{:S(2)}, u32[]{:S(2)}) async-start(f32[16,2,8,384]{3,2,1,0:T(8,128)} %broadcast_in_dim.24), calls=%async_computation | async-start | bytes 786432 | tf_op jit(solution)/shard_map/while/body/eval_jaxpr/all_to_all | solution.py:23
  295.2 8.6 %all-to-all-done = f32[16,2,8,384]{3,2,1,0:T(8,128)S(1)} async-done(((f32[16,2,8,384]{3,2,1,0:T(8,128)}), f32[16,2,8,384]{3,2,1,0:T(8,128)S(1)}, u32[]{:S(2)}, u32[]{:S(2)}) %all-to-all-start) | async-done | bytes 393248 | tf_op jit(solution)/shard_map/while/body/eval_jaxpr/all_to_all | solution.py:23
  304.1 10.3 %fusion.24 = f32[16,384]{1,0:T(8,128)S(1)} fusion(f32[16,6144]{1,0:T(8,128)S(1)} %bitcast.38, f32[384,6144]{1,0:T(8,128)} %get-tuple-element.407), kind=kOutput, calls=%fused_computation.19.clone.1 | convolution fusion | flops 452984832 | bytes 9854976 | tf_op jit(solution)/shard_map/while/body/eval_jaxpr/dot_general | solution.py:31
  314.4 7.9 %fusion.23 = f32[16,384]{1,0:T(8,128)S(1)} fusion(f32[16,6144]{1,0:T(8,128)S(1)} %bitcast.39, f32[384,6144]{1,0:T(8,128)S(1)} %copy-done), kind=kOutput, calls=%fused_computation.20.clone.1 | convolution fusion | flops 452984832 | bytes 9854976 | tf_op jit(solution)/shard_map/while/body/eval_jaxpr/dot_general | solution.py:31
  330.0 5.2 %all-to-all-start = ((f32[16,2,8,384]{3,2,1,0:T(8,128)}), f32[16,2,8,384]{3,2,1,0:T(8,128)S(1)}, u32[]{:S(2)}, u32[]{:S(2)}) async-start(f32[16,2,8,384]{3,2,1,0:T(8,128)} %broadcast_in_dim.24), calls=%async_computation | async-start | bytes 786432 | tf_op jit(solution)/shard_map/while/body/eval_jaxpr/all_to_all | solution.py:23
  335.2 8.6 %all-to-all-done = f32[16,2,8,384]{3,2,1,0:T(8,128)S(1)} async-done(((f32[16,2,8,384]{3,2,1,0:T(8,128)}), f32[16,2,8,384]{3,2,1,0:T(8,128)S(1)}, u32[]{:S(2)}, u32[]{:S(2)}) %all-to-all-start) | async-done | bytes 393248 | tf_op jit(solution)/shard_map/while/body/eval_jaxpr/all_to_all | solution.py:23
  344.1 10.3 %fusion.24 = f32[16,384]{1,0:T(8,128)S(1)} fusion(f32[16,6144]{1,0:T(8,128)S(1)} %bitcast.38, f32[384,6144]{1,0:T(8,128)} %get-tuple-element.407), kind=kOutput, calls=%fused_computation.19.clone.1 | convolution fusion | flops 452984832 | bytes 9854976 | tf_op jit(solution)/shard_map/while/body/eval_jaxpr/dot_general | solution.py:31
  354.4 7.9 %fusion.23 = f32[16,384]{1,0:T(8,128)S(1)} fusion(f32[16,6144]{1,0:T(8,128)S(1)} %bitcast.39, f32[384,6144]{1,0:T(8,128)S(1)} %copy-done), kind=kOutput, calls=%fused_computation.20.clone.1 | convolution fusion | flops 452984832 | bytes 9854976 | tf_op jit(solution)/shard_map/while/body/eval_jaxpr/dot_general | solution.py:31
  365.8 2.7 collective-permute-done.1
  370.0 5.2 %all-to-all-start = ((f32[16,2,8,384]{3,2,1,0:T(8,128)}), f32[16,2,8,384]{3,2,1,0:T(8,128)S(1)}, u32[]{:S(2)}, u32[]{:S(2)}) async-start(f32[16,2,8,384]{3,2,1,0:T(8,128)} %broadcast_in_dim.24), calls=%async_computation | async-start | bytes 786432 | tf_op jit(solution)/shard_map/while/body/eval_jaxpr/all_to_all | solution.py:23
  375.2 8.6 %all-to-all-done = f32[16,2,8,384]{3,2,1,0:T(8,128)S(1)} async-done(((f32[16,2,8,384]{3,2,1,0:T(8,128)}), f32[16,2,8,384]{3,2,1,0:T(8,128)S(1)}, u32[]{:S(2)}, u32[]{:S(2)}) %all-to-all-start) | async-done | bytes 393248 | tf_op jit(solution)/shard_map/while/body/eval_jaxpr/all_to_all | solution.py:23
  384.1 10.3 %fusion.24 = f32[16,384]{1,0:T(8,128)S(1)} fusion(f32[16,6144]{1,0:T(8,128)S(1)} %bitcast.38, f32[384,6144]{1,0:T(8,128)} %get-tuple-element.407), kind=kOutput, calls=%fused_computation.19.clone.1 | convolution fusion | flops 452984832 | bytes 9854976 | tf_op jit(solution)/shard_map/while/body/eval_jaxpr/dot_general | solution.py:31
  394.4 7.9 %fusion.23 = f32[16,384]{1,0:T(8,128)S(1)} fusion(f32[16,6144]{1,0:T(8,128)S(1)} %bitcast.39, f32[384,6144]{1,0:T(8,128)S(1)} %copy-done), kind=kOutput, calls=%fused_computation.20.clone.1 | convolution fusion | flops 452984832 | bytes 9854976 | tf_op jit(solution)/shard_map/while/body/eval_jaxpr/dot_general | solution.py:31
  (157 shorter events, 60.6 us)
Async XLA Ops:
  0.0 6.1 %collective-permute-start.1 = (f32[2,8,384]{2,1,0:T(8,128)S(1)}, f32[2,8,384]{2,1,0:T(8,128)S(1)}, u32[]{:S(2)}, u32[]{:S(2)}) collective-permute-start(f32[2,8,384]{2,1,0:T(8,128)S(1)} %broadcast_select_fusion.2), channel_id=1, source_target_pairs={{0,16},{1,17},{2,18},{3,19},{4,20},{5,21},{6,22},{7,23},{8,24},{9,... | collective-permute-start | bytes 73736 | tf_op jit(solution)/shard_map/while/body/eval_jaxpr/ppermute | solution.py:12
  1.3 4.8 %collective-permute-start = (f32[2,8,384]{2,1,0:T(8,128)S(1)}, f32[2,8,384]{2,1,0:T(8,128)S(1)}, u32[]{:S(2)}, u32[]{:S(2)}) collective-permute-start(f32[2,8,384]{2,1,0:T(8,128)S(1)} %broadcast_select_fusion.2), channel_id=1, source_target_pairs={{0,32},{32,64},{64,96},{1,33},{33,65},{65,97},{2,34},{34,66},{66,9... | collective-permute-start | bytes 73736 | tf_op jit(solution)/shard_map/while/body/eval_jaxpr/ppermute | solution.py:12
  7.7 15.9 %all-to-all-start = ((f32[16,2,8,384]{3,2,1,0:T(8,128)}), f32[16,2,8,384]{3,2,1,0:T(8,128)S(1)}, u32[]{:S(2)}, u32[]{:S(2)}) async-start(f32[16,2,8,384]{3,2,1,0:T(8,128)} %broadcast_in_dim.24), calls=%async_computation | async-start | bytes 786432 | tf_op jit(solution)/shard_map/while/body/eval_jaxpr/all_to_all | solution.py:23
  23.6 10.6 %copy-start = (f32[384,6144]{1,0:T(8,128)S(1)}, f32[384,6144]{1,0:T(8,128)}, u32[]{:S(2)}) copy-start(f32[384,6144]{1,0:T(8,128)} %get-tuple-element.408) | copy-start | bytes 28311556 | tf_op jit(solution)/shard_map/while
  42.1 6.1 %collective-permute-start.1 = (f32[2,8,384]{2,1,0:T(8,128)S(1)}, f32[2,8,384]{2,1,0:T(8,128)S(1)}, u32[]{:S(2)}, u32[]{:S(2)}) collective-permute-start(f32[2,8,384]{2,1,0:T(8,128)S(1)} %broadcast_select_fusion.2), channel_id=1, source_target_pairs={{0,16},{1,17},{2,18},{3,19},{4,20},{5,21},{6,22},{7,23},{8,24},{9,... | collective-permute-start | bytes 73736 | tf_op jit(solution)/shard_map/while/body/eval_jaxpr/ppermute | solution.py:12
  43.4 4.8 %collective-permute-start = (f32[2,8,384]{2,1,0:T(8,128)S(1)}, f32[2,8,384]{2,1,0:T(8,128)S(1)}, u32[]{:S(2)}, u32[]{:S(2)}) collective-permute-start(f32[2,8,384]{2,1,0:T(8,128)S(1)} %broadcast_select_fusion.2), channel_id=1, source_target_pairs={{0,32},{32,64},{64,96},{1,33},{33,65},{65,97},{2,34},{34,66},{66,9... | collective-permute-start | bytes 73736 | tf_op jit(solution)/shard_map/while/body/eval_jaxpr/ppermute | solution.py:12
  49.7 13.9 %all-to-all-start = ((f32[16,2,8,384]{3,2,1,0:T(8,128)}), f32[16,2,8,384]{3,2,1,0:T(8,128)S(1)}, u32[]{:S(2)}, u32[]{:S(2)}) async-start(f32[16,2,8,384]{3,2,1,0:T(8,128)} %broadcast_in_dim.24), calls=%async_computation | async-start | bytes 786432 | tf_op jit(solution)/shard_map/while/body/eval_jaxpr/all_to_all | solution.py:23
  63.6 10.6 %copy-start = (f32[384,6144]{1,0:T(8,128)S(1)}, f32[384,6144]{1,0:T(8,128)}, u32[]{:S(2)}) copy-start(f32[384,6144]{1,0:T(8,128)} %get-tuple-element.408) | copy-start | bytes 28311556 | tf_op jit(solution)/shard_map/while
  82.1 6.1 %collective-permute-start.1 = (f32[2,8,384]{2,1,0:T(8,128)S(1)}, f32[2,8,384]{2,1,0:T(8,128)S(1)}, u32[]{:S(2)}, u32[]{:S(2)}) collective-permute-start(f32[2,8,384]{2,1,0:T(8,128)S(1)} %broadcast_select_fusion.2), channel_id=1, source_target_pairs={{0,16},{1,17},{2,18},{3,19},{4,20},{5,21},{6,22},{7,23},{8,24},{9,... | collective-permute-start | bytes 73736 | tf_op jit(solution)/shard_map/while/body/eval_jaxpr/ppermute | solution.py:12
  83.4 4.8 %collective-permute-start = (f32[2,8,384]{2,1,0:T(8,128)S(1)}, f32[2,8,384]{2,1,0:T(8,128)S(1)}, u32[]{:S(2)}, u32[]{:S(2)}) collective-permute-start(f32[2,8,384]{2,1,0:T(8,128)S(1)} %broadcast_select_fusion.2), channel_id=1, source_target_pairs={{0,32},{32,64},{64,96},{1,33},{33,65},{65,97},{2,34},{34,66},{66,9... | collective-permute-start | bytes 73736 | tf_op jit(solution)/shard_map/while/body/eval_jaxpr/ppermute | solution.py:12
  89.8 13.9 %all-to-all-start = ((f32[16,2,8,384]{3,2,1,0:T(8,128)}), f32[16,2,8,384]{3,2,1,0:T(8,128)S(1)}, u32[]{:S(2)}, u32[]{:S(2)}) async-start(f32[16,2,8,384]{3,2,1,0:T(8,128)} %broadcast_in_dim.24), calls=%async_computation | async-start | bytes 786432 | tf_op jit(solution)/shard_map/while/body/eval_jaxpr/all_to_all | solution.py:23
  103.6 10.6 %copy-start = (f32[384,6144]{1,0:T(8,128)S(1)}, f32[384,6144]{1,0:T(8,128)}, u32[]{:S(2)}) copy-start(f32[384,6144]{1,0:T(8,128)} %get-tuple-element.408) | copy-start | bytes 28311556 | tf_op jit(solution)/shard_map/while
  122.1 6.1 %collective-permute-start.1 = (f32[2,8,384]{2,1,0:T(8,128)S(1)}, f32[2,8,384]{2,1,0:T(8,128)S(1)}, u32[]{:S(2)}, u32[]{:S(2)}) collective-permute-start(f32[2,8,384]{2,1,0:T(8,128)S(1)} %broadcast_select_fusion.2), channel_id=1, source_target_pairs={{0,16},{1,17},{2,18},{3,19},{4,20},{5,21},{6,22},{7,23},{8,24},{9,... | collective-permute-start | bytes 73736 | tf_op jit(solution)/shard_map/while/body/eval_jaxpr/ppermute | solution.py:12
  123.4 4.8 %collective-permute-start = (f32[2,8,384]{2,1,0:T(8,128)S(1)}, f32[2,8,384]{2,1,0:T(8,128)S(1)}, u32[]{:S(2)}, u32[]{:S(2)}) collective-permute-start(f32[2,8,384]{2,1,0:T(8,128)S(1)} %broadcast_select_fusion.2), channel_id=1, source_target_pairs={{0,32},{32,64},{64,96},{1,33},{33,65},{65,97},{2,34},{34,66},{66,9... | collective-permute-start | bytes 73736 | tf_op jit(solution)/shard_map/while/body/eval_jaxpr/ppermute | solution.py:12
  129.8 13.9 %all-to-all-start = ((f32[16,2,8,384]{3,2,1,0:T(8,128)}), f32[16,2,8,384]{3,2,1,0:T(8,128)S(1)}, u32[]{:S(2)}, u32[]{:S(2)}) async-start(f32[16,2,8,384]{3,2,1,0:T(8,128)} %broadcast_in_dim.24), calls=%async_computation | async-start | bytes 786432 | tf_op jit(solution)/shard_map/while/body/eval_jaxpr/all_to_all | solution.py:23
  143.7 10.6 %copy-start = (f32[384,6144]{1,0:T(8,128)S(1)}, f32[384,6144]{1,0:T(8,128)}, u32[]{:S(2)}) copy-start(f32[384,6144]{1,0:T(8,128)} %get-tuple-element.408) | copy-start | bytes 28311556 | tf_op jit(solution)/shard_map/while
  162.2 6.1 %collective-permute-start.1 = (f32[2,8,384]{2,1,0:T(8,128)S(1)}, f32[2,8,384]{2,1,0:T(8,128)S(1)}, u32[]{:S(2)}, u32[]{:S(2)}) collective-permute-start(f32[2,8,384]{2,1,0:T(8,128)S(1)} %broadcast_select_fusion.2), channel_id=1, source_target_pairs={{0,16},{1,17},{2,18},{3,19},{4,20},{5,21},{6,22},{7,23},{8,24},{9,... | collective-permute-start | bytes 73736 | tf_op jit(solution)/shard_map/while/body/eval_jaxpr/ppermute | solution.py:12
  163.5 4.8 %collective-permute-start = (f32[2,8,384]{2,1,0:T(8,128)S(1)}, f32[2,8,384]{2,1,0:T(8,128)S(1)}, u32[]{:S(2)}, u32[]{:S(2)}) collective-permute-start(f32[2,8,384]{2,1,0:T(8,128)S(1)} %broadcast_select_fusion.2), channel_id=1, source_target_pairs={{0,32},{32,64},{64,96},{1,33},{33,65},{65,97},{2,34},{34,66},{66,9... | collective-permute-start | bytes 73736 | tf_op jit(solution)/shard_map/while/body/eval_jaxpr/ppermute | solution.py:12
  169.8 13.9 %all-to-all-start = ((f32[16,2,8,384]{3,2,1,0:T(8,128)}), f32[16,2,8,384]{3,2,1,0:T(8,128)S(1)}, u32[]{:S(2)}, u32[]{:S(2)}) async-start(f32[16,2,8,384]{3,2,1,0:T(8,128)} %broadcast_in_dim.24), calls=%async_computation | async-start | bytes 786432 | tf_op jit(solution)/shard_map/while/body/eval_jaxpr/all_to_all | solution.py:23
  183.7 10.6 %copy-start = (f32[384,6144]{1,0:T(8,128)S(1)}, f32[384,6144]{1,0:T(8,128)}, u32[]{:S(2)}) copy-start(f32[384,6144]{1,0:T(8,128)} %get-tuple-element.408) | copy-start | bytes 28311556 | tf_op jit(solution)/shard_map/while
  202.2 6.1 %collective-permute-start.1 = (f32[2,8,384]{2,1,0:T(8,128)S(1)}, f32[2,8,384]{2,1,0:T(8,128)S(1)}, u32[]{:S(2)}, u32[]{:S(2)}) collective-permute-start(f32[2,8,384]{2,1,0:T(8,128)S(1)} %broadcast_select_fusion.2), channel_id=1, source_target_pairs={{0,16},{1,17},{2,18},{3,19},{4,20},{5,21},{6,22},{7,23},{8,24},{9,... | collective-permute-start | bytes 73736 | tf_op jit(solution)/shard_map/while/body/eval_jaxpr/ppermute | solution.py:12
  203.5 4.8 %collective-permute-start = (f32[2,8,384]{2,1,0:T(8,128)S(1)}, f32[2,8,384]{2,1,0:T(8,128)S(1)}, u32[]{:S(2)}, u32[]{:S(2)}) collective-permute-start(f32[2,8,384]{2,1,0:T(8,128)S(1)} %broadcast_select_fusion.2), channel_id=1, source_target_pairs={{0,32},{32,64},{64,96},{1,33},{33,65},{65,97},{2,34},{34,66},{66,9... | collective-permute-start | bytes 73736 | tf_op jit(solution)/shard_map/while/body/eval_jaxpr/ppermute | solution.py:12
  209.9 13.9 %all-to-all-start = ((f32[16,2,8,384]{3,2,1,0:T(8,128)}), f32[16,2,8,384]{3,2,1,0:T(8,128)S(1)}, u32[]{:S(2)}, u32[]{:S(2)}) async-start(f32[16,2,8,384]{3,2,1,0:T(8,128)} %broadcast_in_dim.24), calls=%async_computation | async-start | bytes 786432 | tf_op jit(solution)/shard_map/while/body/eval_jaxpr/all_to_all | solution.py:23
  223.7 10.6 %copy-start = (f32[384,6144]{1,0:T(8,128)S(1)}, f32[384,6144]{1,0:T(8,128)}, u32[]{:S(2)}) copy-start(f32[384,6144]{1,0:T(8,128)} %get-tuple-element.408) | copy-start | bytes 28311556 | tf_op jit(solution)/shard_map/while
  242.2 6.1 %collective-permute-start.1 = (f32[2,8,384]{2,1,0:T(8,128)S(1)}, f32[2,8,384]{2,1,0:T(8,128)S(1)}, u32[]{:S(2)}, u32[]{:S(2)}) collective-permute-start(f32[2,8,384]{2,1,0:T(8,128)S(1)} %broadcast_select_fusion.2), channel_id=1, source_target_pairs={{0,16},{1,17},{2,18},{3,19},{4,20},{5,21},{6,22},{7,23},{8,24},{9,... | collective-permute-start | bytes 73736 | tf_op jit(solution)/shard_map/while/body/eval_jaxpr/ppermute | solution.py:12
  243.5 4.8 %collective-permute-start = (f32[2,8,384]{2,1,0:T(8,128)S(1)}, f32[2,8,384]{2,1,0:T(8,128)S(1)}, u32[]{:S(2)}, u32[]{:S(2)}) collective-permute-start(f32[2,8,384]{2,1,0:T(8,128)S(1)} %broadcast_select_fusion.2), channel_id=1, source_target_pairs={{0,32},{32,64},{64,96},{1,33},{33,65},{65,97},{2,34},{34,66},{66,9... | collective-permute-start | bytes 73736 | tf_op jit(solution)/shard_map/while/body/eval_jaxpr/ppermute | solution.py:12
  249.9 13.9 %all-to-all-start = ((f32[16,2,8,384]{3,2,1,0:T(8,128)}), f32[16,2,8,384]{3,2,1,0:T(8,128)S(1)}, u32[]{:S(2)}, u32[]{:S(2)}) async-start(f32[16,2,8,384]{3,2,1,0:T(8,128)} %broadcast_in_dim.24), calls=%async_computation | async-start | bytes 786432 | tf_op jit(solution)/shard_map/while/body/eval_jaxpr/all_to_all | solution.py:23
  263.8 10.6 %copy-start = (f32[384,6144]{1,0:T(8,128)S(1)}, f32[384,6144]{1,0:T(8,128)}, u32[]{:S(2)}) copy-start(f32[384,6144]{1,0:T(8,128)} %get-tuple-element.408) | copy-start | bytes 28311556 | tf_op jit(solution)/shard_map/while
  282.3 6.1 %collective-permute-start.1 = (f32[2,8,384]{2,1,0:T(8,128)S(1)}, f32[2,8,384]{2,1,0:T(8,128)S(1)}, u32[]{:S(2)}, u32[]{:S(2)}) collective-permute-start(f32[2,8,384]{2,1,0:T(8,128)S(1)} %broadcast_select_fusion.2), channel_id=1, source_target_pairs={{0,16},{1,17},{2,18},{3,19},{4,20},{5,21},{6,22},{7,23},{8,24},{9,... | collective-permute-start | bytes 73736 | tf_op jit(solution)/shard_map/while/body/eval_jaxpr/ppermute | solution.py:12
  283.6 4.8 %collective-permute-start = (f32[2,8,384]{2,1,0:T(8,128)S(1)}, f32[2,8,384]{2,1,0:T(8,128)S(1)}, u32[]{:S(2)}, u32[]{:S(2)}) collective-permute-start(f32[2,8,384]{2,1,0:T(8,128)S(1)} %broadcast_select_fusion.2), channel_id=1, source_target_pairs={{0,32},{32,64},{64,96},{1,33},{33,65},{65,97},{2,34},{34,66},{66,9... | collective-permute-start | bytes 73736 | tf_op jit(solution)/shard_map/while/body/eval_jaxpr/ppermute | solution.py:12
  289.9 13.9 %all-to-all-start = ((f32[16,2,8,384]{3,2,1,0:T(8,128)}), f32[16,2,8,384]{3,2,1,0:T(8,128)S(1)}, u32[]{:S(2)}, u32[]{:S(2)}) async-start(f32[16,2,8,384]{3,2,1,0:T(8,128)} %broadcast_in_dim.24), calls=%async_computation | async-start | bytes 786432 | tf_op jit(solution)/shard_map/while/body/eval_jaxpr/all_to_all | solution.py:23
  303.8 10.6 %copy-start = (f32[384,6144]{1,0:T(8,128)S(1)}, f32[384,6144]{1,0:T(8,128)}, u32[]{:S(2)}) copy-start(f32[384,6144]{1,0:T(8,128)} %get-tuple-element.408) | copy-start | bytes 28311556 | tf_op jit(solution)/shard_map/while
  322.3 6.1 %collective-permute-start.1 = (f32[2,8,384]{2,1,0:T(8,128)S(1)}, f32[2,8,384]{2,1,0:T(8,128)S(1)}, u32[]{:S(2)}, u32[]{:S(2)}) collective-permute-start(f32[2,8,384]{2,1,0:T(8,128)S(1)} %broadcast_select_fusion.2), channel_id=1, source_target_pairs={{0,16},{1,17},{2,18},{3,19},{4,20},{5,21},{6,22},{7,23},{8,24},{9,... | collective-permute-start | bytes 73736 | tf_op jit(solution)/shard_map/while/body/eval_jaxpr/ppermute | solution.py:12
  323.6 4.8 %collective-permute-start = (f32[2,8,384]{2,1,0:T(8,128)S(1)}, f32[2,8,384]{2,1,0:T(8,128)S(1)}, u32[]{:S(2)}, u32[]{:S(2)}) collective-permute-start(f32[2,8,384]{2,1,0:T(8,128)S(1)} %broadcast_select_fusion.2), channel_id=1, source_target_pairs={{0,32},{32,64},{64,96},{1,33},{33,65},{65,97},{2,34},{34,66},{66,9... | collective-permute-start | bytes 73736 | tf_op jit(solution)/shard_map/while/body/eval_jaxpr/ppermute | solution.py:12
  330.0 13.9 %all-to-all-start = ((f32[16,2,8,384]{3,2,1,0:T(8,128)}), f32[16,2,8,384]{3,2,1,0:T(8,128)S(1)}, u32[]{:S(2)}, u32[]{:S(2)}) async-start(f32[16,2,8,384]{3,2,1,0:T(8,128)} %broadcast_in_dim.24), calls=%async_computation | async-start | bytes 786432 | tf_op jit(solution)/shard_map/while/body/eval_jaxpr/all_to_all | solution.py:23
  343.8 10.6 %copy-start = (f32[384,6144]{1,0:T(8,128)S(1)}, f32[384,6144]{1,0:T(8,128)}, u32[]{:S(2)}) copy-start(f32[384,6144]{1,0:T(8,128)} %get-tuple-element.408) | copy-start | bytes 28311556 | tf_op jit(solution)/shard_map/while
  362.3 6.1 %collective-permute-start.1 = (f32[2,8,384]{2,1,0:T(8,128)S(1)}, f32[2,8,384]{2,1,0:T(8,128)S(1)}, u32[]{:S(2)}, u32[]{:S(2)}) collective-permute-start(f32[2,8,384]{2,1,0:T(8,128)S(1)} %broadcast_select_fusion.2), channel_id=1, source_target_pairs={{0,16},{1,17},{2,18},{3,19},{4,20},{5,21},{6,22},{7,23},{8,24},{9,... | collective-permute-start | bytes 73736 | tf_op jit(solution)/shard_map/while/body/eval_jaxpr/ppermute | solution.py:12
  363.6 4.8 %collective-permute-start = (f32[2,8,384]{2,1,0:T(8,128)S(1)}, f32[2,8,384]{2,1,0:T(8,128)S(1)}, u32[]{:S(2)}, u32[]{:S(2)}) collective-permute-start(f32[2,8,384]{2,1,0:T(8,128)S(1)} %broadcast_select_fusion.2), channel_id=1, source_target_pairs={{0,32},{32,64},{64,96},{1,33},{33,65},{65,97},{2,34},{34,66},{66,9... | collective-permute-start | bytes 73736 | tf_op jit(solution)/shard_map/while/body/eval_jaxpr/ppermute | solution.py:12
  370.0 13.9 %all-to-all-start = ((f32[16,2,8,384]{3,2,1,0:T(8,128)}), f32[16,2,8,384]{3,2,1,0:T(8,128)S(1)}, u32[]{:S(2)}, u32[]{:S(2)}) async-start(f32[16,2,8,384]{3,2,1,0:T(8,128)} %broadcast_in_dim.24), calls=%async_computation | async-start | bytes 786432 | tf_op jit(solution)/shard_map/while/body/eval_jaxpr/all_to_all | solution.py:23
  383.9 10.6 %copy-start = (f32[384,6144]{1,0:T(8,128)S(1)}, f32[384,6144]{1,0:T(8,128)}, u32[]{:S(2)}) copy-start(f32[384,6144]{1,0:T(8,128)} %get-tuple-element.408) | copy-start | bytes 28311556 | tf_op jit(solution)/shard_map/while
  402.4 0.6 copy-start.1
where the time goes:
time: 410 us; the launch traced here: 403 us
  matrix products  182 us (44%)
  waiting for transfers between devices  113 us (28%)
  starting transfers between devices  80.2 us (20%)
  local copies, waits for them, and re-layouts  18.8 us (5%)
  other arithmetic  8.01 us (2%)
    dot_general x20, matrix products, contract(): lax.dot_general(left, right, (((1,), (1,)), ((), ())), precision=lax.Prec...  182 us
    all_to_all x10, waiting for transfers between devices, from_everyone(): return lax.all_to_all(copies, axis, split_axis=0, concat_axis=0, tiled=True)  86.3 us
    all_to_all x10, starting transfers between devices, from_everyone(): return lax.all_to_all(copies, axis, split_axis=0, concat_axis=0, tiled=True)  54.4 us
    ppermute x20, waiting for transfers between devices, from_behind(): return lax.ppermute(value, axis, pairs)  26.8 us
    ppermute x20, starting transfers between devices, from_behind(): return lax.ppermute(value, axis, pairs)  25.8 us
  transfers between devices with their start and end apart: 30, of which 20 were waited for; matrix products, arithmetic and copies ran while one was open for 2% of the time, Pallas kernels for 0%

commit v1 on v0

v1 whole, which is shorter than its diff:
```python
import functools

import jax
import jax.numpy as jnp
from jax import lax
from jax.experimental import pallas as pl
from jax.experimental.pallas import tpu as pltpu
from jax.sharding import Mesh
from jax.sharding import PartitionSpec as P

BF = jnp.bfloat16
F32 = jnp.float32
CHIPS = ("y", "zl")
VMEM_LIMIT = 12 * 1024 * 1024


def split(value):
    high = value.astype(BF)
    return high, (value - high.astype(F32)).astype(BF)


def prepare_body(
    fields_ref, real_hbm, imag_hbm, own_hi, own_lo, other_hi, other_lo, copies_ref, stage, sems
):
    rows, width = real_hbm.shape
    blocks = width // rows // 2
    which = lax.axis_index("core")

    def copies(at, slot):
        half, block = divmod(at, blocks)
        column = (2 * block + (which if half == 0 else 1 - which)) * rows
        column = pl.multiple_of(column, 128)
        return [
            pltpu.make_async_copy(ref.at[:, pl.ds(column, rows)], stage.at[slot, part], sems.at[slot, part])
            for part, ref in enumerate((real_hbm, imag_hbm))
        ]

    depth = stage.shape[0]
    for at in range(depth - 1):
        for copy in copies(at, at):
            copy.start()
    for at in range(2 * blocks):
        ahead = at + depth - 1
        if ahead < 2 * blocks:
            for copy in copies(ahead, ahead % depth):
                copy.start()
        for copy in copies(at, at % depth):
            copy.wait()
        half, block = divmod(at, blocks)
        hi_ref, lo_ref = ((own_hi, own_lo), (other_hi, other_lo))[half]
        for part in range(2):
            hi, lo = split(stage[at % depth, part])
            where = (pl.ds(block * rows, rows), pl.ds(part * rows, rows))
            hi_ref[where] = hi.T
            lo_ref[where] = lo.T
    for at in range(copies_ref.shape[0]):
        copies_ref[at] = fields_ref[...]


def prepare(fields, real_rows, imag_rows):
    rows, width = real_rows.shape
    half = pltpu.VMEM((width // 2, 2 * rows), BF)
    vmem = pl.BlockSpec(memory_space=pltpu.VMEM)
    return pl.pallas_call(
        prepare_body,
        in_specs=[
            vmem,
            pl.BlockSpec(memory_space=pltpu.HBM),
            pl.BlockSpec(memory_space=pltpu.HBM),
        ],
        out_specs=[vmem] * 5,
        out_shape=[half] * 4 + [jax.ShapeDtypeStruct((lax.axis_size(CHIPS), *fields.shape), F32)],
        scratch_shapes=[
            pltpu.VMEM((4, 2, rows, rows), F32),
            pltpu.SemaphoreType.DMA((4, 2)),
        ],
        compiler_params=pltpu.CompilerParams(vmem_limit_bytes=VMEM_LIMIT),
        cost_estimate=pl.CostEstimate(flops=0, transcendentals=0, bytes_accessed=8 * rows * width),
        name="prepare",
    )(
        fields,
        pltpu.with_memory_space_constraint(real_rows, pltpu.HBM),
        pltpu.with_memory_space_constraint(imag_rows, pltpu.HBM),
    )


def product(blocks_ref, hi_ref, lo_ref, xs):
    count, _, sources, rows = blocks_ref.shape
    for at in range(count):
        hi, lo = split(blocks_ref[at].reshape(2 * sources, rows))
        xs[: 2 * sources, pl.ds(at * rows, rows)] = hi
        xs[2 * sources :, pl.ds(at * rows, rows)] = lo
    dims = (((1,), (0,)), ((), ()))
    both = lax.dot_general(xs[...], hi_ref[...], dims, preferred_element_type=F32)
    rest = lax.dot_general(xs[: 2 * sources, :], lo_ref[...], dims, preferred_element_type=F32)
    return both[: 2 * sources] + both[2 * sources :] + rest


def diagonal():
    return lax.axis_index("sx") + lax.axis_index("sy")


def first_half_body(turn, blocks_ref, hi_ref, lo_ref, out_ref, xs):
    @pl.when(diagonal() == turn)
    def _():
        out_ref[...] = product(blocks_ref, hi_ref, lo_ref, xs)


def second_half_body(turn, blocks_ref, hi_ref, lo_ref, first_ref, before_ref, out_ref, xs):
    sources, rows = out_ref.shape[1:]

    @pl.when(diagonal() == turn)
    def _():
        total = first_ref[...] + product(blocks_ref, hi_ref, lo_ref, xs)
        with_real = total[:, :rows]
        with_imag = total[:, rows:]
        out_ref[0] = with_real[:sources] - with_imag[sources:]
        out_ref[1] = with_imag[:sources] + with_real[sources:]

    @pl.when(diagonal() != turn)
    def _():
        out_ref[...] = before_ref[...]


def half_call(body, turn, out_shape, blocks, *operands, name):
    vmem = pl.BlockSpec(memory_space=pltpu.VMEM)
    count, _, sources, rows = blocks.shape
    return pl.pallas_call(
        functools.partial(body, turn),
        in_specs=[vmem] * (1 + len(operands)),
        out_specs=vmem,
        out_shape=jax.ShapeDtypeStruct(out_shape, F32),
        scratch_shapes=[pltpu.VMEM((4 * sources, count * rows), BF)],
        compiler_params=pltpu.CompilerParams(vmem_limit_bytes=VMEM_LIMIT),
        name=name,
    )(blocks, *operands)


def scaled(coef, field):
    real_part = coef[0:1] * field[0] - coef[1:2] * field[1]
    imag_part = coef[0:1] * field[1] + coef[1:2] * field[0]
    return real_part, imag_part


def combine_body(fields_ref, right_ref, upper_ref, left_ref, below_ref, copies_ref):
    by_left = scaled(right_ref[...], left_ref[...])
    by_below = scaled(upper_ref[...], below_ref[...])
    for part in range(2):
        incoming = fields_ref[part] + by_left[part] + by_below[part]
        for at in range(copies_ref.shape[0]):
            copies_ref[at, part] = incoming


def combine(fields, right_coef, upper_coef, from_left, from_below):
    vmem = pl.BlockSpec(memory_space=pltpu.VMEM)
    return pl.pallas_call(
        combine_body,
        in_specs=[vmem] * 5,
        out_specs=vmem,
        out_shape=jax.ShapeDtypeStruct((lax.axis_size(CHIPS), *fields.shape), F32),
        compiler_params=pltpu.CompilerParams(vmem_limit_bytes=2 * 1024 * 1024),
        name="combine",
    )(fields, right_coef, upper_coef, from_left, from_below)


def ring(axis):
    size = lax.axis_size(axis)
    return [(i, (i + 1) % size) for i in range(size)]


def gather_chips(copies):
    return lax.all_to_all(copies, CHIPS, split_axis=0, concat_axis=0, tiled=True)


def hand_over(traces, turn, right, up):
    columns, rows = lax.axis_size("sx"), lax.axis_size("sy")
    pairs = []
    for column in range(columns):
        for row in range(rows):
            if column + row == turn and column + right < columns and row + up < rows:
                pairs.append((column * rows + row, (column + right) * rows + row + up))
    return lax.ppermute(traces, ("sx", "sy"), pairs)


def shards(op_real, op_imag, coef_right, coef_upper, sources):
    fields = sources[0, 0]
    _, count, rows = fields.shape
    right_coef = coef_right[0, 0]
    upper_coef = coef_upper[0, 0]
    rounds = lax.axis_size("sx") + lax.axis_size("sy") - 1
    *weights, copies = prepare(fields, op_real[0, 0], op_imag[0, 0])
    own_hi, own_lo, other_hi, other_lo = weights
    traces = fields
    for turn in range(rounds):
        if turn:
            from_left = hand_over(traces, turn - 1, 1, 0)
            from_below = hand_over(traces, turn - 1, 0, 1)
            copies = combine(fields, right_coef, upper_coef, from_left, from_below)
        own = gather_chips(copies)
        other = lax.ppermute(own, "core", ring("core"))
        first = half_call(
            first_half_body, turn, (2 * count, 2 * rows), own, own_hi, own_lo, name="first_half"
        )
        traces = half_call(
            second_half_body, turn, fields.shape, other, other_hi, other_lo, first, traces,
            name="second_half",
        )
    return traces[None, None]


def solution(mesh):
    fine = Mesh(mesh.devices.reshape(4, 2, 4, 2, 2), ("sx", "sy", "y", "zl", "core"))
    op = ("y", "zl", "core")
    return jax.shard_map(
        shards,
        mesh=fine,
        in_specs=(
            P("sx", "sy", op, None),
            P("sx", "sy", op, None),
            P("sx", "sy", None, op),
            P("sx", "sy", None, op),
            P("sx", "sy", None, None, op),
        ),
        out_specs=P("sx", "sy", None, None, op),
        check_vma=False,
    )
```

time: 410 us -> 106 us (0.26); the launches traced: 403 us -> 105 us
  matrix products: 182 us -> 0 us
  waiting for transfers between devices: 113 us -> 23.4 us
  starting transfers between devices: 80.2 us -> 17.1 us
  blocking collectives: 0 us -> 51.6 us
  local copies, waits for them, and re-layouts: 18.8 us -> 0.81 us
  Pallas kernels: 0 us -> 12.2 us
  other arithmetic: 8.01 us -> 0 us
    dot_general x20 -> x0, matrix products: 182 us -> none  [contract(): lax.dot_general(left, right, (((1,), (1,)), ((), ())), precision=lax.Prec...]
    all_to_all x10 -> x0, waiting for transfers between devices: 86.3 us -> none  [from_everyone(): return lax.all_to_all(copies, axis, split_axis=0, concat_axis=0, tiled=True)]
    all_to_all x10 -> x0, starting transfers between devices: 54.4 us -> none  [from_everyone(): return lax.all_to_all(copies, axis, split_axis=0, concat_axis=0, tiled=True)]
    all_to_all x0 -> x5, blocking collectives: none -> 51.6 us  [gather_chips(): lax.all_to_all(copies, CHIPS, split_axis=0, concat_axis=0, tiled=True)]
    pallas_call x0 -> x15, Pallas kernels: none -> 12.2 us  [the longest x1 8.03 us: prepare(): pl.pallas_call(prepare_body, in_specs=[vmem, pl.BlockSpec(memory_space=pl...]
    ppermute x20 -> x13, starting transfers between devices: 25.8 us -> 17.1 us  [the longest x5 10.4 us: shards(): other = lax.ppermute(own, 'core', ring('core'))]
    slice x10 -> x0, local copies, waits for them, and re-layouts: 7.92 us -> none  [complex_scale(): real_part = coef[0][None, :] * field[0] - coef[1][None, :] * field[1]]
    broadcast_in_dim x11 -> x0, local copies, waits for them, and re-layouts: 7.6 us -> none  [the longest x10 7.6 us: from_everyone(): copies = jnp.broadcast_to(value, (lax.axis_size(axis), *value.shape))]
  transfers between devices with their start and end apart: 30 -> 13, of which waited for: 20 -> 5; matrix products, arithmetic and copies ran while one was open for 2% -> 0% of each run, Pallas kernels for 0% -> 2%
where the time goes in v1:
time: 106 us; the launch traced here: 105 us
  blocking collectives  51.6 us (49%)
  waiting for transfers between devices  23.4 us (22%)
  starting transfers between devices  17.1 us (16%)
  Pallas kernels  12.2 us (12%)
    all_to_all x5, blocking collectives, gather_chips(): lax.all_to_all(copies, CHIPS, split_axis=0, concat_axis=0, tiled=True)  51.6 us
    ppermute x8, waiting for transfers between devices, hand_over(): return lax.ppermute(traces, ('sx', 'sy'), pairs)  18 us
    ppermute x5, starting transfers between devices, shards(): other = lax.ppermute(own, 'core', ring('core'))  10.4 us
    pallas_call x1, Pallas kernels, prepare(): pl.pallas_call(prepare_body, in_specs=[vmem, pl.BlockSpec(memory_space=pl...  8.03 us
    ppermute x8, starting transfers between devices, hand_over(): return lax.ppermute(traces, ('sx', 'sy'), pairs)  6.66 us
    ppermute x5, waiting for transfers between devices, shards(): other = lax.ppermute(own, 'core', ring('core'))  5.4 us
    pallas_call x10, Pallas kernels, half_call(): pl.pallas_call(functools.partial(body, turn), in_specs=[vmem] * (1 + len(...  4.05 us
  transfers between devices with their start and end apart: 13, of which 5 were waited for; matrix products, arithmetic and copies ran while one was open for 0% of the time, Pallas kernels for 2%

profile of v1, /device:TPU:71, one launch (start us, length us, event | category | flops | bytes accessed | tf_op | source)
XLA Modules:
  0.0 105.3 jit_solution(13455342292611641815)
XLA Ops:
  0.0 0.0 copy-start
  0.0 0.8 copy-done
  0.8 8.0 %prepare.1 = (bf16[3072,768]{1,0:T(8,128)(2,1)S(1)}, bf16[3072,768]{1,0:T(8,128)(2,1)S(1)}, bf16[3072,768]{1,0:T(8,128)(2,1)S(1)}, bf16[3072,768]{1,0:T(8,128)(2,1)S(1)}, f32[8,2,16,384]{3,2,1,0:T(8,128)S(1)}) custom-call(f32[2,16,384]{2,1,0:T(8,128)S(1)} %bitcast.6, f32[384,6144]{1,0:T(8,128)} %bitcast.20, f32[384,6144]{1,0:T(8,128)} %bitcast.21), custom_call_target="tpu_custom_call" | custom-call | bytes 18874368 | tf_op jit(solution)/shard_map/prepare/pallas_call | solution.py:64
  8.8 12.2 %all_to_all.25.blocks_ref = f32[8,2,16,384]{3,2,1,0:T(8,128)S(1)} all-to-all(f32[8,2,16,384]{3,2,1,0:T(8,128)S(1)} %get-tuple-element.10), channel_id=1, replica_groups=mesh['sx'=4,'sy'=2,'y'=4,'zl'=2,'core'=2] {'y','zl'}, dimensions={0} | all-to-all | bytes 786432 | tf_op jit(solution)/shard_map/all_to_all | solution.py:172
  21.0 2.3 %collective-permute-start = (f32[8,2,16,384]{3,2,1,0:T(8,128)S(1)}, f32[8,2,16,384]{3,2,1,0:T(8,128)S(1)}, u32[]{:S(2)}, u32[]{:S(2)}) collective-permute-start(f32[8,2,16,384]{3,2,1,0:T(8,128)S(1)} %all_to_all.25.blocks_ref), channel_id=1, source_target_pairs={{0,1},{1,0},{2,3},{3,2},{4,5},{5,4},{6,7},{7,6},{8,9},{9,8},{10,11... | collective-permute-start | bytes 1179656 | tf_op jit(solution)/shard_map/ppermute | solution.py:200
  23.3 1.3 %collective-permute-done.blocks_ref = f32[8,2,16,384]{3,2,1,0:T(8,128)S(1)} collective-permute-done((f32[8,2,16,384]{3,2,1,0:T(8,128)S(1)}, f32[8,2,16,384]{3,2,1,0:T(8,128)S(1)}, u32[]{:S(2)}, u32[]{:S(2)}) %collective-permute-start) | collective-permute-done | bytes 393248 | tf_op jit(solution)/shard_map/ppermute | solution.py:200
  24.7 0.0 copy-start.1
  24.7 0.0 copy-start.2
  24.7 0.8 collective-permute-start.1
  25.5 0.7 collective-permute-start.2
  26.2 0.0 collective-permute-done.1.left_ref
  26.2 0.0 collective-permute-done.2.below_ref
  26.2 0.0 copy-done.1
  26.2 0.0 copy-done.2
  26.3 9.7 %all_to_all.26.blocks_ref = f32[8,2,16,384]{3,2,1,0:T(8,128)S(1)} all-to-all(f32[8,2,16,384]{3,2,1,0:T(8,128)S(1)} %combine.4), channel_id=1, replica_groups=mesh['sx'=4,'sy'=2,'y'=4,'zl'=2,'core'=2] {'y','zl'}, dimensions={0} | all-to-all | bytes 786432 | tf_op jit(solution)/shard_map/all_to_all | solution.py:172
  36.0 2.2 %collective-permute-start.3 = (f32[8,2,16,384]{3,2,1,0:T(8,128)S(1)}, f32[8,2,16,384]{3,2,1,0:T(8,128)S(1)}, u32[]{:S(2)}, u32[]{:S(2)}) collective-permute-start(f32[8,2,16,384]{3,2,1,0:T(8,128)S(1)} %all_to_all.26.blocks_ref), channel_id=1, source_target_pairs={{0,1},{1,0},{2,3},{3,2},{4,5},{5,4},{6,7},{7,6},{8,9},{9,8},{10,11... | collective-permute-start | bytes 1179656 | tf_op jit(solution)/shard_map/ppermute | solution.py:200
  38.1 1.3 %collective-permute-done.3.blocks_ref = f32[8,2,16,384]{3,2,1,0:T(8,128)S(1)} collective-permute-done((f32[8,2,16,384]{3,2,1,0:T(8,128)S(1)}, f32[8,2,16,384]{3,2,1,0:T(8,128)S(1)}, u32[]{:S(2)}, u32[]{:S(2)}) %collective-permute-start.3) | collective-permute-done | bytes 393248 | tf_op jit(solution)/shard_map/ppermute | solution.py:200
  39.5 0.7 collective-permute-start.4
  40.2 0.7 collective-permute-start.5
  40.8 0.0 collective-permute-done.4.left_ref
  40.8 0.0 collective-permute-done.5.below_ref
  40.9 10.0 %all_to_all.27.blocks_ref = f32[8,2,16,384]{3,2,1,0:T(8,128)S(1)} all-to-all(f32[8,2,16,384]{3,2,1,0:T(8,128)S(1)} %combine.5), channel_id=1, replica_groups=mesh['sx'=4,'sy'=2,'y'=4,'zl'=2,'core'=2] {'y','zl'}, dimensions={0} | all-to-all | bytes 786432 | tf_op jit(solution)/shard_map/all_to_all | solution.py:172
  50.9 1.9 %collective-permute-start.6 = (f32[8,2,16,384]{3,2,1,0:T(8,128)S(1)}, f32[8,2,16,384]{3,2,1,0:T(8,128)S(1)}, u32[]{:S(2)}, u32[]{:S(2)}) collective-permute-start(f32[8,2,16,384]{3,2,1,0:T(8,128)S(1)} %all_to_all.27.blocks_ref), channel_id=1, source_target_pairs={{0,1},{1,0},{2,3},{3,2},{4,5},{5,4},{6,7},{7,6},{8,9},{9,8},{10,11... | collective-permute-start | bytes 1179656 | tf_op jit(solution)/shard_map/ppermute | solution.py:200
  52.8 1.3 %collective-permute-done.6.blocks_ref = f32[8,2,16,384]{3,2,1,0:T(8,128)S(1)} collective-permute-done((f32[8,2,16,384]{3,2,1,0:T(8,128)S(1)}, f32[8,2,16,384]{3,2,1,0:T(8,128)S(1)}, u32[]{:S(2)}, u32[]{:S(2)}) %collective-permute-start.6) | collective-permute-done | bytes 393248 | tf_op jit(solution)/shard_map/ppermute | solution.py:200
  54.1 0.7 collective-permute-start.7
  54.8 0.7 collective-permute-start.8
  55.5 0.0 collective-permute-done.7.left_ref
  55.5 0.0 collective-permute-done.8.below_ref
  55.5 10.0 %all_to_all.28.blocks_ref = f32[8,2,16,384]{3,2,1,0:T(8,128)S(1)} all-to-all(f32[8,2,16,384]{3,2,1,0:T(8,128)S(1)} %combine.6), channel_id=1, replica_groups=mesh['sx'=4,'sy'=2,'y'=4,'zl'=2,'core'=2] {'y','zl'}, dimensions={0} | all-to-all | bytes 786432 | tf_op jit(solution)/shard_map/all_to_all | solution.py:172
  65.5 1.9 %collective-permute-start.9 = (f32[8,2,16,384]{3,2,1,0:T(8,128)S(1)}, f32[8,2,16,384]{3,2,1,0:T(8,128)S(1)}, u32[]{:S(2)}, u32[]{:S(2)}) collective-permute-start(f32[8,2,16,384]{3,2,1,0:T(8,128)S(1)} %all_to_all.28.blocks_ref), channel_id=1, source_target_pairs={{0,1},{1,0},{2,3},{3,2},{4,5},{5,4},{6,7},{7,6},{8,9},{9,8},{10,11... | collective-permute-start | bytes 1179656 | tf_op jit(solution)/shard_map/ppermute | solution.py:200
  67.4 1.3 %collective-permute-done.9.blocks_ref = f32[8,2,16,384]{3,2,1,0:T(8,128)S(1)} collective-permute-done((f32[8,2,16,384]{3,2,1,0:T(8,128)S(1)}, f32[8,2,16,384]{3,2,1,0:T(8,128)S(1)}, u32[]{:S(2)}, u32[]{:S(2)}) %collective-permute-start.9) | collective-permute-done | bytes 393248 | tf_op jit(solution)/shard_map/ppermute | solution.py:200
  68.8 1.3 %collective-permute-start.10 = (f32[2,16,384]{2,1,0:T(8,128)S(1)}, f32[2,16,384]{2,1,0:T(8,128)S(1)}, u32[]{:S(2)}, u32[]{:S(2)}) collective-permute-start(f32[2,16,384]{2,1,0:T(8,128)S(1)} %second_half.8.before_ref), channel_id=1, source_target_pairs={{80,112},{81,113},{82,114},{83,115},{84,116},{85,117},{86,118},{87... | collective-permute-start | bytes 147464 | tf_op jit(solution)/shard_map/ppermute | solution.py:182
  70.1 1.3 %collective-permute-start.11 = (f32[2,16,384]{2,1,0:T(8,128)S(1)}, f32[2,16,384]{2,1,0:T(8,128)S(1)}, u32[]{:S(2)}, u32[]{:S(2)}) collective-permute-start(f32[2,16,384]{2,1,0:T(8,128)S(1)} %second_half.8.before_ref), channel_id=1, source_target_pairs={{96,112},{97,113},{98,114},{99,115},{100,116},{101,117},{102,118},... | collective-permute-start | bytes 147464 | tf_op jit(solution)/shard_map/ppermute | solution.py:182
  71.4 17.9 %collective-permute-done.10.left_ref = f32[2,16,384]{2,1,0:T(8,128)S(1)} collective-permute-done((f32[2,16,384]{2,1,0:T(8,128)S(1)}, f32[2,16,384]{2,1,0:T(8,128)S(1)}, u32[]{:S(2)}, u32[]{:S(2)}) %collective-permute-start.10) | collective-permute-done | bytes 49184 | tf_op jit(solution)/shard_map/ppermute | solution.py:182
  89.3 0.0 collective-permute-done.11.below_ref
  89.3 9.7 %all_to_all.29.blocks_ref = f32[8,2,16,384]{3,2,1,0:T(8,128)S(1)} all-to-all(f32[8,2,16,384]{3,2,1,0:T(8,128)S(1)} %combine.7), channel_id=1, replica_groups=mesh['sx'=4,'sy'=2,'y'=4,'zl'=2,'core'=2] {'y','zl'}, dimensions={0} | all-to-all | bytes 786432 | tf_op jit(solution)/shard_map/all_to_all | solution.py:172
  99.0 2.2 %collective-permute-start.12 = (f32[8,2,16,384]{3,2,1,0:T(8,128)S(1)}, f32[8,2,16,384]{3,2,1,0:T(8,128)S(1)}, u32[]{:S(2)}, u32[]{:S(2)}) collective-permute-start(f32[8,2,16,384]{3,2,1,0:T(8,128)S(1)} %all_to_all.29.blocks_ref), channel_id=1, source_target_pairs={{0,1},{1,0},{2,3},{3,2},{4,5},{5,4},{6,7},{7,6},{8,9},{9,8},{10,11... | collective-permute-start | bytes 1179656 | tf_op jit(solution)/shard_map/ppermute | solution.py:200
  101.2 1.7 %first_half.9.first_ref = f32[32,768]{1,0:T(8,128)S(1)} custom-call(f32[8,2,16,384]{3,2,1,0:T(8,128)S(1)} %all_to_all.29.blocks_ref, bf16[3072,768]{1,0:T(8,128)(2,1)S(1)} %get-tuple-element.13.hi_ref, bf16[3072,768]{1,0:T(8,128)(2,1)S(1)} %get-tuple-element.14.lo_ref), custom_call_target="tpu_custom_call" | custom-call | tf_op jit(solution)/shard_map/first_half/pallas_call | solution.py:128
  102.9 0.0 collective-permute-done.12.blocks_ref
  102.9 2.3 %second_half.9 = f32[2,16,384]{2,1,0:T(8,128)} custom-call(f32[8,2,16,384]{3,2,1,0:T(8,128)S(1)} %collective-permute-done.12.blocks_ref, bf16[3072,768]{1,0:T(8,128)(2,1)S(1)} %get-tuple-element.11.hi_ref, bf16[3072,768]{1,0:T(8,128)(2,1)S(1)} %get-tuple-element.12.lo_ref, f32[32,768]{1,0:T(8,128)S(1)} %first_half.9.first_ref, ...), custom_call_target="tpu_custom_call" | custom-call | tf_op jit(solution)/shard_map/second_half/pallas_call | solution.py:128
  (12 shorter events, 0.2 us)
Async XLA Ops:
  0.0 0.8 copy-start
  21.0 3.6 %collective-permute-start = (f32[8,2,16,384]{3,2,1,0:T(8,128)S(1)}, f32[8,2,16,384]{3,2,1,0:T(8,128)S(1)}, u32[]{:S(2)}, u32[]{:S(2)}) collective-permute-start(f32[8,2,16,384]{3,2,1,0:T(8,128)S(1)} %all_to_all.25.blocks_ref), channel_id=1, source_target_pairs={{0,1},{1,0},{2,3},{3,2},{4,5},{5,4},{6,7},{7,6},{8,9},{9,8},{10,11... | collective-permute-start | bytes 1179656 | tf_op jit(solution)/shard_map/ppermute | solution.py:200
  24.7 1.5 %copy-start.1 = (f32[1,1,2,384]{3,2,1,0:T(2,128)S(1)}, f32[1,1,2,384]{3,2,1,0:T(2,128)}, u32[]{:S(2)}) copy-start(f32[1,1,2,384]{3,2,1,0:T(2,128)} %param.7) | copy-start | bytes 9220
  24.7 1.5 %copy-start.2 = (f32[1,1,2,384]{3,2,1,0:T(2,128)S(1)}, f32[1,1,2,384]{3,2,1,0:T(2,128)}, u32[]{:S(2)}) copy-start(f32[1,1,2,384]{3,2,1,0:T(2,128)} %param.8) | copy-start | bytes 9220
  24.7 1.5 %collective-permute-start.1 = (f32[2,16,384]{2,1,0:T(8,128)S(1)}, f32[2,16,384]{2,1,0:T(8,128)S(1)}, u32[]{:S(2)}, u32[]{:S(2)}) collective-permute-start(f32[2,16,384]{2,1,0:T(8,128)S(1)} %second_half.5.before_ref), channel_id=1, source_target_pairs={{0,32},{1,33},{2,34},{3,35},{4,36},{5,37},{6,38},{7,39},{8,40},{9,... | collective-permute-start | bytes 147464 | tf_op jit(solution)/shard_map/ppermute | solution.py:182
  25.5 0.7 collective-permute-start.2
  36.0 3.5 %collective-permute-start.3 = (f32[8,2,16,384]{3,2,1,0:T(8,128)S(1)}, f32[8,2,16,384]{3,2,1,0:T(8,128)S(1)}, u32[]{:S(2)}, u32[]{:S(2)}) collective-permute-start(f32[8,2,16,384]{3,2,1,0:T(8,128)S(1)} %all_to_all.26.blocks_ref), channel_id=1, source_target_pairs={{0,1},{1,0},{2,3},{3,2},{4,5},{5,4},{6,7},{7,6},{8,9},{9,8},{10,11... | collective-permute-start | bytes 1179656 | tf_op jit(solution)/shard_map/ppermute | solution.py:200
  39.5 1.3 %collective-permute-start.4 = (f32[2,16,384]{2,1,0:T(8,128)S(1)}, f32[2,16,384]{2,1,0:T(8,128)S(1)}, u32[]{:S(2)}, u32[]{:S(2)}) collective-permute-start(f32[2,16,384]{2,1,0:T(8,128)S(1)} %second_half.6.before_ref), channel_id=1, source_target_pairs={{16,48},{32,64},{17,49},{33,65},{18,50},{34,66},{19,51},{35,67},{2... | collective-permute-start | bytes 147464 | tf_op jit(solution)/shard_map/ppermute | solution.py:182
  40.2 0.7 collective-permute-start.5
  50.9 3.2 %collective-permute-start.6 = (f32[8,2,16,384]{3,2,1,0:T(8,128)S(1)}, f32[8,2,16,384]{3,2,1,0:T(8,128)S(1)}, u32[]{:S(2)}, u32[]{:S(2)}) collective-permute-start(f32[8,2,16,384]{3,2,1,0:T(8,128)S(1)} %all_to_all.27.blocks_ref), channel_id=1, source_target_pairs={{0,1},{1,0},{2,3},{3,2},{4,5},{5,4},{6,7},{7,6},{8,9},{9,8},{10,11... | collective-permute-start | bytes 1179656 | tf_op jit(solution)/shard_map/ppermute | solution.py:200
  54.1 1.3 %collective-permute-start.7 = (f32[2,16,384]{2,1,0:T(8,128)S(1)}, f32[2,16,384]{2,1,0:T(8,128)S(1)}, u32[]{:S(2)}, u32[]{:S(2)}) collective-permute-start(f32[2,16,384]{2,1,0:T(8,128)S(1)} %second_half.7.before_ref), channel_id=1, source_target_pairs={{48,80},{64,96},{49,81},{65,97},{50,82},{66,98},{51,83},{67,99},{5... | collective-permute-start | bytes 147464 | tf_op jit(solution)/shard_map/ppermute | solution.py:182
  54.8 0.7 collective-permute-start.8
  65.5 3.2 %collective-permute-start.9 = (f32[8,2,16,384]{3,2,1,0:T(8,128)S(1)}, f32[8,2,16,384]{3,2,1,0:T(8,128)S(1)}, u32[]{:S(2)}, u32[]{:S(2)}) collective-permute-start(f32[8,2,16,384]{3,2,1,0:T(8,128)S(1)} %all_to_all.28.blocks_ref), channel_id=1, source_target_pairs={{0,1},{1,0},{2,3},{3,2},{4,5},{5,4},{6,7},{7,6},{8,9},{9,8},{10,11... | collective-permute-start | bytes 1179656 | tf_op jit(solution)/shard_map/ppermute | solution.py:200
  68.8 20.5 %collective-permute-start.10 = (f32[2,16,384]{2,1,0:T(8,128)S(1)}, f32[2,16,384]{2,1,0:T(8,128)S(1)}, u32[]{:S(2)}, u32[]{:S(2)}) collective-permute-start(f32[2,16,384]{2,1,0:T(8,128)S(1)} %second_half.8.before_ref), channel_id=1, source_target_pairs={{80,112},{81,113},{82,114},{83,115},{84,116},{85,117},{86,118},{87... | collective-permute-start | bytes 147464 | tf_op jit(solution)/shard_map/ppermute | solution.py:182
  70.1 19.3 %collective-permute-start.11 = (f32[2,16,384]{2,1,0:T(8,128)S(1)}, f32[2,16,384]{2,1,0:T(8,128)S(1)}, u32[]{:S(2)}, u32[]{:S(2)}) collective-permute-start(f32[2,16,384]{2,1,0:T(8,128)S(1)} %second_half.8.before_ref), channel_id=1, source_target_pairs={{96,112},{97,113},{98,114},{99,115},{100,116},{101,117},{102,118},... | collective-permute-start | bytes 147464 | tf_op jit(solution)/shard_map/ppermute | solution.py:182
  99.0 3.9 %collective-permute-start.12 = (f32[8,2,16,384]{3,2,1,0:T(8,128)S(1)}, f32[8,2,16,384]{3,2,1,0:T(8,128)S(1)}, u32[]{:S(2)}, u32[]{:S(2)}) collective-permute-start(f32[8,2,16,384]{3,2,1,0:T(8,128)S(1)} %all_to_all.29.blocks_ref), channel_id=1, source_target_pairs={{0,1},{1,0},{2,3},{3,2},{4,5},{5,4},{6,7},{7,6},{8,9},{9,8},{10,11... | collective-permute-start | bytes 1179656 | tf_op jit(solution)/shard_map/ppermute | solution.py:200

commit v2 on v1

--- a/solution.py
+++ b/solution.py
@@ -19,77 +19,78 @@
     return high, (value - high.astype(F32)).astype(BF)
 
 
-def prepare_body(
-    fields_ref, real_hbm, imag_hbm, own_hi, own_lo, other_hi, other_lo, copies_ref, stage, sems
-):
+def prepare_body(other, real_hbm, imag_hbm, *refs):
+    hi_ref, lo_ref, stage, sems = refs[-4:]
     rows, width = real_hbm.shape
     blocks = width // rows // 2
     which = lax.axis_index("core")
-
-    def copies(at, slot):
-        half, block = divmod(at, blocks)
-        column = (2 * block + (which if half == 0 else 1 - which)) * rows
-        column = pl.multiple_of(column, 128)
+    which = 1 - which if other else which
+
+    def copies(block, slot):
+        column = pl.multiple_of((2 * block + which) * rows, 128)
         return [
             pltpu.make_async_copy(ref.at[:, pl.ds(column, rows)], stage.at[slot, part], sems.at[slot, part])
             for part, ref in enumerate((real_hbm, imag_hbm))
         ]
 
     depth = stage.shape[0]
-    for at in range(depth - 1):
-        for copy in copies(at, at):
+    for block in range(depth - 1):
+        for copy in copies(block, block):
             copy.start()
-    for at in range(2 * blocks):
-        ahead = at + depth - 1
-        if ahead < 2 * blocks:
+    for block in range(blocks):
+        ahead = block + depth - 1
+        if ahead < blocks:
             for copy in copies(ahead, ahead % depth):
                 copy.start()
-        for copy in copies(at, at % depth):
+        for copy in copies(block, block % depth):
             copy.wait()
-        half, block = divmod(at, blocks)
-        hi_ref, lo_ref = ((own_hi, own_lo), (other_hi, other_lo))[half]
         for part in range(2):
-            hi, lo = split(stage[at % depth, part])
+            hi, lo = split(stage[block % depth, part])
             where = (pl.ds(block * rows, rows), pl.ds(part * rows, rows))
             hi_ref[where] = hi.T
             lo_ref[where] = lo.T
-    for at in range(copies_ref.shape[0]):
-        copies_ref[at] = fields_ref[...]
-
-
-def prepare(fields, real_rows, imag_rows):
+
+
+def prepare(other, real_rows, imag_rows, *after):
     rows, width = real_rows.shape
     half = pltpu.VMEM((width // 2, 2 * rows), BF)
-    vmem = pl.BlockSpec(memory_space=pltpu.VMEM)
-    return pl.pallas_call(
-        prepare_body,
+    return pl.pallas_call(
+        functools.partial(prepare_body, other),
         in_specs=[
-            vmem,
             pl.BlockSpec(memory_space=pltpu.HBM),
             pl.BlockSpec(memory_space=pltpu.HBM),
+            *[pl.BlockSpec(memory_space=pltpu.VMEM)] * len(after),
         ],
-        out_specs=[vmem] * 5,
-        out_shape=[half] * 4 + [jax.ShapeDtypeStruct((lax.axis_size(CHIPS), *fields.shape), F32)],
+        out_specs=[pl.BlockSpec(memory_space=pltpu.VMEM)] * 2,
+        out_shape=[half] * 2,
         scratch_shapes=[
             pltpu.VMEM((4, 2, rows, rows), F32),
             pltpu.SemaphoreType.DMA((4, 2)),
         ],
         compiler_params=pltpu.CompilerParams(vmem_limit_bytes=VMEM_LIMIT),
-        cost_estimate=pl.CostEstimate(flops=0, transcendentals=0, bytes_accessed=8 * rows * width),
-        name="prepare",
+        cost_estimate=pl.CostEstimate(flops=0, transcendentals=0, bytes_accessed=4 * rows * width),
+        name="prepare_other" if other else "prepare_own",
     )(
-        fields,
         pltpu.with_memory_space_constraint(real_rows, pltpu.HBM),
         pltpu.with_memory_space_constraint(imag_rows, pltpu.HBM),
+        *after,
     )
 
 
-def product(blocks_ref, hi_ref, lo_ref, xs):
+def relative(at):
+    step, across = divmod(at, 2)
+    count = lax.axis_size("y")
+    y, zl = lax.axis_index("y"), lax.axis_index("zl")
+    return 2 * ((y + count - step) % count) + (1 - zl if across else zl)
+
+
+def product(turn, blocks_ref, hi_ref, lo_ref, xs):
     count, _, sources, rows = blocks_ref.shape
     for at in range(count):
         hi, lo = split(blocks_ref[at].reshape(2 * sources, rows))
-        xs[: 2 * sources, pl.ds(at * rows, rows)] = hi
-        xs[2 * sources :, pl.ds(at * rows, rows)] = lo
+        column = at * rows if turn else pl.multiple_of(relative(at) * rows, 128)
+        xs[: 2 * sources, pl.ds(column, rows)] = hi
+        xs[2 * sources :, pl.ds(column, rows)] = lo
     dims = (((1,), (0,)), ((), ()))
     both = lax.dot_general(xs[...], hi_ref[...], dims, preferred_element_type=F32)
     rest = lax.dot_general(xs[: 2 * sources, :], lo_ref[...], dims, preferred_element_type=F32)
@@ -103,7 +104,7 @@
 def first_half_body(turn, blocks_ref, hi_ref, lo_ref, out_ref, xs):
     @pl.when(diagonal() == turn)
     def _():
-        out_ref[...] = product(blocks_ref, hi_ref, lo_ref, xs)
+        out_ref[...] = product(turn, blocks_ref, hi_ref, lo_ref, xs)
 
 
 def second_half_body(turn, blocks_ref, hi_ref, lo_ref, first_ref, before_ref, out_ref, xs):
@@ -111,7 +112,7 @@
 
     @pl.when(diagonal() == turn)
     def _():
-        total = first_ref[...] + product(blocks_ref, hi_ref, lo_ref, xs)
+        total = first_ref[...] + product(turn, blocks_ref, hi_ref, lo_ref, xs)
         with_real = total[:, :rows]
         with_imag = total[:, rows:]
         out_ref[0] = with_real[:sources] - with_imag[sources:]
@@ -172,6 +173,41 @@
     return lax.all_to_all(copies, CHIPS, split_axis=0, concat_axis=0, tiled=True)
 
 
+def stack_body(count, *refs):
+    out_ref = refs[-1]
+    at = 0
+    for ref in refs[:count]:
+        for block in range(ref.shape[0]):
+            out_ref[at] = ref[block]
+            at += 1
+
+
+def stack(blocks, after):
+    total = sum(block.shape[0] for block in blocks)
+    vmem = pl.BlockSpec(memory_space=pltpu.VMEM)
+    return pl.pallas_call(
+        functools.partial(stack_body, len(blocks)),
+        in_specs=[vmem] * (len(blocks) + 1),
+        out_specs=vmem,
+        out_shape=jax.ShapeDtypeStruct((total, *blocks[0].shape[1:]), F32),
+        compiler_params=pltpu.CompilerParams(vmem_limit_bytes=2 * 1024 * 1024),
+        name="stack",
+    )(*blocks, after)
+
+
+def start(fields, real_rows, imag_rows):
+    count = lax.axis_size("y")
+    across = lax.ppermute(fields, "zl", ring("zl"))
+    own_weights = prepare(False, real_rows, imag_rows)
+    pair = stack([fields[None], across[None]], own_weights[0])
+    others = [
+        lax.ppermute(pair, "y", [(i, (i + step) % count) for i in range(count)])
+        for step in range(1, count)
+    ]
+    other_weights = prepare(True, real_rows, imag_rows, pair)
+    return stack([pair, *others], other_weights[0]), *own_weights, *other_weights
+
+
 def hand_over(traces, turn, right, up):
     columns, rows = lax.axis_size("sx"), lax.axis_size("sy")
     pairs = []
@@ -188,15 +224,13 @@
     right_coef = coef_right[0, 0]
     upper_coef = coef_upper[0, 0]
     rounds = lax.axis_size("sx") + lax.axis_size("sy") - 1
-    *weights, copies = prepare(fields, op_real[0, 0], op_imag[0, 0])
-    own_hi, own_lo, other_hi, other_lo = weights
+    own, own_hi, own_lo, other_hi, other_lo = start(fields, op_real[0, 0], op_imag[0, 0])
     traces = fields
     for turn in range(rounds):
         if turn:
             from_left = hand_over(traces, turn - 1, 1, 0)
             from_below = hand_over(traces, turn - 1, 0, 1)
-            copies = combine(fields, right_coef, upper_coef, from_left, from_below)
-        own = gather_chips(copies)
+            own = gather_chips(combine(fields, right_coef, upper_coef, from_left, from_below))
         other = lax.ppermute(own, "core", ring("core"))
         first = half_call(
             first_half_body, turn, (2 * count, 2 * rows), own, own_hi, own_lo, name="first_half"

time: 106 us -> 99.6 us (0.940)
  blocking collectives: 51.6 us -> 40 us
  starting transfers between devices: 17.1 us -> 22.4 us
    all_to_all x5 -> x4, blocking collectives: 51.6 us -> 40 us  [gather_chips(): lax.all_to_all(copies, CHIPS, split_axis=0, concat_axis=0, tiled=True)]
    ppermute x0 -> x4, starting transfers between devices: none -> 6.4 us  [the longest x3 5.05 us: start(): lax.ppermute(pair, 'y', [(i, (i + step) % count) for i in range(count)])]
    pallas_call x1 -> x4, Pallas kernels: 8.03 us -> 9.06 us  [the longest x2 9.03 us: prepare(): pl.pallas_call(functools.partial(prepare_body, other), in_specs=[pl.Block...]
  transfers between devices with their start and end apart: 13 -> 17, of which waited for: 5 -> 5; matrix products, arithmetic and copies ran while one was open for 0% -> 0% of each run, Pallas kernels for 2% -> 11%
where the time goes in v2:
time: 99.6 us; the launch traced here: 99.2 us
  blocking collectives  40 us (40%)
  waiting for transfers between devices  23.3 us (23%)
  starting transfers between devices  22.4 us (22%)
  Pallas kernels  13.2 us (13%)
    all_to_all x4, blocking collectives, gather_chips(): lax.all_to_all(copies, CHIPS, split_axis=0, concat_axis=0, tiled=True)  40 us
    ppermute x8, waiting for transfers between devices, hand_over(): return lax.ppermute(traces, ('sx', 'sy'), pairs)  17.9 us
    ppermute x5, starting transfers between devices, shards(): other = lax.ppermute(own, 'core', ring('core'))  9.39 us
    pallas_call x2, Pallas kernels, prepare(): pl.pallas_call(functools.partial(prepare_body, other), in_specs=[pl.Block...  9.03 us
    ppermute x8, starting transfers between devices, hand_over(): return lax.ppermute(traces, ('sx', 'sy'), pairs)  6.66 us
    ppermute x5, waiting for transfers between devices, shards(): other = lax.ppermute(own, 'core', ring('core'))  5.4 us
    ppermute x3, starting transfers between devices, start(): lax.ppermute(pair, 'y', [(i, (i + step) % count) for i in range(count)])  5.05 us
    pallas_call x10, Pallas kernels, half_call(): pl.pallas_call(functools.partial(body, turn), in_specs=[vmem] * (1 + len(...  4.05 us
  transfers between devices with their start and end apart: 17, of which 5 were waited for; matrix products, arithmetic and copies ran while one was open for 0% of the time, Pallas kernels for 11%

profile of v2, /device:TPU:71, one launch (start us, length us, event | category | flops | bytes accessed | tf_op | source)
XLA Modules:
  0.0 99.2 jit_solution(9272423735123700141)
XLA Ops:
  0.0 1.3 %collective-permute-start = (f32[2,16,384]{2,1,0:T(8,128)}, f32[2,16,384]{2,1,0:T(8,128)S(1)}, u32[]{:S(2)}, u32[]{:S(2)}) collective-permute-start(f32[2,16,384]{2,1,0:T(8,128)} %bitcast.8), channel_id=1, source_target_pairs={{0,2},{2,0},{1,3},{3,1},{4,6},{6,4},{5,7},{7,5},{8,10},{10,8},{9,1... | collective-permute-start | bytes 147464 | tf_op jit(solution)/shard_map/ppermute | solution.py:200
  1.3 0.0 copy-start
  1.3 4.5 %prepare_own.1 = (bf16[3072,768]{1,0:T(8,128)(2,1)S(1)}, bf16[3072,768]{1,0:T(8,128)(2,1)S(1)}) custom-call(f32[384,6144]{1,0:T(8,128)} %bitcast.24, f32[384,6144]{1,0:T(8,128)} %bitcast.26), custom_call_target="tpu_custom_call" | custom-call | bytes 9437184 | tf_op jit(solution)/shard_map/prepare_own/pallas_call | solution.py:57
  5.9 0.0 collective-permute-done
  5.9 0.0 copy-done
  5.9 1.4 %collective-permute-start.1 = (f32[2,2,16,384]{3,2,1,0:T(8,128)S(1)}, f32[2,2,16,384]{3,2,1,0:T(8,128)S(1)}, u32[]{:S(2)}, u32[]{:S(2)}) collective-permute-start(f32[2,2,16,384]{3,2,1,0:T(8,128)S(1)} %stack.2.refs_0_), channel_id=1, source_target_pairs={{0,4},{4,8},{8,12},{12,0},{1,5},{5,9},{9,13},{13,1},{2,6},{6,10},{... | collective-permute-start | bytes 294920 | tf_op jit(solution)/shard_map/ppermute | solution.py:204
  7.3 2.6 %collective-permute-start.2 = (f32[2,2,16,384]{3,2,1,0:T(8,128)S(1)}, f32[2,2,16,384]{3,2,1,0:T(8,128)S(1)}, u32[]{:S(2)}, u32[]{:S(2)}) collective-permute-start(f32[2,2,16,384]{3,2,1,0:T(8,128)S(1)} %stack.2.refs_0_), channel_id=1, source_target_pairs={{0,8},{4,12},{8,0},{12,4},{1,9},{5,13},{9,1},{13,5},{2,10},{6,14},... | collective-permute-start | bytes 294920 | tf_op jit(solution)/shard_map/ppermute | solution.py:204
  9.9 1.1 %collective-permute-start.3 = (f32[2,2,16,384]{3,2,1,0:T(8,128)S(1)}, f32[2,2,16,384]{3,2,1,0:T(8,128)S(1)}, u32[]{:S(2)}, u32[]{:S(2)}) collective-permute-start(f32[2,2,16,384]{3,2,1,0:T(8,128)S(1)} %stack.2.refs_0_), channel_id=1, source_target_pairs={{0,12},{4,0},{8,4},{12,8},{1,13},{5,1},{9,5},{13,9},{2,14},{6,2},{... | collective-permute-start | bytes 294920 | tf_op jit(solution)/shard_map/ppermute | solution.py:204
  11.0 4.5 %prepare_other.1 = (bf16[3072,768]{1,0:T(8,128)(2,1)S(1)}, bf16[3072,768]{1,0:T(8,128)(2,1)S(1)}) custom-call(f32[384,6144]{1,0:T(8,128)} %bitcast.25, f32[384,6144]{1,0:T(8,128)} %bitcast.27, f32[2,2,16,384]{3,2,1,0:T(8,128)S(1)} %stack.2.refs_0_), custom_call_target="tpu_custom_call" | custom-call | bytes 9437184 | tf_op jit(solution)/shard_map/prepare_other/pallas_call | solution.py:57
  15.5 0.0 collective-permute-done.1.refs_1_
  15.5 0.0 collective-permute-done.2.refs_2_
  15.5 0.0 collective-permute-done.3.refs_3_
  15.6 1.9 %collective-permute-start.4 = (f32[8,2,16,384]{3,2,1,0:T(8,128)S(1)}, f32[8,2,16,384]{3,2,1,0:T(8,128)S(1)}, u32[]{:S(2)}, u32[]{:S(2)}) collective-permute-start(f32[8,2,16,384]{3,2,1,0:T(8,128)S(1)} %stack.3.blocks_ref), channel_id=1, source_target_pairs={{0,1},{1,0},{2,3},{3,2},{4,5},{5,4},{6,7},{7,6},{8,9},{9,8},{10,11... | collective-permute-start | bytes 1179656 | tf_op jit(solution)/shard_map/ppermute | solution.py:234
  17.4 1.3 %collective-permute-done.4.blocks_ref = f32[8,2,16,384]{3,2,1,0:T(8,128)S(1)} collective-permute-done((f32[8,2,16,384]{3,2,1,0:T(8,128)S(1)}, f32[8,2,16,384]{3,2,1,0:T(8,128)S(1)}, u32[]{:S(2)}, u32[]{:S(2)}) %collective-permute-start.4) | collective-permute-done | bytes 393248 | tf_op jit(solution)/shard_map/ppermute | solution.py:234
  18.8 0.0 copy-start.1
  18.8 0.0 copy-start.2
  18.8 0.8 collective-permute-start.5
  19.6 0.7 collective-permute-start.6
  20.3 0.0 collective-permute-done.5.left_ref
  20.3 0.0 collective-permute-done.6.below_ref
  20.3 0.0 copy-done.1
  20.3 0.0 copy-done.2
  20.3 10.3 %all_to_all.20.blocks_ref = f32[8,2,16,384]{3,2,1,0:T(8,128)S(1)} all-to-all(f32[8,2,16,384]{3,2,1,0:T(8,128)S(1)} %combine.4), channel_id=1, replica_groups=mesh['sx'=4,'sy'=2,'y'=4,'zl'=2,'core'=2] {'y','zl'}, dimensions={0} | all-to-all | bytes 786432 | tf_op jit(solution)/shard_map/all_to_all | solution.py:173
  30.6 1.6 %collective-permute-start.7 = (f32[8,2,16,384]{3,2,1,0:T(8,128)S(1)}, f32[8,2,16,384]{3,2,1,0:T(8,128)S(1)}, u32[]{:S(2)}, u32[]{:S(2)}) collective-permute-start(f32[8,2,16,384]{3,2,1,0:T(8,128)S(1)} %all_to_all.20.blocks_ref), channel_id=1, source_target_pairs={{0,1},{1,0},{2,3},{3,2},{4,5},{5,4},{6,7},{7,6},{8,9},{9,8},{10,11... | collective-permute-start | bytes 1179656 | tf_op jit(solution)/shard_map/ppermute | solution.py:234
  32.2 1.3 %collective-permute-done.7.blocks_ref = f32[8,2,16,384]{3,2,1,0:T(8,128)S(1)} collective-permute-done((f32[8,2,16,384]{3,2,1,0:T(8,128)S(1)}, f32[8,2,16,384]{3,2,1,0:T(8,128)S(1)}, u32[]{:S(2)}, u32[]{:S(2)}) %collective-permute-start.7) | collective-permute-done | bytes 393248 | tf_op jit(solution)/shard_map/ppermute | solution.py:234
  33.6 0.7 collective-permute-start.8
  34.2 0.7 collective-permute-start.9
  34.9 0.0 collective-permute-done.8.left_ref
  34.9 0.0 collective-permute-done.9.below_ref
  34.9 10.0 %all_to_all.21.blocks_ref = f32[8,2,16,384]{3,2,1,0:T(8,128)S(1)} all-to-all(f32[8,2,16,384]{3,2,1,0:T(8,128)S(1)} %combine.5), channel_id=1, replica_groups=mesh['sx'=4,'sy'=2,'y'=4,'zl'=2,'core'=2] {'y','zl'}, dimensions={0} | all-to-all | bytes 786432 | tf_op jit(solution)/shard_map/all_to_all | solution.py:173
  44.9 1.9 %collective-permute-start.10 = (f32[8,2,16,384]{3,2,1,0:T(8,128)S(1)}, f32[8,2,16,384]{3,2,1,0:T(8,128)S(1)}, u32[]{:S(2)}, u32[]{:S(2)}) collective-permute-start(f32[8,2,16,384]{3,2,1,0:T(8,128)S(1)} %all_to_all.21.blocks_ref), channel_id=1, source_target_pairs={{0,1},{1,0},{2,3},{3,2},{4,5},{5,4},{6,7},{7,6},{8,9},{9,8},{10,11... | collective-permute-start | bytes 1179656 | tf_op jit(solution)/shard_map/ppermute | solution.py:234
  46.8 1.3 %collective-permute-done.10.blocks_ref = f32[8,2,16,384]{3,2,1,0:T(8,128)S(1)} collective-permute-done((f32[8,2,16,384]{3,2,1,0:T(8,128)S(1)}, f32[8,2,16,384]{3,2,1,0:T(8,128)S(1)}, u32[]{:S(2)}, u32[]{:S(2)}) %collective-permute-start.10) | collective-permute-done | bytes 393248 | tf_op jit(solution)/shard_map/ppermute | solution.py:234
  48.2 0.7 collective-permute-start.11
  48.8 0.7 collective-permute-start.12
  49.5 0.0 collective-permute-done.11.left_ref
  49.5 0.0 collective-permute-done.12.below_ref
  49.6 10.0 %all_to_all.22.blocks_ref = f32[8,2,16,384]{3,2,1,0:T(8,128)S(1)} all-to-all(f32[8,2,16,384]{3,2,1,0:T(8,128)S(1)} %combine.6), channel_id=1, replica_groups=mesh['sx'=4,'sy'=2,'y'=4,'zl'=2,'core'=2] {'y','zl'}, dimensions={0} | all-to-all | bytes 786432 | tf_op jit(solution)/shard_map/all_to_all | solution.py:173
  59.6 1.9 %collective-permute-start.13 = (f32[8,2,16,384]{3,2,1,0:T(8,128)S(1)}, f32[8,2,16,384]{3,2,1,0:T(8,128)S(1)}, u32[]{:S(2)}, u32[]{:S(2)}) collective-permute-start(f32[8,2,16,384]{3,2,1,0:T(8,128)S(1)} %all_to_all.22.blocks_ref), channel_id=1, source_target_pairs={{0,1},{1,0},{2,3},{3,2},{4,5},{5,4},{6,7},{7,6},{8,9},{9,8},{10,11... | collective-permute-start | bytes 1179656 | tf_op jit(solution)/shard_map/ppermute | solution.py:234
  61.5 1.3 %collective-permute-done.13.blocks_ref = f32[8,2,16,384]{3,2,1,0:T(8,128)S(1)} collective-permute-done((f32[8,2,16,384]{3,2,1,0:T(8,128)S(1)}, f32[8,2,16,384]{3,2,1,0:T(8,128)S(1)}, u32[]{:S(2)}, u32[]{:S(2)}) %collective-permute-start.13) | collective-permute-done | bytes 393248 | tf_op jit(solution)/shard_map/ppermute | solution.py:234
  62.8 1.3 %collective-permute-start.14 = (f32[2,16,384]{2,1,0:T(8,128)S(1)}, f32[2,16,384]{2,1,0:T(8,128)S(1)}, u32[]{:S(2)}, u32[]{:S(2)}) collective-permute-start(f32[2,16,384]{2,1,0:T(8,128)S(1)} %second_half.8.before_ref), channel_id=1, source_target_pairs={{80,112},{81,113},{82,114},{83,115},{84,116},{85,117},{86,118},{87... | collective-permute-start | bytes 147464 | tf_op jit(solution)/shard_map/ppermute | solution.py:218
  64.1 1.3 %collective-permute-start.15 = (f32[2,16,384]{2,1,0:T(8,128)S(1)}, f32[2,16,384]{2,1,0:T(8,128)S(1)}, u32[]{:S(2)}, u32[]{:S(2)}) collective-permute-start(f32[2,16,384]{2,1,0:T(8,128)S(1)} %second_half.8.before_ref), channel_id=1, source_target_pairs={{96,112},{97,113},{98,114},{99,115},{100,116},{101,117},{102,118},... | collective-permute-start | bytes 147464 | tf_op jit(solution)/shard_map/ppermute | solution.py:218
  65.4 17.9 %collective-permute-done.14.left_ref = f32[2,16,384]{2,1,0:T(8,128)S(1)} collective-permute-done((f32[2,16,384]{2,1,0:T(8,128)S(1)}, f32[2,16,384]{2,1,0:T(8,128)S(1)}, u32[]{:S(2)}, u32[]{:S(2)}) %collective-permute-start.14) | collective-permute-done | bytes 49184 | tf_op jit(solution)/shard_map/ppermute | solution.py:218
  83.3 0.0 collective-permute-done.15.below_ref
  83.3 9.7 %all_to_all.23.blocks_ref = f32[8,2,16,384]{3,2,1,0:T(8,128)S(1)} all-to-all(f32[8,2,16,384]{3,2,1,0:T(8,128)S(1)} %combine.7), channel_id=1, replica_groups=mesh['sx'=4,'sy'=2,'y'=4,'zl'=2,'core'=2] {'y','zl'}, dimensions={0} | all-to-all | bytes 786432 | tf_op jit(solution)/shard_map/all_to_all | solution.py:173
  93.0 2.2 %collective-permute-start.16 = (f32[8,2,16,384]{3,2,1,0:T(8,128)S(1)}, f32[8,2,16,384]{3,2,1,0:T(8,128)S(1)}, u32[]{:S(2)}, u32[]{:S(2)}) collective-permute-start(f32[8,2,16,384]{3,2,1,0:T(8,128)S(1)} %all_to_all.23.blocks_ref), channel_id=1, source_target_pairs={{0,1},{1,0},{2,3},{3,2},{4,5},{5,4},{6,7},{7,6},{8,9},{9,8},{10,11... | collective-permute-start | bytes 1179656 | tf_op jit(solution)/shard_map/ppermute | solution.py:234
  95.2 1.7 %first_half.9.first_ref = f32[32,768]{1,0:T(8,128)S(1)} custom-call(f32[8,2,16,384]{3,2,1,0:T(8,128)S(1)} %all_to_all.23.blocks_ref, bf16[3072,768]{1,0:T(8,128)(2,1)S(1)} %get-tuple-element.9.refs_2_.hi_ref, bf16[3072,768]{1,0:T(8,128)(2,1)S(1)} %get-tuple-element.12.lo_ref), custom_call_target="tpu_custom_call" | custom-call | tf_op jit(solution)/shard_map/first_half/pallas_call | solution.py:129
  96.9 0.0 collective-permute-done.16.blocks_ref
  96.9 2.3 %second_half.9 = f32[2,16,384]{2,1,0:T(8,128)} custom-call(f32[8,2,16,384]{3,2,1,0:T(8,128)S(1)} %collective-permute-done.16.blocks_ref, bf16[3072,768]{1,0:T(8,128)(2,1)S(1)} %get-tuple-element.10.refs_4_.hi_ref, bf16[3072,768]{1,0:T(8,128)(2,1)S(1)} %get-tuple-element.11.lo_ref, f32[32,768]{1,0:T(8,128)S(1)} %first_half.9.first_ref, ...), custom_call_target="tpu_custom_call" | custom-call | tf_op jit(solution)/shard_map/second_half/pallas_call | solution.py:129
  (14 shorter events, 0.2 us)
Async XLA Ops:
  0.0 5.9 %collective-permute-start = (f32[2,16,384]{2,1,0:T(8,128)}, f32[2,16,384]{2,1,0:T(8,128)S(1)}, u32[]{:S(2)}, u32[]{:S(2)}) collective-permute-start(f32[2,16,384]{2,1,0:T(8,128)} %bitcast.8), channel_id=1, source_target_pairs={{0,2},{2,0},{1,3},{3,1},{4,6},{6,4},{5,7},{7,5},{8,10},{10,8},{9,1... | collective-permute-start | bytes 147464 | tf_op jit(solution)/shard_map/ppermute | solution.py:200
  1.3 4.5 %copy-start = (f32[1,1,2,16,384]{4,3,2,1,0:T(8,128)S(1)}, f32[1,1,2,16,384]{4,3,2,1,0:T(8,128)}, u32[]{:S(2)}) copy-start(f32[1,1,2,16,384]{4,3,2,1,0:T(8,128)} %param.9) | copy-start | bytes 147460
  5.9 9.6 %collective-permute-start.1 = (f32[2,2,16,384]{3,2,1,0:T(8,128)S(1)}, f32[2,2,16,384]{3,2,1,0:T(8,128)S(1)}, u32[]{:S(2)}, u32[]{:S(2)}) collective-permute-start(f32[2,2,16,384]{3,2,1,0:T(8,128)S(1)} %stack.2.refs_0_), channel_id=1, source_target_pairs={{0,4},{4,8},{8,12},{12,0},{1,5},{5,9},{9,13},{13,1},{2,6},{6,10},{... | collective-permute-start | bytes 294920 | tf_op jit(solution)/shard_map/ppermute | solution.py:204
  7.3 8.2 %collective-permute-start.2 = (f32[2,2,16,384]{3,2,1,0:T(8,128)S(1)}, f32[2,2,16,384]{3,2,1,0:T(8,128)S(1)}, u32[]{:S(2)}, u32[]{:S(2)}) collective-permute-start(f32[2,2,16,384]{3,2,1,0:T(8,128)S(1)} %stack.2.refs_0_), channel_id=1, source_target_pairs={{0,8},{4,12},{8,0},{12,4},{1,9},{5,13},{9,1},{13,5},{2,10},{6,14},... | collective-permute-start | bytes 294920 | tf_op jit(solution)/shard_map/ppermute | solution.py:204
  9.9 5.6 %collective-permute-start.3 = (f32[2,2,16,384]{3,2,1,0:T(8,128)S(1)}, f32[2,2,16,384]{3,2,1,0:T(8,128)S(1)}, u32[]{:S(2)}, u32[]{:S(2)}) collective-permute-start(f32[2,2,16,384]{3,2,1,0:T(8,128)S(1)} %stack.2.refs_0_), channel_id=1, source_target_pairs={{0,12},{4,0},{8,4},{12,8},{1,13},{5,1},{9,5},{13,9},{2,14},{6,2},{... | collective-permute-start | bytes 294920 | tf_op jit(solution)/shard_map/ppermute | solution.py:204
  15.6 3.2 %collective-permute-start.4 = (f32[8,2,16,384]{3,2,1,0:T(8,128)S(1)}, f32[8,2,16,384]{3,2,1,0:T(8,128)S(1)}, u32[]{:S(2)}, u32[]{:S(2)}) collective-permute-start(f32[8,2,16,384]{3,2,1,0:T(8,128)S(1)} %stack.3.blocks_ref), channel_id=1, source_target_pairs={{0,1},{1,0},{2,3},{3,2},{4,5},{5,4},{6,7},{7,6},{8,9},{9,8},{10,11... | collective-permute-start | bytes 1179656 | tf_op jit(solution)/shard_map/ppermute | solution.py:234
  18.8 1.5 %copy-start.1 = (f32[1,1,2,384]{3,2,1,0:T(2,128)S(1)}, f32[1,1,2,384]{3,2,1,0:T(2,128)}, u32[]{:S(2)}) copy-start(f32[1,1,2,384]{3,2,1,0:T(2,128)} %param.7) | copy-start | bytes 9220
  18.8 1.5 %copy-start.2 = (f32[1,1,2,384]{3,2,1,0:T(2,128)S(1)}, f32[1,1,2,384]{3,2,1,0:T(2,128)}, u32[]{:S(2)}) copy-start(f32[1,1,2,384]{3,2,1,0:T(2,128)} %param.8) | copy-start | bytes 9220
  18.8 1.5 %collective-permute-start.5 = (f32[2,16,384]{2,1,0:T(8,128)S(1)}, f32[2,16,384]{2,1,0:T(8,128)S(1)}, u32[]{:S(2)}, u32[]{:S(2)}) collective-permute-start(f32[2,16,384]{2,1,0:T(8,128)S(1)} %second_half.5.before_ref), channel_id=1, source_target_pairs={{0,32},{1,33},{2,34},{3,35},{4,36},{5,37},{6,38},{7,39},{8,40},{9,... | collective-permute-start | bytes 147464 | tf_op jit(solution)/shard_map/ppermute | solution.py:218
  19.6 0.7 collective-permute-start.6
  30.6 2.9 %collective-permute-start.7 = (f32[8,2,16,384]{3,2,1,0:T(8,128)S(1)}, f32[8,2,16,384]{3,2,1,0:T(8,128)S(1)}, u32[]{:S(2)}, u32[]{:S(2)}) collective-permute-start(f32[8,2,16,384]{3,2,1,0:T(8,128)S(1)} %all_to_all.20.blocks_ref), channel_id=1, source_target_pairs={{0,1},{1,0},{2,3},{3,2},{4,5},{5,4},{6,7},{7,6},{8,9},{9,8},{10,11... | collective-permute-start | bytes 1179656 | tf_op jit(solution)/shard_map/ppermute | solution.py:234
  33.6 1.3 %collective-permute-start.8 = (f32[2,16,384]{2,1,0:T(8,128)S(1)}, f32[2,16,384]{2,1,0:T(8,128)S(1)}, u32[]{:S(2)}, u32[]{:S(2)}) collective-permute-start(f32[2,16,384]{2,1,0:T(8,128)S(1)} %second_half.6.before_ref), channel_id=1, source_target_pairs={{16,48},{32,64},{17,49},{33,65},{18,50},{34,66},{19,51},{35,67},{2... | collective-permute-start | bytes 147464 | tf_op jit(solution)/shard_map/ppermute | solution.py:218
  34.2 0.7 collective-permute-start.9
  44.9 3.2 %collective-permute-start.10 = (f32[8,2,16,384]{3,2,1,0:T(8,128)S(1)}, f32[8,2,16,384]{3,2,1,0:T(8,128)S(1)}, u32[]{:S(2)}, u32[]{:S(2)}) collective-permute-start(f32[8,2,16,384]{3,2,1,0:T(8,128)S(1)} %all_to_all.21.blocks_ref), channel_id=1, source_target_pairs={{0,1},{1,0},{2,3},{3,2},{4,5},{5,4},{6,7},{7,6},{8,9},{9,8},{10,11... | collective-permute-start | bytes 1179656 | tf_op jit(solution)/shard_map/ppermute | solution.py:234
  48.2 1.3 %collective-permute-start.11 = (f32[2,16,384]{2,1,0:T(8,128)S(1)}, f32[2,16,384]{2,1,0:T(8,128)S(1)}, u32[]{:S(2)}, u32[]{:S(2)}) collective-permute-start(f32[2,16,384]{2,1,0:T(8,128)S(1)} %second_half.7.before_ref), channel_id=1, source_target_pairs={{48,80},{64,96},{49,81},{65,97},{50,82},{66,98},{51,83},{67,99},{5... | collective-permute-start | bytes 147464 | tf_op jit(solution)/shard_map/ppermute | solution.py:218
  48.8 0.7 collective-permute-start.12
  59.6 3.2 %collective-permute-start.13 = (f32[8,2,16,384]{3,2,1,0:T(8,128)S(1)}, f32[8,2,16,384]{3,2,1,0:T(8,128)S(1)}, u32[]{:S(2)}, u32[]{:S(2)}) collective-permute-start(f32[8,2,16,384]{3,2,1,0:T(8,128)S(1)} %all_to_all.22.blocks_ref), channel_id=1, source_target_pairs={{0,1},{1,0},{2,3},{3,2},{4,5},{5,4},{6,7},{7,6},{8,9},{9,8},{10,11... | collective-permute-start | bytes 1179656 | tf_op jit(solution)/shard_map/ppermute | solution.py:234
  62.8 20.4 %collective-permute-start.14 = (f32[2,16,384]{2,1,0:T(8,128)S(1)}, f32[2,16,384]{2,1,0:T(8,128)S(1)}, u32[]{:S(2)}, u32[]{:S(2)}) collective-permute-start(f32[2,16,384]{2,1,0:T(8,128)S(1)} %second_half.8.before_ref), channel_id=1, source_target_pairs={{80,112},{81,113},{82,114},{83,115},{84,116},{85,117},{86,118},{87... | collective-permute-start | bytes 147464 | tf_op jit(solution)/shard_map/ppermute | solution.py:218
  64.1 19.2 %collective-permute-start.15 = (f32[2,16,384]{2,1,0:T(8,128)S(1)}, f32[2,16,384]{2,1,0:T(8,128)S(1)}, u32[]{:S(2)}, u32[]{:S(2)}) collective-permute-start(f32[2,16,384]{2,1,0:T(8,128)S(1)} %second_half.8.before_ref), channel_id=1, source_target_pairs={{96,112},{97,113},{98,114},{99,115},{100,116},{101,117},{102,118},... | collective-permute-start | bytes 147464 | tf_op jit(solution)/shard_map/ppermute | solution.py:218
  93.0 3.9 %collective-permute-start.16 = (f32[8,2,16,384]{3,2,1,0:T(8,128)S(1)}, f32[8,2,16,384]{3,2,1,0:T(8,128)S(1)}, u32[]{:S(2)}, u32[]{:S(2)}) collective-permute-start(f32[8,2,16,384]{3,2,1,0:T(8,128)S(1)} %all_to_all.23.blocks_ref), channel_id=1, source_target_pairs={{0,1},{1,0},{2,3},{3,2},{4,5},{5,4},{6,7},{7,6},{8,9},{9,8},{10,11... | collective-permute-start | bytes 1179656 | tf_op jit(solution)/shard_map/ppermute | solution.py:234

commit v3 on v2

--- a/solution.py
+++ b/solution.py
@@ -11,6 +11,7 @@
 BF = jnp.bfloat16
 F32 = jnp.float32
 CHIPS = ("y", "zl")
+CHUNK = 256
 VMEM_LIMIT = 12 * 1024 * 1024
 
 
@@ -64,8 +65,8 @@
         out_specs=[pl.BlockSpec(memory_space=pltpu.VMEM)] * 2,
         out_shape=[half] * 2,
         scratch_shapes=[
-            pltpu.VMEM((4, 2, rows, rows), F32),
-            pltpu.SemaphoreType.DMA((4, 2)),
+            pltpu.VMEM((8, 2, rows, rows), F32),
+            pltpu.SemaphoreType.DMA((8, 2)),
         ],
         compiler_params=pltpu.CompilerParams(vmem_limit_bytes=VMEM_LIMIT),
         cost_estimate=pl.CostEstimate(flops=0, transcendentals=0, bytes_accessed=4 * rows * width),
@@ -92,9 +93,16 @@
         xs[: 2 * sources, pl.ds(column, rows)] = hi
         xs[2 * sources :, pl.ds(column, rows)] = lo
     dims = (((1,), (0,)), ((), ()))
-    both = lax.dot_general(xs[...], hi_ref[...], dims, preferred_element_type=F32)
-    rest = lax.dot_general(xs[: 2 * sources, :], lo_ref[...], dims, preferred_element_type=F32)
-    return both[: 2 * sources] + both[2 * sources :] + rest
+    total = None
+    for at in range(0, count * rows, CHUNK):
+        part = pl.ds(at, CHUNK)
+        both = lax.dot_general(xs[:, part], hi_ref[part, :], dims, preferred_element_type=F32)
+        rest = lax.dot_general(
+            xs[: 2 * sources, part], lo_ref[part, :], dims, preferred_element_type=F32
+        )
+        both = both[: 2 * sources] + both[2 * sources :] + rest
+        total = both if total is None else total + both
+    return total
 
 
 def diagonal():
@@ -144,8 +152,8 @@
 
 
 def combine_body(fields_ref, right_ref, upper_ref, left_ref, below_ref, copies_ref):
-    by_left = scaled(right_ref[...], left_ref[...])
-    by_below = scaled(upper_ref[...], below_ref[...])
+    by_left = scaled(jnp.where(lax.axis_index("sx") > 0, right_ref[...], 0.0), left_ref[...])
+    by_below = scaled(jnp.where(lax.axis_index("sy") > 0, upper_ref[...], 0.0), below_ref[...])
     for part in range(2):
         incoming = fields_ref[part] + by_left[part] + by_below[part]
         for at in range(copies_ref.shape[0]):
@@ -209,13 +217,27 @@
 
 
 def hand_over(traces, turn, right, up):
-    columns, rows = lax.axis_size("sx"), lax.axis_size("sy")
+    columns, rows, cores = (lax.axis_size(name) for name in ("sx", "sy", "core"))
+    windows = [(column, row) for column in range(columns) for row in range(rows)]
+    target = {}
+    for column, row in windows:
+        there = (column + right, row + up)
+        if column + row == turn and there in windows:
+            target[column, row] = there
+            if up:
+                target[there] = (column, row)
+
+    def index(window, core):
+        return (window[0] * rows + window[1]) * cores + core
+
     pairs = []
-    for column in range(columns):
-        for row in range(rows):
-            if column + row == turn and column + right < columns and row + up < rows:
-                pairs.append((column * rows + row, (column + right) * rows + row + up))
-    return lax.ppermute(traces, ("sx", "sy"), pairs)
+    for window in windows:
+        for core in range(cores):
+            if window in target:
+                pairs.append((index(window, core), index(target[window], core)))
+            elif up:
+                pairs.append((index(window, core), index(window, (core + 1) % cores)))
+    return lax.ppermute(traces, ("sx", "sy", "core"), pairs)
 
 
 def shards(op_real, op_imag, coef_right, coef_upper, sources):

time: 99.6 us -> 96.8 us (0.972)
  waiting for transfers between devices: 23.3 us -> 11.6 us
  starting transfers between devices: 22.4 us -> 32.3 us
    ppermute x8, waiting for transfers between devices: 17.9 us -> 6.16 us  [hand_over(): return lax.ppermute(traces, ('sx', 'sy', 'core'), pairs)]
    ppermute x8, starting transfers between devices: 6.66 us -> 16.3 us  [hand_over(): return lax.ppermute(traces, ('sx', 'sy', 'core'), pairs)]
  transfers between devices with their start and end apart: 17 -> 17, of which waited for: 5 -> 8; matrix products, arithmetic and copies ran while one was open for 0% -> 0% of each run, Pallas kernels for 11% -> 11%
where the time goes in v3:
time: 96.8 us; the launch traced here: 96.5 us
  blocking collectives  39.8 us (41%)
  starting transfers between devices  32.3 us (33%)
  Pallas kernels  12.7 us (13%)
  waiting for transfers between devices  11.6 us (12%)
    all_to_all x4, blocking collectives, gather_chips(): lax.all_to_all(copies, CHIPS, split_axis=0, concat_axis=0, tiled=True)  39.8 us
    ppermute x8, starting transfers between devices, hand_over(): return lax.ppermute(traces, ('sx', 'sy', 'core'), pairs)  16.3 us
    ppermute x5, starting transfers between devices, shards(): other = lax.ppermute(own, 'core', ring('core'))  9.56 us
    pallas_call x2, Pallas kernels, prepare(): pl.pallas_call(functools.partial(prepare_body, other), in_specs=[pl.Block...  8.55 us
    ppermute x8, waiting for transfers between devices, hand_over(): return lax.ppermute(traces, ('sx', 'sy', 'core'), pairs)  6.16 us
    ppermute x5, waiting for transfers between devices, shards(): other = lax.ppermute(own, 'core', ring('core'))  5.4 us
    ppermute x3, starting transfers between devices, start(): lax.ppermute(pair, 'y', [(i, (i + step) % count) for i in range(count)])  5.05 us
    pallas_call x10, Pallas kernels, half_call(): pl.pallas_call(functools.partial(body, turn), in_specs=[vmem] * (1 + len(...  3.94 us
  transfers between devices with their start and end apart: 17, of which 8 were waited for; matrix products, arithmetic and copies ran while one was open for 0% of the time, Pallas kernels for 11%

profile of v3, /device:TPU:71, one launch (start us, length us, event | category | flops | bytes accessed | tf_op | source)
XLA Modules:
  0.0 96.5 jit_solution(6498215067284427236)
XLA Ops:
  0.0 1.3 %collective-permute-start = (f32[2,16,384]{2,1,0:T(8,128)}, f32[2,16,384]{2,1,0:T(8,128)S(1)}, u32[]{:S(2)}, u32[]{:S(2)}) collective-permute-start(f32[2,16,384]{2,1,0:T(8,128)} %bitcast.8), channel_id=1, source_target_pairs={{0,2},{2,0},{1,3},{3,1},{4,6},{6,4},{5,7},{7,5},{8,10},{10,8},{9,1... | collective-permute-start | bytes 147464 | tf_op jit(solution)/shard_map/ppermute | solution.py:208
  1.3 0.0 copy-start
  1.3 4.3 %prepare_own.1 = (bf16[3072,768]{1,0:T(8,128)(2,1)S(1)}, bf16[3072,768]{1,0:T(8,128)(2,1)S(1)}) custom-call(f32[384,6144]{1,0:T(8,128)} %bitcast.24, f32[384,6144]{1,0:T(8,128)} %bitcast.26), custom_call_target="tpu_custom_call" | custom-call | bytes 9437184 | tf_op jit(solution)/shard_map/prepare_own/pallas_call | solution.py:58
  5.6 0.0 collective-permute-done
  5.6 0.0 copy-done
  5.7 1.4 %collective-permute-start.1 = (f32[2,2,16,384]{3,2,1,0:T(8,128)S(1)}, f32[2,2,16,384]{3,2,1,0:T(8,128)S(1)}, u32[]{:S(2)}, u32[]{:S(2)}) collective-permute-start(f32[2,2,16,384]{3,2,1,0:T(8,128)S(1)} %stack.2.refs_0_), channel_id=1, source_target_pairs={{0,4},{4,8},{8,12},{12,0},{1,5},{5,9},{9,13},{13,1},{2,6},{6,10},{... | collective-permute-start | bytes 294920 | tf_op jit(solution)/shard_map/ppermute | solution.py:212
  7.0 2.6 %collective-permute-start.2 = (f32[2,2,16,384]{3,2,1,0:T(8,128)S(1)}, f32[2,2,16,384]{3,2,1,0:T(8,128)S(1)}, u32[]{:S(2)}, u32[]{:S(2)}) collective-permute-start(f32[2,2,16,384]{3,2,1,0:T(8,128)S(1)} %stack.2.refs_0_), channel_id=1, source_target_pairs={{0,8},{4,12},{8,0},{12,4},{1,9},{5,13},{9,1},{13,5},{2,10},{6,14},... | collective-permute-start | bytes 294920 | tf_op jit(solution)/shard_map/ppermute | solution.py:212
  9.7 1.1 %collective-permute-start.3 = (f32[2,2,16,384]{3,2,1,0:T(8,128)S(1)}, f32[2,2,16,384]{3,2,1,0:T(8,128)S(1)}, u32[]{:S(2)}, u32[]{:S(2)}) collective-permute-start(f32[2,2,16,384]{3,2,1,0:T(8,128)S(1)} %stack.2.refs_0_), channel_id=1, source_target_pairs={{0,12},{4,0},{8,4},{12,8},{1,13},{5,1},{9,5},{13,9},{2,14},{6,2},{... | collective-permute-start | bytes 294920 | tf_op jit(solution)/shard_map/ppermute | solution.py:212
  10.7 4.3 %prepare_other.1 = (bf16[3072,768]{1,0:T(8,128)(2,1)S(1)}, bf16[3072,768]{1,0:T(8,128)(2,1)S(1)}) custom-call(f32[384,6144]{1,0:T(8,128)} %bitcast.25, f32[384,6144]{1,0:T(8,128)} %bitcast.27, f32[2,2,16,384]{3,2,1,0:T(8,128)S(1)} %stack.2.refs_0_), custom_call_target="tpu_custom_call" | custom-call | bytes 9437184 | tf_op jit(solution)/shard_map/prepare_other/pallas_call | solution.py:58
  15.0 0.0 collective-permute-done.1.refs_1_
  15.0 0.0 collective-permute-done.2.refs_2_
  15.0 0.0 collective-permute-done.3.refs_3_
  15.1 1.9 %collective-permute-start.4 = (f32[8,2,16,384]{3,2,1,0:T(8,128)S(1)}, f32[8,2,16,384]{3,2,1,0:T(8,128)S(1)}, u32[]{:S(2)}, u32[]{:S(2)}) collective-permute-start(f32[8,2,16,384]{3,2,1,0:T(8,128)S(1)} %stack.3.blocks_ref), channel_id=1, source_target_pairs={{0,1},{1,0},{2,3},{3,2},{4,5},{5,4},{6,7},{7,6},{8,9},{9,8},{10,11... | collective-permute-start | bytes 1179656 | tf_op jit(solution)/shard_map/ppermute | solution.py:256
  17.0 1.3 %collective-permute-done.4.blocks_ref = f32[8,2,16,384]{3,2,1,0:T(8,128)S(1)} collective-permute-done((f32[8,2,16,384]{3,2,1,0:T(8,128)S(1)}, f32[8,2,16,384]{3,2,1,0:T(8,128)S(1)}, u32[]{:S(2)}, u32[]{:S(2)}) %collective-permute-start.4) | collective-permute-done | bytes 393248 | tf_op jit(solution)/shard_map/ppermute | solution.py:256
  18.3 0.0 copy-start.1
  18.3 0.0 copy-start.2
  18.3 0.8 collective-permute-start.5
  19.1 0.5 collective-permute-start.6
  19.6 0.0 collective-permute-done.5.left_ref
  19.6 0.9 collective-permute-done.6.below_ref
  20.5 0.0 copy-done.1
  20.5 0.0 copy-done.2
  20.5 10.1 %all_to_all.20.blocks_ref = f32[8,2,16,384]{3,2,1,0:T(8,128)S(1)} all-to-all(f32[8,2,16,384]{3,2,1,0:T(8,128)S(1)} %combine.4), channel_id=1, replica_groups=mesh['sx'=4,'sy'=2,'y'=4,'zl'=2,'core'=2] {'y','zl'}, dimensions={0} | all-to-all | bytes 786432 | tf_op jit(solution)/shard_map/all_to_all | solution.py:181
  30.6 1.7 %collective-permute-start.7 = (f32[8,2,16,384]{3,2,1,0:T(8,128)S(1)}, f32[8,2,16,384]{3,2,1,0:T(8,128)S(1)}, u32[]{:S(2)}, u32[]{:S(2)}) collective-permute-start(f32[8,2,16,384]{3,2,1,0:T(8,128)S(1)} %all_to_all.20.blocks_ref), channel_id=1, source_target_pairs={{0,1},{1,0},{2,3},{3,2},{4,5},{5,4},{6,7},{7,6},{8,9},{9,8},{10,11... | collective-permute-start | bytes 1179656 | tf_op jit(solution)/shard_map/ppermute | solution.py:256
  32.4 1.3 %collective-permute-done.7.blocks_ref = f32[8,2,16,384]{3,2,1,0:T(8,128)S(1)} collective-permute-done((f32[8,2,16,384]{3,2,1,0:T(8,128)S(1)}, f32[8,2,16,384]{3,2,1,0:T(8,128)S(1)}, u32[]{:S(2)}, u32[]{:S(2)}) %collective-permute-start.7) | collective-permute-done | bytes 393248 | tf_op jit(solution)/shard_map/ppermute | solution.py:256
  33.7 0.7 collective-permute-start.8
  34.4 0.5 collective-permute-start.9
  34.8 0.0 collective-permute-done.8.left_ref
  34.8 0.9 collective-permute-done.9.below_ref
  35.8 10.0 %all_to_all.21.blocks_ref = f32[8,2,16,384]{3,2,1,0:T(8,128)S(1)} all-to-all(f32[8,2,16,384]{3,2,1,0:T(8,128)S(1)} %combine.5), channel_id=1, replica_groups=mesh['sx'=4,'sy'=2,'y'=4,'zl'=2,'core'=2] {'y','zl'}, dimensions={0} | all-to-all | bytes 786432 | tf_op jit(solution)/shard_map/all_to_all | solution.py:181
  45.8 1.8 %collective-permute-start.10 = (f32[8,2,16,384]{3,2,1,0:T(8,128)S(1)}, f32[8,2,16,384]{3,2,1,0:T(8,128)S(1)}, u32[]{:S(2)}, u32[]{:S(2)}) collective-permute-start(f32[8,2,16,384]{3,2,1,0:T(8,128)S(1)} %all_to_all.21.blocks_ref), channel_id=1, source_target_pairs={{0,1},{1,0},{2,3},{3,2},{4,5},{5,4},{6,7},{7,6},{8,9},{9,8},{10,11... | collective-permute-start | bytes 1179656 | tf_op jit(solution)/shard_map/ppermute | solution.py:256
  47.6 1.3 %collective-permute-done.10.blocks_ref = f32[8,2,16,384]{3,2,1,0:T(8,128)S(1)} collective-permute-done((f32[8,2,16,384]{3,2,1,0:T(8,128)S(1)}, f32[8,2,16,384]{3,2,1,0:T(8,128)S(1)}, u32[]{:S(2)}, u32[]{:S(2)}) %collective-permute-start.10) | collective-permute-done | bytes 393248 | tf_op jit(solution)/shard_map/ppermute | solution.py:256
  49.0 0.7 collective-permute-start.11
  49.6 0.5 collective-permute-start.12
  50.1 0.0 collective-permute-done.11.left_ref
  50.1 0.9 collective-permute-done.12.below_ref
  51.0 10.0 %all_to_all.22.blocks_ref = f32[8,2,16,384]{3,2,1,0:T(8,128)S(1)} all-to-all(f32[8,2,16,384]{3,2,1,0:T(8,128)S(1)} %combine.6), channel_id=1, replica_groups=mesh['sx'=4,'sy'=2,'y'=4,'zl'=2,'core'=2] {'y','zl'}, dimensions={0} | all-to-all | bytes 786432 | tf_op jit(solution)/shard_map/all_to_all | solution.py:181
  61.1 1.8 %collective-permute-start.13 = (f32[8,2,16,384]{3,2,1,0:T(8,128)S(1)}, f32[8,2,16,384]{3,2,1,0:T(8,128)S(1)}, u32[]{:S(2)}, u32[]{:S(2)}) collective-permute-start(f32[8,2,16,384]{3,2,1,0:T(8,128)S(1)} %all_to_all.22.blocks_ref), channel_id=1, source_target_pairs={{0,1},{1,0},{2,3},{3,2},{4,5},{5,4},{6,7},{7,6},{8,9},{9,8},{10,11... | collective-permute-start | bytes 1179656 | tf_op jit(solution)/shard_map/ppermute | solution.py:256
  62.9 1.3 %collective-permute-done.13.blocks_ref = f32[8,2,16,384]{3,2,1,0:T(8,128)S(1)} collective-permute-done((f32[8,2,16,384]{3,2,1,0:T(8,128)S(1)}, f32[8,2,16,384]{3,2,1,0:T(8,128)S(1)}, u32[]{:S(2)}, u32[]{:S(2)}) %collective-permute-start.13) | collective-permute-done | bytes 393248 | tf_op jit(solution)/shard_map/ppermute | solution.py:256
  64.3 1.3 %collective-permute-start.14 = (f32[2,16,384]{2,1,0:T(8,128)S(1)}, f32[2,16,384]{2,1,0:T(8,128)S(1)}, u32[]{:S(2)}, u32[]{:S(2)}) collective-permute-start(f32[2,16,384]{2,1,0:T(8,128)S(1)} %second_half.8.before_ref), channel_id=1, source_target_pairs={{80,112},{81,113},{82,114},{83,115},{84,116},{85,117},{86,118},{87... | collective-permute-start | bytes 147464 | tf_op jit(solution)/shard_map/ppermute | solution.py:240
  65.6 11.6 %collective-permute-start.15 = (f32[2,16,384]{2,1,0:T(8,128)S(1)}, f32[2,16,384]{2,1,0:T(8,128)S(1)}, u32[]{:S(2)}, u32[]{:S(2)}) collective-permute-start(f32[2,16,384]{2,1,0:T(8,128)S(1)} %second_half.8.before_ref), channel_id=1, source_target_pairs={{0,1},{1,0},{16,17},{17,16},{32,33},{33,32},{48,49},{49,48},{64,65... | collective-permute-start | bytes 147464 | tf_op jit(solution)/shard_map/ppermute | solution.py:240
  77.1 3.5 %collective-permute-done.14.left_ref = f32[2,16,384]{2,1,0:T(8,128)S(1)} collective-permute-done((f32[2,16,384]{2,1,0:T(8,128)S(1)}, f32[2,16,384]{2,1,0:T(8,128)S(1)}, u32[]{:S(2)}, u32[]{:S(2)}) %collective-permute-start.14) | collective-permute-done | bytes 49184 | tf_op jit(solution)/shard_map/ppermute | solution.py:240
  80.7 0.0 collective-permute-done.15.below_ref
  80.7 9.6 %all_to_all.23.blocks_ref = f32[8,2,16,384]{3,2,1,0:T(8,128)S(1)} all-to-all(f32[8,2,16,384]{3,2,1,0:T(8,128)S(1)} %combine.7), channel_id=1, replica_groups=mesh['sx'=4,'sy'=2,'y'=4,'zl'=2,'core'=2] {'y','zl'}, dimensions={0} | all-to-all | bytes 786432 | tf_op jit(solution)/shard_map/all_to_all | solution.py:181
  90.3 2.3 %collective-permute-start.16 = (f32[8,2,16,384]{3,2,1,0:T(8,128)S(1)}, f32[8,2,16,384]{3,2,1,0:T(8,128)S(1)}, u32[]{:S(2)}, u32[]{:S(2)}) collective-permute-start(f32[8,2,16,384]{3,2,1,0:T(8,128)S(1)} %all_to_all.23.blocks_ref), channel_id=1, source_target_pairs={{0,1},{1,0},{2,3},{3,2},{4,5},{5,4},{6,7},{7,6},{8,9},{9,8},{10,11... | collective-permute-start | bytes 1179656 | tf_op jit(solution)/shard_map/ppermute | solution.py:256
  92.6 1.6 %first_half.9.first_ref = f32[32,768]{1,0:T(8,128)S(1)} custom-call(f32[8,2,16,384]{3,2,1,0:T(8,128)S(1)} %all_to_all.23.blocks_ref, bf16[3072,768]{1,0:T(8,128)(2,1)S(1)} %get-tuple-element.9.refs_2_.hi_ref, bf16[3072,768]{1,0:T(8,128)(2,1)S(1)} %get-tuple-element.12.lo_ref), custom_call_target="tpu_custom_call" | custom-call | tf_op jit(solution)/shard_map/first_half/pallas_call | solution.py:137
  94.2 0.0 collective-permute-done.16.blocks_ref
  94.2 2.3 %second_half.9 = f32[2,16,384]{2,1,0:T(8,128)} custom-call(f32[8,2,16,384]{3,2,1,0:T(8,128)S(1)} %collective-permute-done.16.blocks_ref, bf16[3072,768]{1,0:T(8,128)(2,1)S(1)} %get-tuple-element.10.refs_4_.hi_ref, bf16[3072,768]{1,0:T(8,128)(2,1)S(1)} %get-tuple-element.11.lo_ref, f32[32,768]{1,0:T(8,128)S(1)} %first_half.9.first_ref, ...), custom_call_target="tpu_custom_call" | custom-call | tf_op jit(solution)/shard_map/second_half/pallas_call | solution.py:137
  (14 shorter events, 0.2 us)
Async XLA Ops:
  0.0 5.6 %collective-permute-start = (f32[2,16,384]{2,1,0:T(8,128)}, f32[2,16,384]{2,1,0:T(8,128)S(1)}, u32[]{:S(2)}, u32[]{:S(2)}) collective-permute-start(f32[2,16,384]{2,1,0:T(8,128)} %bitcast.8), channel_id=1, source_target_pairs={{0,2},{2,0},{1,3},{3,1},{4,6},{6,4},{5,7},{7,5},{8,10},{10,8},{9,1... | collective-permute-start | bytes 147464 | tf_op jit(solution)/shard_map/ppermute | solution.py:208
  1.3 4.3 %copy-start = (f32[1,1,2,16,384]{4,3,2,1,0:T(8,128)S(1)}, f32[1,1,2,16,384]{4,3,2,1,0:T(8,128)}, u32[]{:S(2)}) copy-start(f32[1,1,2,16,384]{4,3,2,1,0:T(8,128)} %param.9) | copy-start | bytes 147460
  5.7 9.3 %collective-permute-start.1 = (f32[2,2,16,384]{3,2,1,0:T(8,128)S(1)}, f32[2,2,16,384]{3,2,1,0:T(8,128)S(1)}, u32[]{:S(2)}, u32[]{:S(2)}) collective-permute-start(f32[2,2,16,384]{3,2,1,0:T(8,128)S(1)} %stack.2.refs_0_), channel_id=1, source_target_pairs={{0,4},{4,8},{8,12},{12,0},{1,5},{5,9},{9,13},{13,1},{2,6},{6,10},{... | collective-permute-start | bytes 294920 | tf_op jit(solution)/shard_map/ppermute | solution.py:212
  7.0 8.0 %collective-permute-start.2 = (f32[2,2,16,384]{3,2,1,0:T(8,128)S(1)}, f32[2,2,16,384]{3,2,1,0:T(8,128)S(1)}, u32[]{:S(2)}, u32[]{:S(2)}) collective-permute-start(f32[2,2,16,384]{3,2,1,0:T(8,128)S(1)} %stack.2.refs_0_), channel_id=1, source_target_pairs={{0,8},{4,12},{8,0},{12,4},{1,9},{5,13},{9,1},{13,5},{2,10},{6,14},... | collective-permute-start | bytes 294920 | tf_op jit(solution)/shard_map/ppermute | solution.py:212
  9.7 5.4 %collective-permute-start.3 = (f32[2,2,16,384]{3,2,1,0:T(8,128)S(1)}, f32[2,2,16,384]{3,2,1,0:T(8,128)S(1)}, u32[]{:S(2)}, u32[]{:S(2)}) collective-permute-start(f32[2,2,16,384]{3,2,1,0:T(8,128)S(1)} %stack.2.refs_0_), channel_id=1, source_target_pairs={{0,12},{4,0},{8,4},{12,8},{1,13},{5,1},{9,5},{13,9},{2,14},{6,2},{... | collective-permute-start | bytes 294920 | tf_op jit(solution)/shard_map/ppermute | solution.py:212
  15.1 3.2 %collective-permute-start.4 = (f32[8,2,16,384]{3,2,1,0:T(8,128)S(1)}, f32[8,2,16,384]{3,2,1,0:T(8,128)S(1)}, u32[]{:S(2)}, u32[]{:S(2)}) collective-permute-start(f32[8,2,16,384]{3,2,1,0:T(8,128)S(1)} %stack.3.blocks_ref), channel_id=1, source_target_pairs={{0,1},{1,0},{2,3},{3,2},{4,5},{5,4},{6,7},{7,6},{8,9},{9,8},{10,11... | collective-permute-start | bytes 1179656 | tf_op jit(solution)/shard_map/ppermute | solution.py:256
  18.3 2.2 %copy-start.1 = (f32[1,1,2,384]{3,2,1,0:T(2,128)S(1)}, f32[1,1,2,384]{3,2,1,0:T(2,128)}, u32[]{:S(2)}) copy-start(f32[1,1,2,384]{3,2,1,0:T(2,128)} %param.7) | copy-start | bytes 9220
  18.3 2.2 %copy-start.2 = (f32[1,1,2,384]{3,2,1,0:T(2,128)S(1)}, f32[1,1,2,384]{3,2,1,0:T(2,128)}, u32[]{:S(2)}) copy-start(f32[1,1,2,384]{3,2,1,0:T(2,128)} %param.8) | copy-start | bytes 9220
  18.3 1.3 %collective-permute-start.5 = (f32[2,16,384]{2,1,0:T(8,128)S(1)}, f32[2,16,384]{2,1,0:T(8,128)S(1)}, u32[]{:S(2)}, u32[]{:S(2)}) collective-permute-start(f32[2,16,384]{2,1,0:T(8,128)S(1)} %second_half.5.before_ref), channel_id=1, source_target_pairs={{0,32},{1,33},{2,34},{3,35},{4,36},{5,37},{6,38},{7,39},{8,40},{9,... | collective-permute-start | bytes 147464 | tf_op jit(solution)/shard_map/ppermute | solution.py:240
  19.1 1.3 %collective-permute-start.6 = (f32[2,16,384]{2,1,0:T(8,128)S(1)}, f32[2,16,384]{2,1,0:T(8,128)S(1)}, u32[]{:S(2)}, u32[]{:S(2)}) collective-permute-start(f32[2,16,384]{2,1,0:T(8,128)S(1)} %second_half.5.before_ref), channel_id=1, source_target_pairs={{0,16},{1,17},{16,0},{17,1},{32,33},{33,32},{48,49},{49,48},{64,65... | collective-permute-start | bytes 147464 | tf_op jit(solution)/shard_map/ppermute | solution.py:240
  30.6 3.1 %collective-permute-start.7 = (f32[8,2,16,384]{3,2,1,0:T(8,128)S(1)}, f32[8,2,16,384]{3,2,1,0:T(8,128)S(1)}, u32[]{:S(2)}, u32[]{:S(2)}) collective-permute-start(f32[8,2,16,384]{3,2,1,0:T(8,128)S(1)} %all_to_all.20.blocks_ref), channel_id=1, source_target_pairs={{0,1},{1,0},{2,3},{3,2},{4,5},{5,4},{6,7},{7,6},{8,9},{9,8},{10,11... | collective-permute-start | bytes 1179656 | tf_op jit(solution)/shard_map/ppermute | solution.py:256
  33.7 1.1 %collective-permute-start.8 = (f32[2,16,384]{2,1,0:T(8,128)S(1)}, f32[2,16,384]{2,1,0:T(8,128)S(1)}, u32[]{:S(2)}, u32[]{:S(2)}) collective-permute-start(f32[2,16,384]{2,1,0:T(8,128)S(1)} %second_half.6.before_ref), channel_id=1, source_target_pairs={{16,48},{17,49},{32,64},{33,65},{18,50},{19,51},{34,66},{35,67},{2... | collective-permute-start | bytes 147464 | tf_op jit(solution)/shard_map/ppermute | solution.py:240
  34.4 1.3 %collective-permute-start.9 = (f32[2,16,384]{2,1,0:T(8,128)S(1)}, f32[2,16,384]{2,1,0:T(8,128)S(1)}, u32[]{:S(2)}, u32[]{:S(2)}) collective-permute-start(f32[2,16,384]{2,1,0:T(8,128)S(1)} %second_half.6.before_ref), channel_id=1, source_target_pairs={{0,1},{1,0},{16,17},{17,16},{32,48},{33,49},{48,32},{49,33},{64,65... | collective-permute-start | bytes 147464 | tf_op jit(solution)/shard_map/ppermute | solution.py:240
  45.8 3.2 %collective-permute-start.10 = (f32[8,2,16,384]{3,2,1,0:T(8,128)S(1)}, f32[8,2,16,384]{3,2,1,0:T(8,128)S(1)}, u32[]{:S(2)}, u32[]{:S(2)}) collective-permute-start(f32[8,2,16,384]{3,2,1,0:T(8,128)S(1)} %all_to_all.21.blocks_ref), channel_id=1, source_target_pairs={{0,1},{1,0},{2,3},{3,2},{4,5},{5,4},{6,7},{7,6},{8,9},{9,8},{10,11... | collective-permute-start | bytes 1179656 | tf_op jit(solution)/shard_map/ppermute | solution.py:256
  49.0 1.1 %collective-permute-start.11 = (f32[2,16,384]{2,1,0:T(8,128)S(1)}, f32[2,16,384]{2,1,0:T(8,128)S(1)}, u32[]{:S(2)}, u32[]{:S(2)}) collective-permute-start(f32[2,16,384]{2,1,0:T(8,128)S(1)} %second_half.7.before_ref), channel_id=1, source_target_pairs={{48,80},{49,81},{64,96},{65,97},{50,82},{51,83},{66,98},{67,99},{5... | collective-permute-start | bytes 147464 | tf_op jit(solution)/shard_map/ppermute | solution.py:240
  49.6 1.3 %collective-permute-start.12 = (f32[2,16,384]{2,1,0:T(8,128)S(1)}, f32[2,16,384]{2,1,0:T(8,128)S(1)}, u32[]{:S(2)}, u32[]{:S(2)}) collective-permute-start(f32[2,16,384]{2,1,0:T(8,128)S(1)} %second_half.7.before_ref), channel_id=1, source_target_pairs={{0,1},{1,0},{16,17},{17,16},{32,33},{33,32},{48,49},{49,48},{64,80... | collective-permute-start | bytes 147464 | tf_op jit(solution)/shard_map/ppermute | solution.py:240
  61.1 3.2 %collective-permute-start.13 = (f32[8,2,16,384]{3,2,1,0:T(8,128)S(1)}, f32[8,2,16,384]{3,2,1,0:T(8,128)S(1)}, u32[]{:S(2)}, u32[]{:S(2)}) collective-permute-start(f32[8,2,16,384]{3,2,1,0:T(8,128)S(1)} %all_to_all.22.blocks_ref), channel_id=1, source_target_pairs={{0,1},{1,0},{2,3},{3,2},{4,5},{5,4},{6,7},{7,6},{8,9},{9,8},{10,11... | collective-permute-start | bytes 1179656 | tf_op jit(solution)/shard_map/ppermute | solution.py:256
  64.3 16.4 %collective-permute-start.14 = (f32[2,16,384]{2,1,0:T(8,128)S(1)}, f32[2,16,384]{2,1,0:T(8,128)S(1)}, u32[]{:S(2)}, u32[]{:S(2)}) collective-permute-start(f32[2,16,384]{2,1,0:T(8,128)S(1)} %second_half.8.before_ref), channel_id=1, source_target_pairs={{80,112},{81,113},{82,114},{83,115},{84,116},{85,117},{86,118},{87... | collective-permute-start | bytes 147464 | tf_op jit(solution)/shard_map/ppermute | solution.py:240
  65.6 15.1 %collective-permute-start.15 = (f32[2,16,384]{2,1,0:T(8,128)S(1)}, f32[2,16,384]{2,1,0:T(8,128)S(1)}, u32[]{:S(2)}, u32[]{:S(2)}) collective-permute-start(f32[2,16,384]{2,1,0:T(8,128)S(1)} %second_half.8.before_ref), channel_id=1, source_target_pairs={{0,1},{1,0},{16,17},{17,16},{32,33},{33,32},{48,49},{49,48},{64,65... | collective-permute-start | bytes 147464 | tf_op jit(solution)/shard_map/ppermute | solution.py:240
  90.3 3.9 %collective-permute-start.16 = (f32[8,2,16,384]{3,2,1,0:T(8,128)S(1)}, f32[8,2,16,384]{3,2,1,0:T(8,128)S(1)}, u32[]{:S(2)}, u32[]{:S(2)}) collective-permute-start(f32[8,2,16,384]{3,2,1,0:T(8,128)S(1)} %all_to_all.23.blocks_ref), channel_id=1, source_target_pairs={{0,1},{1,0},{2,3},{3,2},{4,5},{5,4},{6,7},{7,6},{8,9},{9,8},{10,11... | collective-permute-start | bytes 1179656 | tf_op jit(solution)/shard_map/ppermute | solution.py:256

commit v4 on v3

--- a/solution.py
+++ b/solution.py
@@ -46,10 +46,8 @@
         for copy in copies(block, block % depth):
             copy.wait()
         for part in range(2):
-            hi, lo = split(stage[block % depth, part])
             where = (pl.ds(block * rows, rows), pl.ds(part * rows, rows))
-            hi_ref[where] = hi.T
-            lo_ref[where] = lo.T
+            hi_ref[where], lo_ref[where] = split(stage[block % depth, part].T)
 
 
 def prepare(other, real_rows, imag_rows, *after):
@@ -80,6 +78,7 @@
 
 def relative(at):
     step, across = divmod(at, 2)
+    step = (0, 1, 3, 2)[step]
     count = lax.axis_size("y")
     y, zl = lax.axis_index("y"), lax.axis_index("zl")
     return 2 * ((y + count - step) % count) + (1 - zl if across else zl)
@@ -210,7 +209,7 @@
     pair = stack([fields[None], across[None]], own_weights[0])
     others = [
         lax.ppermute(pair, "y", [(i, (i + step) % count) for i in range(count)])
-        for step in range(1, count)
+        for step in (1, 3, 2)
     ]
     other_weights = prepare(True, real_rows, imag_rows, pair)
     return stack([pair, *others], other_weights[0]), *own_weights, *other_weights

time: 96.8 us -> 96.9 us (level)
  no operation moved by 1% of the time
where the time goes in v4:
time: 96.9 us; the launch traced here: 96.6 us
  blocking collectives  39.8 us (41%)
  starting transfers between devices  32.1 us (33%)
  Pallas kernels  12.9 us (13%)
  waiting for transfers between devices  11.5 us (12%)
    all_to_all x4, blocking collectives, gather_chips(): lax.all_to_all(copies, CHIPS, split_axis=0, concat_axis=0, tiled=True)  39.8 us
    ppermute x8, starting transfers between devices, hand_over(): return lax.ppermute(traces, ('sx', 'sy', 'core'), pairs)  16.7 us
    ppermute x5, starting transfers between devices, shards(): other = lax.ppermute(own, 'core', ring('core'))  9.67 us
    pallas_call x2, Pallas kernels, prepare(): pl.pallas_call(functools.partial(prepare_body, other), in_specs=[pl.Block...  8.81 us
    ppermute x8, waiting for transfers between devices, hand_over(): return lax.ppermute(traces, ('sx', 'sy', 'core'), pairs)  6.12 us
    ppermute x5, waiting for transfers between devices, shards(): other = lax.ppermute(own, 'core', ring('core'))  5.4 us
    ppermute x3, starting transfers between devices, start(): lax.ppermute(pair, 'y', [(i, (i + step) % count) for i in range(count)])  4.45 us
    pallas_call x10, Pallas kernels, half_call(): pl.pallas_call(functools.partial(body, turn), in_specs=[vmem] * (1 + len(...  3.94 us
  transfers between devices with their start and end apart: 17, of which 8 were waited for; matrix products, arithmetic and copies ran while one was open for 0% of the time, Pallas kernels for 11%

profile of v4, /device:TPU:71, one launch (start us, length us, event | category | flops | bytes accessed | tf_op | source)
XLA Modules:
  0.0 96.6 jit_solution(2326470767164055412)
XLA Ops:
  0.0 1.3 %collective-permute-start = (f32[2,16,384]{2,1,0:T(8,128)}, f32[2,16,384]{2,1,0:T(8,128)S(1)}, u32[]{:S(2)}, u32[]{:S(2)}) collective-permute-start(f32[2,16,384]{2,1,0:T(8,128)} %bitcast.8), channel_id=1, source_target_pairs={{0,2},{2,0},{1,3},{3,1},{4,6},{6,4},{5,7},{7,5},{8,10},{10,8},{9,1... | collective-permute-start | bytes 147464 | tf_op jit(solution)/shard_map/ppermute | solution.py:207
  1.3 0.0 copy-start
  1.3 4.4 %prepare_own.1 = (bf16[3072,768]{1,0:T(8,128)(2,1)S(1)}, bf16[3072,768]{1,0:T(8,128)(2,1)S(1)}) custom-call(f32[384,6144]{1,0:T(8,128)} %bitcast.24, f32[384,6144]{1,0:T(8,128)} %bitcast.26), custom_call_target="tpu_custom_call" | custom-call | bytes 9437184 | tf_op jit(solution)/shard_map/prepare_own/pallas_call | solution.py:56
  5.8 0.0 collective-permute-done
  5.8 0.0 copy-done
  5.8 1.4 %collective-permute-start.1 = (f32[2,2,16,384]{3,2,1,0:T(8,128)S(1)}, f32[2,2,16,384]{3,2,1,0:T(8,128)S(1)}, u32[]{:S(2)}, u32[]{:S(2)}) collective-permute-start(f32[2,2,16,384]{3,2,1,0:T(8,128)S(1)} %stack.2.refs_0_), channel_id=1, source_target_pairs={{0,4},{4,8},{8,12},{12,0},{1,5},{5,9},{9,13},{13,1},{2,6},{6,10},{... | collective-permute-start | bytes 294920 | tf_op jit(solution)/shard_map/ppermute | solution.py:211
  7.2 1.5 %collective-permute-start.2 = (f32[2,2,16,384]{3,2,1,0:T(8,128)S(1)}, f32[2,2,16,384]{3,2,1,0:T(8,128)S(1)}, u32[]{:S(2)}, u32[]{:S(2)}) collective-permute-start(f32[2,2,16,384]{3,2,1,0:T(8,128)S(1)} %stack.2.refs_0_), channel_id=1, source_target_pairs={{0,12},{4,0},{8,4},{12,8},{1,13},{5,1},{9,5},{13,9},{2,14},{6,2},{... | collective-permute-start | bytes 294920 | tf_op jit(solution)/shard_map/ppermute | solution.py:211
  8.7 1.6 %collective-permute-start.3 = (f32[2,2,16,384]{3,2,1,0:T(8,128)S(1)}, f32[2,2,16,384]{3,2,1,0:T(8,128)S(1)}, u32[]{:S(2)}, u32[]{:S(2)}) collective-permute-start(f32[2,2,16,384]{3,2,1,0:T(8,128)S(1)} %stack.2.refs_0_), channel_id=1, source_target_pairs={{0,8},{4,12},{8,0},{12,4},{1,9},{5,13},{9,1},{13,5},{2,10},{6,14},... | collective-permute-start | bytes 294920 | tf_op jit(solution)/shard_map/ppermute | solution.py:211
  10.2 4.4 %prepare_other.1 = (bf16[3072,768]{1,0:T(8,128)(2,1)S(1)}, bf16[3072,768]{1,0:T(8,128)(2,1)S(1)}) custom-call(f32[384,6144]{1,0:T(8,128)} %bitcast.25, f32[384,6144]{1,0:T(8,128)} %bitcast.27, f32[2,2,16,384]{3,2,1,0:T(8,128)S(1)} %stack.2.refs_0_), custom_call_target="tpu_custom_call" | custom-call | bytes 9437184 | tf_op jit(solution)/shard_map/prepare_other/pallas_call | solution.py:56
  14.7 0.0 collective-permute-done.1.refs_1_
  14.7 0.0 collective-permute-done.2.refs_2_
  14.7 0.0 collective-permute-done.3.refs_3_
  14.7 1.9 %collective-permute-start.4 = (f32[8,2,16,384]{3,2,1,0:T(8,128)S(1)}, f32[8,2,16,384]{3,2,1,0:T(8,128)S(1)}, u32[]{:S(2)}, u32[]{:S(2)}) collective-permute-start(f32[8,2,16,384]{3,2,1,0:T(8,128)S(1)} %stack.3.blocks_ref), channel_id=1, source_target_pairs={{0,1},{1,0},{2,3},{3,2},{4,5},{5,4},{6,7},{7,6},{8,9},{9,8},{10,11... | collective-permute-start | bytes 1179656 | tf_op jit(solution)/shard_map/ppermute | solution.py:255
  16.6 1.3 %collective-permute-done.4.blocks_ref = f32[8,2,16,384]{3,2,1,0:T(8,128)S(1)} collective-permute-done((f32[8,2,16,384]{3,2,1,0:T(8,128)S(1)}, f32[8,2,16,384]{3,2,1,0:T(8,128)S(1)}, u32[]{:S(2)}, u32[]{:S(2)}) %collective-permute-start.4) | collective-permute-done | bytes 393248 | tf_op jit(solution)/shard_map/ppermute | solution.py:255
  18.0 0.0 copy-start.1
  18.0 0.0 copy-start.2
  18.0 0.8 collective-permute-start.5
  18.8 0.5 collective-permute-start.6
  19.2 0.0 collective-permute-done.5.left_ref
  19.2 0.9 collective-permute-done.6.below_ref
  20.1 0.0 copy-done.1
  20.1 0.0 copy-done.2
  20.2 10.1 %all_to_all.20.blocks_ref = f32[8,2,16,384]{3,2,1,0:T(8,128)S(1)} all-to-all(f32[8,2,16,384]{3,2,1,0:T(8,128)S(1)} %combine.4), channel_id=1, replica_groups=mesh['sx'=4,'sy'=2,'y'=4,'zl'=2,'core'=2] {'y','zl'}, dimensions={0} | all-to-all | bytes 786432 | tf_op jit(solution)/shard_map/all_to_all | solution.py:180
  30.2 1.8 %collective-permute-start.7 = (f32[8,2,16,384]{3,2,1,0:T(8,128)S(1)}, f32[8,2,16,384]{3,2,1,0:T(8,128)S(1)}, u32[]{:S(2)}, u32[]{:S(2)}) collective-permute-start(f32[8,2,16,384]{3,2,1,0:T(8,128)S(1)} %all_to_all.20.blocks_ref), channel_id=1, source_target_pairs={{0,1},{1,0},{2,3},{3,2},{4,5},{5,4},{6,7},{7,6},{8,9},{9,8},{10,11... | collective-permute-start | bytes 1179656 | tf_op jit(solution)/shard_map/ppermute | solution.py:255
  32.1 1.3 %collective-permute-done.7.blocks_ref = f32[8,2,16,384]{3,2,1,0:T(8,128)S(1)} collective-permute-done((f32[8,2,16,384]{3,2,1,0:T(8,128)S(1)}, f32[8,2,16,384]{3,2,1,0:T(8,128)S(1)}, u32[]{:S(2)}, u32[]{:S(2)}) %collective-permute-start.7) | collective-permute-done | bytes 393248 | tf_op jit(solution)/shard_map/ppermute | solution.py:255
  33.4 0.7 collective-permute-start.8
  34.1 0.5 collective-permute-start.9
  34.5 0.0 collective-permute-done.8.left_ref
  34.6 0.9 collective-permute-done.9.below_ref
  35.5 10.0 %all_to_all.21.blocks_ref = f32[8,2,16,384]{3,2,1,0:T(8,128)S(1)} all-to-all(f32[8,2,16,384]{3,2,1,0:T(8,128)S(1)} %combine.5), channel_id=1, replica_groups=mesh['sx'=4,'sy'=2,'y'=4,'zl'=2,'core'=2] {'y','zl'}, dimensions={0} | all-to-all | bytes 786432 | tf_op jit(solution)/shard_map/all_to_all | solution.py:180
  45.5 1.8 %collective-permute-start.10 = (f32[8,2,16,384]{3,2,1,0:T(8,128)S(1)}, f32[8,2,16,384]{3,2,1,0:T(8,128)S(1)}, u32[]{:S(2)}, u32[]{:S(2)}) collective-permute-start(f32[8,2,16,384]{3,2,1,0:T(8,128)S(1)} %all_to_all.21.blocks_ref), channel_id=1, source_target_pairs={{0,1},{1,0},{2,3},{3,2},{4,5},{5,4},{6,7},{7,6},{8,9},{9,8},{10,11... | collective-permute-start | bytes 1179656 | tf_op jit(solution)/shard_map/ppermute | solution.py:255
  47.4 1.3 %collective-permute-done.10.blocks_ref = f32[8,2,16,384]{3,2,1,0:T(8,128)S(1)} collective-permute-done((f32[8,2,16,384]{3,2,1,0:T(8,128)S(1)}, f32[8,2,16,384]{3,2,1,0:T(8,128)S(1)}, u32[]{:S(2)}, u32[]{:S(2)}) %collective-permute-start.10) | collective-permute-done | bytes 393248 | tf_op jit(solution)/shard_map/ppermute | solution.py:255
  48.7 0.7 collective-permute-start.11
  49.4 0.5 collective-permute-start.12
  49.8 0.0 collective-permute-done.11.left_ref
  49.8 0.9 collective-permute-done.12.below_ref
  50.8 10.0 %all_to_all.22.blocks_ref = f32[8,2,16,384]{3,2,1,0:T(8,128)S(1)} all-to-all(f32[8,2,16,384]{3,2,1,0:T(8,128)S(1)} %combine.6), channel_id=1, replica_groups=mesh['sx'=4,'sy'=2,'y'=4,'zl'=2,'core'=2] {'y','zl'}, dimensions={0} | all-to-all | bytes 786432 | tf_op jit(solution)/shard_map/all_to_all | solution.py:180
  60.8 1.8 %collective-permute-start.13 = (f32[8,2,16,384]{3,2,1,0:T(8,128)S(1)}, f32[8,2,16,384]{3,2,1,0:T(8,128)S(1)}, u32[]{:S(2)}, u32[]{:S(2)}) collective-permute-start(f32[8,2,16,384]{3,2,1,0:T(8,128)S(1)} %all_to_all.22.blocks_ref), channel_id=1, source_target_pairs={{0,1},{1,0},{2,3},{3,2},{4,5},{5,4},{6,7},{7,6},{8,9},{9,8},{10,11... | collective-permute-start | bytes 1179656 | tf_op jit(solution)/shard_map/ppermute | solution.py:255
  62.6 1.3 %collective-permute-done.13.blocks_ref = f32[8,2,16,384]{3,2,1,0:T(8,128)S(1)} collective-permute-done((f32[8,2,16,384]{3,2,1,0:T(8,128)S(1)}, f32[8,2,16,384]{3,2,1,0:T(8,128)S(1)}, u32[]{:S(2)}, u32[]{:S(2)}) %collective-permute-start.13) | collective-permute-done | bytes 393248 | tf_op jit(solution)/shard_map/ppermute | solution.py:255
  64.0 1.3 %collective-permute-start.14 = (f32[2,16,384]{2,1,0:T(8,128)S(1)}, f32[2,16,384]{2,1,0:T(8,128)S(1)}, u32[]{:S(2)}, u32[]{:S(2)}) collective-permute-start(f32[2,16,384]{2,1,0:T(8,128)S(1)} %second_half.8.before_ref), channel_id=1, source_target_pairs={{80,112},{81,113},{82,114},{83,115},{84,116},{85,117},{86,118},{87... | collective-permute-start | bytes 147464 | tf_op jit(solution)/shard_map/ppermute | solution.py:239
  65.3 11.9 %collective-permute-start.15 = (f32[2,16,384]{2,1,0:T(8,128)S(1)}, f32[2,16,384]{2,1,0:T(8,128)S(1)}, u32[]{:S(2)}, u32[]{:S(2)}) collective-permute-start(f32[2,16,384]{2,1,0:T(8,128)S(1)} %second_half.8.before_ref), channel_id=1, source_target_pairs={{0,1},{1,0},{16,17},{17,16},{32,33},{33,32},{48,49},{49,48},{64,65... | collective-permute-start | bytes 147464 | tf_op jit(solution)/shard_map/ppermute | solution.py:239
  77.2 3.5 %collective-permute-done.14.left_ref = f32[2,16,384]{2,1,0:T(8,128)S(1)} collective-permute-done((f32[2,16,384]{2,1,0:T(8,128)S(1)}, f32[2,16,384]{2,1,0:T(8,128)S(1)}, u32[]{:S(2)}, u32[]{:S(2)}) %collective-permute-start.14) | collective-permute-done | bytes 49184 | tf_op jit(solution)/shard_map/ppermute | solution.py:239
  80.7 0.0 collective-permute-done.15.below_ref
  80.7 9.6 %all_to_all.23.blocks_ref = f32[8,2,16,384]{3,2,1,0:T(8,128)S(1)} all-to-all(f32[8,2,16,384]{3,2,1,0:T(8,128)S(1)} %combine.7), channel_id=1, replica_groups=mesh['sx'=4,'sy'=2,'y'=4,'zl'=2,'core'=2] {'y','zl'}, dimensions={0} | all-to-all | bytes 786432 | tf_op jit(solution)/shard_map/all_to_all | solution.py:180
  90.4 2.2 %collective-permute-start.16 = (f32[8,2,16,384]{3,2,1,0:T(8,128)S(1)}, f32[8,2,16,384]{3,2,1,0:T(8,128)S(1)}, u32[]{:S(2)}, u32[]{:S(2)}) collective-permute-start(f32[8,2,16,384]{3,2,1,0:T(8,128)S(1)} %all_to_all.23.blocks_ref), channel_id=1, source_target_pairs={{0,1},{1,0},{2,3},{3,2},{4,5},{5,4},{6,7},{7,6},{8,9},{9,8},{10,11... | collective-permute-start | bytes 1179656 | tf_op jit(solution)/shard_map/ppermute | solution.py:255
  92.6 1.6 %first_half.9.first_ref = f32[32,768]{1,0:T(8,128)S(1)} custom-call(f32[8,2,16,384]{3,2,1,0:T(8,128)S(1)} %all_to_all.23.blocks_ref, bf16[3072,768]{1,0:T(8,128)(2,1)S(1)} %get-tuple-element.9.refs_2_.hi_ref, bf16[3072,768]{1,0:T(8,128)(2,1)S(1)} %get-tuple-element.12.lo_ref), custom_call_target="tpu_custom_call" | custom-call | tf_op jit(solution)/shard_map/first_half/pallas_call | solution.py:136
  94.3 0.0 collective-permute-done.16.blocks_ref
  94.3 2.3 %second_half.9 = f32[2,16,384]{2,1,0:T(8,128)} custom-call(f32[8,2,16,384]{3,2,1,0:T(8,128)S(1)} %collective-permute-done.16.blocks_ref, bf16[3072,768]{1,0:T(8,128)(2,1)S(1)} %get-tuple-element.10.refs_4_.hi_ref, bf16[3072,768]{1,0:T(8,128)(2,1)S(1)} %get-tuple-element.11.lo_ref, f32[32,768]{1,0:T(8,128)S(1)} %first_half.9.first_ref, ...), custom_call_target="tpu_custom_call" | custom-call | tf_op jit(solution)/shard_map/second_half/pallas_call | solution.py:136
  (14 shorter events, 0.2 us)
Async XLA Ops:
  0.0 5.8 %collective-permute-start = (f32[2,16,384]{2,1,0:T(8,128)}, f32[2,16,384]{2,1,0:T(8,128)S(1)}, u32[]{:S(2)}, u32[]{:S(2)}) collective-permute-start(f32[2,16,384]{2,1,0:T(8,128)} %bitcast.8), channel_id=1, source_target_pairs={{0,2},{2,0},{1,3},{3,1},{4,6},{6,4},{5,7},{7,5},{8,10},{10,8},{9,1... | collective-permute-start | bytes 147464 | tf_op jit(solution)/shard_map/ppermute | solution.py:207
  1.3 4.4 %copy-start = (f32[1,1,2,16,384]{4,3,2,1,0:T(8,128)S(1)}, f32[1,1,2,16,384]{4,3,2,1,0:T(8,128)}, u32[]{:S(2)}) copy-start(f32[1,1,2,16,384]{4,3,2,1,0:T(8,128)} %param.9) | copy-start | bytes 147460
  5.8 8.9 %collective-permute-start.1 = (f32[2,2,16,384]{3,2,1,0:T(8,128)S(1)}, f32[2,2,16,384]{3,2,1,0:T(8,128)S(1)}, u32[]{:S(2)}, u32[]{:S(2)}) collective-permute-start(f32[2,2,16,384]{3,2,1,0:T(8,128)S(1)} %stack.2.refs_0_), channel_id=1, source_target_pairs={{0,4},{4,8},{8,12},{12,0},{1,5},{5,9},{9,13},{13,1},{2,6},{6,10},{... | collective-permute-start | bytes 294920 | tf_op jit(solution)/shard_map/ppermute | solution.py:211
  7.2 7.5 %collective-permute-start.2 = (f32[2,2,16,384]{3,2,1,0:T(8,128)S(1)}, f32[2,2,16,384]{3,2,1,0:T(8,128)S(1)}, u32[]{:S(2)}, u32[]{:S(2)}) collective-permute-start(f32[2,2,16,384]{3,2,1,0:T(8,128)S(1)} %stack.2.refs_0_), channel_id=1, source_target_pairs={{0,12},{4,0},{8,4},{12,8},{1,13},{5,1},{9,5},{13,9},{2,14},{6,2},{... | collective-permute-start | bytes 294920 | tf_op jit(solution)/shard_map/ppermute | solution.py:211
  8.7 6.0 %collective-permute-start.3 = (f32[2,2,16,384]{3,2,1,0:T(8,128)S(1)}, f32[2,2,16,384]{3,2,1,0:T(8,128)S(1)}, u32[]{:S(2)}, u32[]{:S(2)}) collective-permute-start(f32[2,2,16,384]{3,2,1,0:T(8,128)S(1)} %stack.2.refs_0_), channel_id=1, source_target_pairs={{0,8},{4,12},{8,0},{12,4},{1,9},{5,13},{9,1},{13,5},{2,10},{6,14},... | collective-permute-start | bytes 294920 | tf_op jit(solution)/shard_map/ppermute | solution.py:211
  14.7 3.2 %collective-permute-start.4 = (f32[8,2,16,384]{3,2,1,0:T(8,128)S(1)}, f32[8,2,16,384]{3,2,1,0:T(8,128)S(1)}, u32[]{:S(2)}, u32[]{:S(2)}) collective-permute-start(f32[8,2,16,384]{3,2,1,0:T(8,128)S(1)} %stack.3.blocks_ref), channel_id=1, source_target_pairs={{0,1},{1,0},{2,3},{3,2},{4,5},{5,4},{6,7},{7,6},{8,9},{9,8},{10,11... | collective-permute-start | bytes 1179656 | tf_op jit(solution)/shard_map/ppermute | solution.py:255
  18.0 2.2 %copy-start.1 = (f32[1,1,2,384]{3,2,1,0:T(2,128)S(1)}, f32[1,1,2,384]{3,2,1,0:T(2,128)}, u32[]{:S(2)}) copy-start(f32[1,1,2,384]{3,2,1,0:T(2,128)} %param.7) | copy-start | bytes 9220
  18.0 2.2 %copy-start.2 = (f32[1,1,2,384]{3,2,1,0:T(2,128)S(1)}, f32[1,1,2,384]{3,2,1,0:T(2,128)}, u32[]{:S(2)}) copy-start(f32[1,1,2,384]{3,2,1,0:T(2,128)} %param.8) | copy-start | bytes 9220
  18.0 1.3 %collective-permute-start.5 = (f32[2,16,384]{2,1,0:T(8,128)S(1)}, f32[2,16,384]{2,1,0:T(8,128)S(1)}, u32[]{:S(2)}, u32[]{:S(2)}) collective-permute-start(f32[2,16,384]{2,1,0:T(8,128)S(1)} %second_half.5.before_ref), channel_id=1, source_target_pairs={{0,32},{1,33},{2,34},{3,35},{4,36},{5,37},{6,38},{7,39},{8,40},{9,... | collective-permute-start | bytes 147464 | tf_op jit(solution)/shard_map/ppermute | solution.py:239
  18.8 1.3 %collective-permute-start.6 = (f32[2,16,384]{2,1,0:T(8,128)S(1)}, f32[2,16,384]{2,1,0:T(8,128)S(1)}, u32[]{:S(2)}, u32[]{:S(2)}) collective-permute-start(f32[2,16,384]{2,1,0:T(8,128)S(1)} %second_half.5.before_ref), channel_id=1, source_target_pairs={{0,16},{1,17},{16,0},{17,1},{32,33},{33,32},{48,49},{49,48},{64,65... | collective-permute-start | bytes 147464 | tf_op jit(solution)/shard_map/ppermute | solution.py:239
  30.2 3.2 %collective-permute-start.7 = (f32[8,2,16,384]{3,2,1,0:T(8,128)S(1)}, f32[8,2,16,384]{3,2,1,0:T(8,128)S(1)}, u32[]{:S(2)}, u32[]{:S(2)}) collective-permute-start(f32[8,2,16,384]{3,2,1,0:T(8,128)S(1)} %all_to_all.20.blocks_ref), channel_id=1, source_target_pairs={{0,1},{1,0},{2,3},{3,2},{4,5},{5,4},{6,7},{7,6},{8,9},{9,8},{10,11... | collective-permute-start | bytes 1179656 | tf_op jit(solution)/shard_map/ppermute | solution.py:255
  33.4 1.1 %collective-permute-start.8 = (f32[2,16,384]{2,1,0:T(8,128)S(1)}, f32[2,16,384]{2,1,0:T(8,128)S(1)}, u32[]{:S(2)}, u32[]{:S(2)}) collective-permute-start(f32[2,16,384]{2,1,0:T(8,128)S(1)} %second_half.6.before_ref), channel_id=1, source_target_pairs={{16,48},{17,49},{32,64},{33,65},{18,50},{19,51},{34,66},{35,67},{2... | collective-permute-start | bytes 147464 | tf_op jit(solution)/shard_map/ppermute | solution.py:239
  34.1 1.3 %collective-permute-start.9 = (f32[2,16,384]{2,1,0:T(8,128)S(1)}, f32[2,16,384]{2,1,0:T(8,128)S(1)}, u32[]{:S(2)}, u32[]{:S(2)}) collective-permute-start(f32[2,16,384]{2,1,0:T(8,128)S(1)} %second_half.6.before_ref), channel_id=1, source_target_pairs={{0,1},{1,0},{16,17},{17,16},{32,48},{33,49},{48,32},{49,33},{64,65... | collective-permute-start | bytes 147464 | tf_op jit(solution)/shard_map/ppermute | solution.py:239
  45.5 3.2 %collective-permute-start.10 = (f32[8,2,16,384]{3,2,1,0:T(8,128)S(1)}, f32[8,2,16,384]{3,2,1,0:T(8,128)S(1)}, u32[]{:S(2)}, u32[]{:S(2)}) collective-permute-start(f32[8,2,16,384]{3,2,1,0:T(8,128)S(1)} %all_to_all.21.blocks_ref), channel_id=1, source_target_pairs={{0,1},{1,0},{2,3},{3,2},{4,5},{5,4},{6,7},{7,6},{8,9},{9,8},{10,11... | collective-permute-start | bytes 1179656 | tf_op jit(solution)/shard_map/ppermute | solution.py:255
  48.7 1.1 %collective-permute-start.11 = (f32[2,16,384]{2,1,0:T(8,128)S(1)}, f32[2,16,384]{2,1,0:T(8,128)S(1)}, u32[]{:S(2)}, u32[]{:S(2)}) collective-permute-start(f32[2,16,384]{2,1,0:T(8,128)S(1)} %second_half.7.before_ref), channel_id=1, source_target_pairs={{48,80},{49,81},{64,96},{65,97},{50,82},{51,83},{66,98},{67,99},{5... | collective-permute-start | bytes 147464 | tf_op jit(solution)/shard_map/ppermute | solution.py:239
  49.4 1.3 %collective-permute-start.12 = (f32[2,16,384]{2,1,0:T(8,128)S(1)}, f32[2,16,384]{2,1,0:T(8,128)S(1)}, u32[]{:S(2)}, u32[]{:S(2)}) collective-permute-start(f32[2,16,384]{2,1,0:T(8,128)S(1)} %second_half.7.before_ref), channel_id=1, source_target_pairs={{0,1},{1,0},{16,17},{17,16},{32,33},{33,32},{48,49},{49,48},{64,80... | collective-permute-start | bytes 147464 | tf_op jit(solution)/shard_map/ppermute | solution.py:239
  60.8 3.2 %collective-permute-start.13 = (f32[8,2,16,384]{3,2,1,0:T(8,128)S(1)}, f32[8,2,16,384]{3,2,1,0:T(8,128)S(1)}, u32[]{:S(2)}, u32[]{:S(2)}) collective-permute-start(f32[8,2,16,384]{3,2,1,0:T(8,128)S(1)} %all_to_all.22.blocks_ref), channel_id=1, source_target_pairs={{0,1},{1,0},{2,3},{3,2},{4,5},{5,4},{6,7},{7,6},{8,9},{9,8},{10,11... | collective-permute-start | bytes 1179656 | tf_op jit(solution)/shard_map/ppermute | solution.py:255
  64.0 16.7 %collective-permute-start.14 = (f32[2,16,384]{2,1,0:T(8,128)S(1)}, f32[2,16,384]{2,1,0:T(8,128)S(1)}, u32[]{:S(2)}, u32[]{:S(2)}) collective-permute-start(f32[2,16,384]{2,1,0:T(8,128)S(1)} %second_half.8.before_ref), channel_id=1, source_target_pairs={{80,112},{81,113},{82,114},{83,115},{84,116},{85,117},{86,118},{87... | collective-permute-start | bytes 147464 | tf_op jit(solution)/shard_map/ppermute | solution.py:239
  65.3 15.4 %collective-permute-start.15 = (f32[2,16,384]{2,1,0:T(8,128)S(1)}, f32[2,16,384]{2,1,0:T(8,128)S(1)}, u32[]{:S(2)}, u32[]{:S(2)}) collective-permute-start(f32[2,16,384]{2,1,0:T(8,128)S(1)} %second_half.8.before_ref), channel_id=1, source_target_pairs={{0,1},{1,0},{16,17},{17,16},{32,33},{33,32},{48,49},{49,48},{64,65... | collective-permute-start | bytes 147464 | tf_op jit(solution)/shard_map/ppermute | solution.py:239
  90.4 3.9 %collective-permute-start.16 = (f32[8,2,16,384]{3,2,1,0:T(8,128)S(1)}, f32[8,2,16,384]{3,2,1,0:T(8,128)S(1)}, u32[]{:S(2)}, u32[]{:S(2)}) collective-permute-start(f32[8,2,16,384]{3,2,1,0:T(8,128)S(1)} %all_to_all.23.blocks_ref), channel_id=1, source_target_pairs={{0,1},{1,0},{2,3},{3,2},{4,5},{5,4},{6,7},{7,6},{8,9},{9,8},{10,11... | collective-permute-start | bytes 1179656 | tf_op jit(solution)/shard_map/ppermute | solution.py:255

commit v5 on v4

--- a/solution.py
+++ b/solution.py
@@ -43,9 +43,9 @@
         if ahead < blocks:
             for copy in copies(ahead, ahead % depth):
                 copy.start()
-        for copy in copies(block, block % depth):
-            copy.wait()
+        arriving = copies(block, block % depth)
         for part in range(2):
+            arriving[part].wait()
             where = (pl.ds(block * rows, rows), pl.ds(part * rows, rows))
             hi_ref[where], lo_ref[where] = split(stage[block % depth, part].T)
 

time: 96.9 us -> 97.8 us (level)
  Pallas kernels: 12.9 us -> 14.2 us
    pallas_call x2, Pallas kernels: 8.81 us -> 10.1 us  [prepare(): pl.pallas_call(functools.partial(prepare_body, other), in_specs=[pl.Block...]
  transfers between devices with their start and end apart: 17 -> 17, of which waited for: 8 -> 8; matrix products, arithmetic and copies ran while one was open for 0% -> 0% of each run, Pallas kernels for 11% -> 12%
where the time goes in v5:
time: 97.8 us; the launch traced here: 97.5 us
  blocking collectives  39.8 us (41%)
  starting transfers between devices  31.8 us (33%)
  Pallas kernels  14.2 us (15%)
  waiting for transfers between devices  11.6 us (12%)
    all_to_all x4, blocking collectives, gather_chips(): lax.all_to_all(copies, CHIPS, split_axis=0, concat_axis=0, tiled=True)  39.8 us
    ppermute x8, starting transfers between devices, hand_over(): return lax.ppermute(traces, ('sx', 'sy', 'core'), pairs)  16.4 us
    pallas_call x2, Pallas kernels, prepare(): pl.pallas_call(functools.partial(prepare_body, other), in_specs=[pl.Block...  10.1 us
    ppermute x5, starting transfers between devices, shards(): other = lax.ppermute(own, 'core', ring('core'))  9.61 us
    ppermute x8, waiting for transfers between devices, hand_over(): return lax.ppermute(traces, ('sx', 'sy', 'core'), pairs)  6.19 us
    ppermute x5, waiting for transfers between devices, shards(): other = lax.ppermute(own, 'core', ring('core'))  5.4 us
    ppermute x3, starting transfers between devices, start(): lax.ppermute(pair, 'y', [(i, (i + step) % count) for i in range(count)])  4.45 us
    pallas_call x10, Pallas kernels, half_call(): pl.pallas_call(functools.partial(body, turn), in_specs=[vmem] * (1 + len(...  3.94 us
  transfers between devices with their start and end apart: 17, of which 8 were waited for; matrix products, arithmetic and copies ran while one was open for 0% of the time, Pallas kernels for 12%

profile of v5, /device:TPU:71, one launch (start us, length us, event | category | flops | bytes accessed | tf_op | source)
XLA Modules:
  0.0 97.5 jit_solution(18159582373421771845)
XLA Ops:
  0.0 1.3 %collective-permute-start = (f32[2,16,384]{2,1,0:T(8,128)}, f32[2,16,384]{2,1,0:T(8,128)S(1)}, u32[]{:S(2)}, u32[]{:S(2)}) collective-permute-start(f32[2,16,384]{2,1,0:T(8,128)} %bitcast.8), channel_id=1, source_target_pairs={{0,2},{2,0},{1,3},{3,1},{4,6},{6,4},{5,7},{7,5},{8,10},{10,8},{9,1... | collective-permute-start | bytes 147464 | tf_op jit(solution)/shard_map/ppermute | solution.py:207
  1.3 0.0 copy-start
  1.3 5.1 %prepare_own.1 = (bf16[3072,768]{1,0:T(8,128)(2,1)S(1)}, bf16[3072,768]{1,0:T(8,128)(2,1)S(1)}) custom-call(f32[384,6144]{1,0:T(8,128)} %bitcast.24, f32[384,6144]{1,0:T(8,128)} %bitcast.26), custom_call_target="tpu_custom_call" | custom-call | bytes 9437184 | tf_op jit(solution)/shard_map/prepare_own/pallas_call | solution.py:56
  6.4 0.0 collective-permute-done
  6.4 0.0 copy-done
  6.4 1.4 %collective-permute-start.1 = (f32[2,2,16,384]{3,2,1,0:T(8,128)S(1)}, f32[2,2,16,384]{3,2,1,0:T(8,128)S(1)}, u32[]{:S(2)}, u32[]{:S(2)}) collective-permute-start(f32[2,2,16,384]{3,2,1,0:T(8,128)S(1)} %stack.2.refs_0_), channel_id=1, source_target_pairs={{0,4},{4,8},{8,12},{12,0},{1,5},{5,9},{9,13},{13,1},{2,6},{6,10},{... | collective-permute-start | bytes 294920 | tf_op jit(solution)/shard_map/ppermute | solution.py:211
  7.8 1.5 %collective-permute-start.2 = (f32[2,2,16,384]{3,2,1,0:T(8,128)S(1)}, f32[2,2,16,384]{3,2,1,0:T(8,128)S(1)}, u32[]{:S(2)}, u32[]{:S(2)}) collective-permute-start(f32[2,2,16,384]{3,2,1,0:T(8,128)S(1)} %stack.2.refs_0_), channel_id=1, source_target_pairs={{0,12},{4,0},{8,4},{12,8},{1,13},{5,1},{9,5},{13,9},{2,14},{6,2},{... | collective-permute-start | bytes 294920 | tf_op jit(solution)/shard_map/ppermute | solution.py:211
  9.3 1.6 %collective-permute-start.3 = (f32[2,2,16,384]{3,2,1,0:T(8,128)S(1)}, f32[2,2,16,384]{3,2,1,0:T(8,128)S(1)}, u32[]{:S(2)}, u32[]{:S(2)}) collective-permute-start(f32[2,2,16,384]{3,2,1,0:T(8,128)S(1)} %stack.2.refs_0_), channel_id=1, source_target_pairs={{0,8},{4,12},{8,0},{12,4},{1,9},{5,13},{9,1},{13,5},{2,10},{6,14},... | collective-permute-start | bytes 294920 | tf_op jit(solution)/shard_map/ppermute | solution.py:211
  10.9 5.1 %prepare_other.1 = (bf16[3072,768]{1,0:T(8,128)(2,1)S(1)}, bf16[3072,768]{1,0:T(8,128)(2,1)S(1)}) custom-call(f32[384,6144]{1,0:T(8,128)} %bitcast.25, f32[384,6144]{1,0:T(8,128)} %bitcast.27, f32[2,2,16,384]{3,2,1,0:T(8,128)S(1)} %stack.2.refs_0_), custom_call_target="tpu_custom_call" | custom-call | bytes 9437184 | tf_op jit(solution)/shard_map/prepare_other/pallas_call | solution.py:56
  16.0 0.0 collective-permute-done.1.refs_1_
  16.0 0.0 collective-permute-done.2.refs_2_
  16.0 0.0 collective-permute-done.3.refs_3_
  16.0 1.9 %collective-permute-start.4 = (f32[8,2,16,384]{3,2,1,0:T(8,128)S(1)}, f32[8,2,16,384]{3,2,1,0:T(8,128)S(1)}, u32[]{:S(2)}, u32[]{:S(2)}) collective-permute-start(f32[8,2,16,384]{3,2,1,0:T(8,128)S(1)} %stack.3.blocks_ref), channel_id=1, source_target_pairs={{0,1},{1,0},{2,3},{3,2},{4,5},{5,4},{6,7},{7,6},{8,9},{9,8},{10,11... | collective-permute-start | bytes 1179656 | tf_op jit(solution)/shard_map/ppermute | solution.py:255
  17.9 1.3 %collective-permute-done.4.blocks_ref = f32[8,2,16,384]{3,2,1,0:T(8,128)S(1)} collective-permute-done((f32[8,2,16,384]{3,2,1,0:T(8,128)S(1)}, f32[8,2,16,384]{3,2,1,0:T(8,128)S(1)}, u32[]{:S(2)}, u32[]{:S(2)}) %collective-permute-start.4) | collective-permute-done | bytes 393248 | tf_op jit(solution)/shard_map/ppermute | solution.py:255
  19.3 0.0 copy-start.1
  19.3 0.0 copy-start.2
  19.3 0.8 collective-permute-start.5
  20.1 0.5 collective-permute-start.6
  20.5 0.0 collective-permute-done.5.left_ref
  20.5 0.9 collective-permute-done.6.below_ref
  21.4 0.0 copy-done.1
  21.4 0.0 copy-done.2
  21.5 10.1 %all_to_all.20.blocks_ref = f32[8,2,16,384]{3,2,1,0:T(8,128)S(1)} all-to-all(f32[8,2,16,384]{3,2,1,0:T(8,128)S(1)} %combine.4), channel_id=1, replica_groups=mesh['sx'=4,'sy'=2,'y'=4,'zl'=2,'core'=2] {'y','zl'}, dimensions={0} | all-to-all | bytes 786432 | tf_op jit(solution)/shard_map/all_to_all | solution.py:180
  31.5 1.8 %collective-permute-start.7 = (f32[8,2,16,384]{3,2,1,0:T(8,128)S(1)}, f32[8,2,16,384]{3,2,1,0:T(8,128)S(1)}, u32[]{:S(2)}, u32[]{:S(2)}) collective-permute-start(f32[8,2,16,384]{3,2,1,0:T(8,128)S(1)} %all_to_all.20.blocks_ref), channel_id=1, source_target_pairs={{0,1},{1,0},{2,3},{3,2},{4,5},{5,4},{6,7},{7,6},{8,9},{9,8},{10,11... | collective-permute-start | bytes 1179656 | tf_op jit(solution)/shard_map/ppermute | solution.py:255
  33.3 1.3 %collective-permute-done.7.blocks_ref = f32[8,2,16,384]{3,2,1,0:T(8,128)S(1)} collective-permute-done((f32[8,2,16,384]{3,2,1,0:T(8,128)S(1)}, f32[8,2,16,384]{3,2,1,0:T(8,128)S(1)}, u32[]{:S(2)}, u32[]{:S(2)}) %collective-permute-start.7) | collective-permute-done | bytes 393248 | tf_op jit(solution)/shard_map/ppermute | solution.py:255
  34.7 0.7 collective-permute-start.8
  35.3 0.5 collective-permute-start.9
  35.8 0.0 collective-permute-done.8.left_ref
  35.8 0.9 collective-permute-done.9.below_ref
  36.7 10.0 %all_to_all.21.blocks_ref = f32[8,2,16,384]{3,2,1,0:T(8,128)S(1)} all-to-all(f32[8,2,16,384]{3,2,1,0:T(8,128)S(1)} %combine.5), channel_id=1, replica_groups=mesh['sx'=4,'sy'=2,'y'=4,'zl'=2,'core'=2] {'y','zl'}, dimensions={0} | all-to-all | bytes 786432 | tf_op jit(solution)/shard_map/all_to_all | solution.py:180
  46.7 1.8 %collective-permute-start.10 = (f32[8,2,16,384]{3,2,1,0:T(8,128)S(1)}, f32[8,2,16,384]{3,2,1,0:T(8,128)S(1)}, u32[]{:S(2)}, u32[]{:S(2)}) collective-permute-start(f32[8,2,16,384]{3,2,1,0:T(8,128)S(1)} %all_to_all.21.blocks_ref), channel_id=1, source_target_pairs={{0,1},{1,0},{2,3},{3,2},{4,5},{5,4},{6,7},{7,6},{8,9},{9,8},{10,11... | collective-permute-start | bytes 1179656 | tf_op jit(solution)/shard_map/ppermute | solution.py:255
  48.6 1.3 %collective-permute-done.10.blocks_ref = f32[8,2,16,384]{3,2,1,0:T(8,128)S(1)} collective-permute-done((f32[8,2,16,384]{3,2,1,0:T(8,128)S(1)}, f32[8,2,16,384]{3,2,1,0:T(8,128)S(1)}, u32[]{:S(2)}, u32[]{:S(2)}) %collective-permute-start.10) | collective-permute-done | bytes 393248 | tf_op jit(solution)/shard_map/ppermute | solution.py:255
  49.9 0.7 collective-permute-start.11
  50.6 0.5 collective-permute-start.12
  51.0 0.0 collective-permute-done.11.left_ref
  51.0 0.9 collective-permute-done.12.below_ref
  52.0 10.0 %all_to_all.22.blocks_ref = f32[8,2,16,384]{3,2,1,0:T(8,128)S(1)} all-to-all(f32[8,2,16,384]{3,2,1,0:T(8,128)S(1)} %combine.6), channel_id=1, replica_groups=mesh['sx'=4,'sy'=2,'y'=4,'zl'=2,'core'=2] {'y','zl'}, dimensions={0} | all-to-all | bytes 786432 | tf_op jit(solution)/shard_map/all_to_all | solution.py:180
  62.0 1.8 %collective-permute-start.13 = (f32[8,2,16,384]{3,2,1,0:T(8,128)S(1)}, f32[8,2,16,384]{3,2,1,0:T(8,128)S(1)}, u32[]{:S(2)}, u32[]{:S(2)}) collective-permute-start(f32[8,2,16,384]{3,2,1,0:T(8,128)S(1)} %all_to_all.22.blocks_ref), channel_id=1, source_target_pairs={{0,1},{1,0},{2,3},{3,2},{4,5},{5,4},{6,7},{7,6},{8,9},{9,8},{10,11... | collective-permute-start | bytes 1179656 | tf_op jit(solution)/shard_map/ppermute | solution.py:255
  63.9 1.3 %collective-permute-done.13.blocks_ref = f32[8,2,16,384]{3,2,1,0:T(8,128)S(1)} collective-permute-done((f32[8,2,16,384]{3,2,1,0:T(8,128)S(1)}, f32[8,2,16,384]{3,2,1,0:T(8,128)S(1)}, u32[]{:S(2)}, u32[]{:S(2)}) %collective-permute-start.13) | collective-permute-done | bytes 393248 | tf_op jit(solution)/shard_map/ppermute | solution.py:255
  65.2 1.3 %collective-permute-start.14 = (f32[2,16,384]{2,1,0:T(8,128)S(1)}, f32[2,16,384]{2,1,0:T(8,128)S(1)}, u32[]{:S(2)}, u32[]{:S(2)}) collective-permute-start(f32[2,16,384]{2,1,0:T(8,128)S(1)} %second_half.8.before_ref), channel_id=1, source_target_pairs={{80,112},{81,113},{82,114},{83,115},{84,116},{85,117},{86,118},{87... | collective-permute-start | bytes 147464 | tf_op jit(solution)/shard_map/ppermute | solution.py:239
  66.5 11.6 %collective-permute-start.15 = (f32[2,16,384]{2,1,0:T(8,128)S(1)}, f32[2,16,384]{2,1,0:T(8,128)S(1)}, u32[]{:S(2)}, u32[]{:S(2)}) collective-permute-start(f32[2,16,384]{2,1,0:T(8,128)S(1)} %second_half.8.before_ref), channel_id=1, source_target_pairs={{0,1},{1,0},{16,17},{17,16},{32,33},{33,32},{48,49},{49,48},{64,65... | collective-permute-start | bytes 147464 | tf_op jit(solution)/shard_map/ppermute | solution.py:239
  78.1 3.5 %collective-permute-done.14.left_ref = f32[2,16,384]{2,1,0:T(8,128)S(1)} collective-permute-done((f32[2,16,384]{2,1,0:T(8,128)S(1)}, f32[2,16,384]{2,1,0:T(8,128)S(1)}, u32[]{:S(2)}, u32[]{:S(2)}) %collective-permute-start.14) | collective-permute-done | bytes 49184 | tf_op jit(solution)/shard_map/ppermute | solution.py:239
  81.7 0.0 collective-permute-done.15.below_ref
  81.7 9.6 %all_to_all.23.blocks_ref = f32[8,2,16,384]{3,2,1,0:T(8,128)S(1)} all-to-all(f32[8,2,16,384]{3,2,1,0:T(8,128)S(1)} %combine.7), channel_id=1, replica_groups=mesh['sx'=4,'sy'=2,'y'=4,'zl'=2,'core'=2] {'y','zl'}, dimensions={0} | all-to-all | bytes 786432 | tf_op jit(solution)/shard_map/all_to_all | solution.py:180
  91.3 2.3 %collective-permute-start.16 = (f32[8,2,16,384]{3,2,1,0:T(8,128)S(1)}, f32[8,2,16,384]{3,2,1,0:T(8,128)S(1)}, u32[]{:S(2)}, u32[]{:S(2)}) collective-permute-start(f32[8,2,16,384]{3,2,1,0:T(8,128)S(1)} %all_to_all.23.blocks_ref), channel_id=1, source_target_pairs={{0,1},{1,0},{2,3},{3,2},{4,5},{5,4},{6,7},{7,6},{8,9},{9,8},{10,11... | collective-permute-start | bytes 1179656 | tf_op jit(solution)/shard_map/ppermute | solution.py:255
  93.6 1.6 %first_half.9.first_ref = f32[32,768]{1,0:T(8,128)S(1)} custom-call(f32[8,2,16,384]{3,2,1,0:T(8,128)S(1)} %all_to_all.23.blocks_ref, bf16[3072,768]{1,0:T(8,128)(2,1)S(1)} %get-tuple-element.9.refs_2_.hi_ref, bf16[3072,768]{1,0:T(8,128)(2,1)S(1)} %get-tuple-element.12.lo_ref), custom_call_target="tpu_custom_call" | custom-call | tf_op jit(solution)/shard_map/first_half/pallas_call | solution.py:136
  95.2 0.0 collective-permute-done.16.blocks_ref
  95.3 2.3 %second_half.9 = f32[2,16,384]{2,1,0:T(8,128)} custom-call(f32[8,2,16,384]{3,2,1,0:T(8,128)S(1)} %collective-permute-done.16.blocks_ref, bf16[3072,768]{1,0:T(8,128)(2,1)S(1)} %get-tuple-element.10.refs_4_.hi_ref, bf16[3072,768]{1,0:T(8,128)(2,1)S(1)} %get-tuple-element.11.lo_ref, f32[32,768]{1,0:T(8,128)S(1)} %first_half.9.first_ref, ...), custom_call_target="tpu_custom_call" | custom-call | tf_op jit(solution)/shard_map/second_half/pallas_call | solution.py:136
  (14 shorter events, 0.2 us)
Async XLA Ops:
  0.0 6.4 %collective-permute-start = (f32[2,16,384]{2,1,0:T(8,128)}, f32[2,16,384]{2,1,0:T(8,128)S(1)}, u32[]{:S(2)}, u32[]{:S(2)}) collective-permute-start(f32[2,16,384]{2,1,0:T(8,128)} %bitcast.8), channel_id=1, source_target_pairs={{0,2},{2,0},{1,3},{3,1},{4,6},{6,4},{5,7},{7,5},{8,10},{10,8},{9,1... | collective-permute-start | bytes 147464 | tf_op jit(solution)/shard_map/ppermute | solution.py:207
  1.3 5.1 %copy-start = (f32[1,1,2,16,384]{4,3,2,1,0:T(8,128)S(1)}, f32[1,1,2,16,384]{4,3,2,1,0:T(8,128)}, u32[]{:S(2)}) copy-start(f32[1,1,2,16,384]{4,3,2,1,0:T(8,128)} %param.9) | copy-start | bytes 147460
  6.4 9.5 %collective-permute-start.1 = (f32[2,2,16,384]{3,2,1,0:T(8,128)S(1)}, f32[2,2,16,384]{3,2,1,0:T(8,128)S(1)}, u32[]{:S(2)}, u32[]{:S(2)}) collective-permute-start(f32[2,2,16,384]{3,2,1,0:T(8,128)S(1)} %stack.2.refs_0_), channel_id=1, source_target_pairs={{0,4},{4,8},{8,12},{12,0},{1,5},{5,9},{9,13},{13,1},{2,6},{6,10},{... | collective-permute-start | bytes 294920 | tf_op jit(solution)/shard_map/ppermute | solution.py:211
  7.8 8.2 %collective-permute-start.2 = (f32[2,2,16,384]{3,2,1,0:T(8,128)S(1)}, f32[2,2,16,384]{3,2,1,0:T(8,128)S(1)}, u32[]{:S(2)}, u32[]{:S(2)}) collective-permute-start(f32[2,2,16,384]{3,2,1,0:T(8,128)S(1)} %stack.2.refs_0_), channel_id=1, source_target_pairs={{0,12},{4,0},{8,4},{12,8},{1,13},{5,1},{9,5},{13,9},{2,14},{6,2},{... | collective-permute-start | bytes 294920 | tf_op jit(solution)/shard_map/ppermute | solution.py:211
  9.3 6.6 %collective-permute-start.3 = (f32[2,2,16,384]{3,2,1,0:T(8,128)S(1)}, f32[2,2,16,384]{3,2,1,0:T(8,128)S(1)}, u32[]{:S(2)}, u32[]{:S(2)}) collective-permute-start(f32[2,2,16,384]{3,2,1,0:T(8,128)S(1)} %stack.2.refs_0_), channel_id=1, source_target_pairs={{0,8},{4,12},{8,0},{12,4},{1,9},{5,13},{9,1},{13,5},{2,10},{6,14},... | collective-permute-start | bytes 294920 | tf_op jit(solution)/shard_map/ppermute | solution.py:211
  16.0 3.2 %collective-permute-start.4 = (f32[8,2,16,384]{3,2,1,0:T(8,128)S(1)}, f32[8,2,16,384]{3,2,1,0:T(8,128)S(1)}, u32[]{:S(2)}, u32[]{:S(2)}) collective-permute-start(f32[8,2,16,384]{3,2,1,0:T(8,128)S(1)} %stack.3.blocks_ref), channel_id=1, source_target_pairs={{0,1},{1,0},{2,3},{3,2},{4,5},{5,4},{6,7},{7,6},{8,9},{9,8},{10,11... | collective-permute-start | bytes 1179656 | tf_op jit(solution)/shard_map/ppermute | solution.py:255
  19.3 2.2 %copy-start.1 = (f32[1,1,2,384]{3,2,1,0:T(2,128)S(1)}, f32[1,1,2,384]{3,2,1,0:T(2,128)}, u32[]{:S(2)}) copy-start(f32[1,1,2,384]{3,2,1,0:T(2,128)} %param.7) | copy-start | bytes 9220
  19.3 2.2 %copy-start.2 = (f32[1,1,2,384]{3,2,1,0:T(2,128)S(1)}, f32[1,1,2,384]{3,2,1,0:T(2,128)}, u32[]{:S(2)}) copy-start(f32[1,1,2,384]{3,2,1,0:T(2,128)} %param.8) | copy-start | bytes 9220
  19.3 1.3 %collective-permute-start.5 = (f32[2,16,384]{2,1,0:T(8,128)S(1)}, f32[2,16,384]{2,1,0:T(8,128)S(1)}, u32[]{:S(2)}, u32[]{:S(2)}) collective-permute-start(f32[2,16,384]{2,1,0:T(8,128)S(1)} %second_half.5.before_ref), channel_id=1, source_target_pairs={{0,32},{1,33},{2,34},{3,35},{4,36},{5,37},{6,38},{7,39},{8,40},{9,... | collective-permute-start | bytes 147464 | tf_op jit(solution)/shard_map/ppermute | solution.py:239
  20.1 1.3 %collective-permute-start.6 = (f32[2,16,384]{2,1,0:T(8,128)S(1)}, f32[2,16,384]{2,1,0:T(8,128)S(1)}, u32[]{:S(2)}, u32[]{:S(2)}) collective-permute-start(f32[2,16,384]{2,1,0:T(8,128)S(1)} %second_half.5.before_ref), channel_id=1, source_target_pairs={{0,16},{1,17},{16,0},{17,1},{32,33},{33,32},{48,49},{49,48},{64,65... | collective-permute-start | bytes 147464 | tf_op jit(solution)/shard_map/ppermute | solution.py:239
  31.5 3.1 %collective-permute-start.7 = (f32[8,2,16,384]{3,2,1,0:T(8,128)S(1)}, f32[8,2,16,384]{3,2,1,0:T(8,128)S(1)}, u32[]{:S(2)}, u32[]{:S(2)}) collective-permute-start(f32[8,2,16,384]{3,2,1,0:T(8,128)S(1)} %all_to_all.20.blocks_ref), channel_id=1, source_target_pairs={{0,1},{1,0},{2,3},{3,2},{4,5},{5,4},{6,7},{7,6},{8,9},{9,8},{10,11... | collective-permute-start | bytes 1179656 | tf_op jit(solution)/shard_map/ppermute | solution.py:255
  34.7 1.1 %collective-permute-start.8 = (f32[2,16,384]{2,1,0:T(8,128)S(1)}, f32[2,16,384]{2,1,0:T(8,128)S(1)}, u32[]{:S(2)}, u32[]{:S(2)}) collective-permute-start(f32[2,16,384]{2,1,0:T(8,128)S(1)} %second_half.6.before_ref), channel_id=1, source_target_pairs={{16,48},{17,49},{32,64},{33,65},{18,50},{19,51},{34,66},{35,67},{2... | collective-permute-start | bytes 147464 | tf_op jit(solution)/shard_map/ppermute | solution.py:239
  35.3 1.3 %collective-permute-start.9 = (f32[2,16,384]{2,1,0:T(8,128)S(1)}, f32[2,16,384]{2,1,0:T(8,128)S(1)}, u32[]{:S(2)}, u32[]{:S(2)}) collective-permute-start(f32[2,16,384]{2,1,0:T(8,128)S(1)} %second_half.6.before_ref), channel_id=1, source_target_pairs={{0,1},{1,0},{16,17},{17,16},{32,48},{33,49},{48,32},{49,33},{64,65... | collective-permute-start | bytes 147464 | tf_op jit(solution)/shard_map/ppermute | solution.py:239
  46.7 3.2 %collective-permute-start.10 = (f32[8,2,16,384]{3,2,1,0:T(8,128)S(1)}, f32[8,2,16,384]{3,2,1,0:T(8,128)S(1)}, u32[]{:S(2)}, u32[]{:S(2)}) collective-permute-start(f32[8,2,16,384]{3,2,1,0:T(8,128)S(1)} %all_to_all.21.blocks_ref), channel_id=1, source_target_pairs={{0,1},{1,0},{2,3},{3,2},{4,5},{5,4},{6,7},{7,6},{8,9},{9,8},{10,11... | collective-permute-start | bytes 1179656 | tf_op jit(solution)/shard_map/ppermute | solution.py:255
  49.9 1.1 %collective-permute-start.11 = (f32[2,16,384]{2,1,0:T(8,128)S(1)}, f32[2,16,384]{2,1,0:T(8,128)S(1)}, u32[]{:S(2)}, u32[]{:S(2)}) collective-permute-start(f32[2,16,384]{2,1,0:T(8,128)S(1)} %second_half.7.before_ref), channel_id=1, source_target_pairs={{48,80},{49,81},{64,96},{65,97},{50,82},{51,83},{66,98},{67,99},{5... | collective-permute-start | bytes 147464 | tf_op jit(solution)/shard_map/ppermute | solution.py:239
  50.6 1.3 %collective-permute-start.12 = (f32[2,16,384]{2,1,0:T(8,128)S(1)}, f32[2,16,384]{2,1,0:T(8,128)S(1)}, u32[]{:S(2)}, u32[]{:S(2)}) collective-permute-start(f32[2,16,384]{2,1,0:T(8,128)S(1)} %second_half.7.before_ref), channel_id=1, source_target_pairs={{0,1},{1,0},{16,17},{17,16},{32,33},{33,32},{48,49},{49,48},{64,80... | collective-permute-start | bytes 147464 | tf_op jit(solution)/shard_map/ppermute | solution.py:239
  62.0 3.2 %collective-permute-start.13 = (f32[8,2,16,384]{3,2,1,0:T(8,128)S(1)}, f32[8,2,16,384]{3,2,1,0:T(8,128)S(1)}, u32[]{:S(2)}, u32[]{:S(2)}) collective-permute-start(f32[8,2,16,384]{3,2,1,0:T(8,128)S(1)} %all_to_all.22.blocks_ref), channel_id=1, source_target_pairs={{0,1},{1,0},{2,3},{3,2},{4,5},{5,4},{6,7},{7,6},{8,9},{9,8},{10,11... | collective-permute-start | bytes 1179656 | tf_op jit(solution)/shard_map/ppermute | solution.py:255
  65.2 16.5 %collective-permute-start.14 = (f32[2,16,384]{2,1,0:T(8,128)S(1)}, f32[2,16,384]{2,1,0:T(8,128)S(1)}, u32[]{:S(2)}, u32[]{:S(2)}) collective-permute-start(f32[2,16,384]{2,1,0:T(8,128)S(1)} %second_half.8.before_ref), channel_id=1, source_target_pairs={{80,112},{81,113},{82,114},{83,115},{84,116},{85,117},{86,118},{87... | collective-permute-start | bytes 147464 | tf_op jit(solution)/shard_map/ppermute | solution.py:239
  66.5 15.2 %collective-permute-start.15 = (f32[2,16,384]{2,1,0:T(8,128)S(1)}, f32[2,16,384]{2,1,0:T(8,128)S(1)}, u32[]{:S(2)}, u32[]{:S(2)}) collective-permute-start(f32[2,16,384]{2,1,0:T(8,128)S(1)} %second_half.8.before_ref), channel_id=1, source_target_pairs={{0,1},{1,0},{16,17},{17,16},{32,33},{33,32},{48,49},{49,48},{64,65... | collective-permute-start | bytes 147464 | tf_op jit(solution)/shard_map/ppermute | solution.py:239
  91.3 3.9 %collective-permute-start.16 = (f32[8,2,16,384]{3,2,1,0:T(8,128)S(1)}, f32[8,2,16,384]{3,2,1,0:T(8,128)S(1)}, u32[]{:S(2)}, u32[]{:S(2)}) collective-permute-start(f32[8,2,16,384]{3,2,1,0:T(8,128)S(1)} %all_to_all.23.blocks_ref), channel_id=1, source_target_pairs={{0,1},{1,0},{2,3},{3,2},{4,5},{5,4},{6,7},{7,6},{8,9},{9,8},{10,11... | collective-permute-start | bytes 1179656 | tf_op jit(solution)/shard_map/ppermute | solution.py:255
